TPU v7x, 32 devices: a whole 2x2x4 slice. The times are simulated.
32 devices in a mesh: sec: 2 (over x), blk: 8 (over z, y), mp: 2 (over core).
Axes of the slice: x: 2, y: 2, z: 4, core: 2. Of those that a mesh axis runs over, the one named last changes fastest.
Arguments:
- image_pooled: bfloat16 [1536, 1536], P('blk', ('sec', 'mp')), may hold values from -4 to 4
- text_pooled: bfloat16 [1536, 2048], P('blk', ('sec', 'mp')), may hold values from -4 to 4
- image_proj: bfloat16 [1536, 1152], P(('sec', 'mp')), may hold values from -0.15625 to 0.15625
- text_proj: bfloat16 [2048, 1152], P(('sec', 'mp')), may hold values from -0.125 to 0.125
- natural_log_multiplier: float32 [1], replicated, may hold values from 1.4 to 2.3
- logit_bias: float32 [1], replicated, may hold values from -2 to -0.5
- match_cluster_labels: int32 [1536], P('blk'), may hold values from 0 to 1535
Outputs:
- pair_loss: float32 [2, 1536], P('sec', 'blk')
- image_grad: bfloat16 [1536, 1536], P('blk', ('sec', 'mp'))
- text_grad: bfloat16 [1536, 2048], P('blk', ('sec', 'mp'))
All inputs are finite; a program needn't handle non-finite values.
Results may differ from a plain program's by a relative error of at most 0.0065.
Values may be sent and summed in bfloat16 or wider, within the bound.
No kernel may reach another device: no remote copies, remote signals or barrier semaphores. Data moves between devices by JAX's collectives and lax.ppermute only.
A program may use at most 128 MiB of HBM per device.

v0:
```python
import jax
import jax.numpy as jnp
from jax import lax
from jax.sharding import PartitionSpec as P


def unit_rows(embedding):
    row_norm = jnp.sqrt(jnp.sum(embedding * embedding, axis=1, keepdims=True) + 1e-06)
    return (embedding / row_norm, row_norm)


def per_device(
    image_pooled,
    text_pooled,
    image_proj,
    text_proj,
    natural_log_multiplier,
    logit_bias,
    match_cluster_labels,
):
    part_image = jnp.dot(image_pooled, image_proj, preferred_element_type=jnp.float32)
    part_text = jnp.dot(text_pooled, text_proj, preferred_element_type=jnp.float32)
    stacked = jnp.stack([part_image, part_text])
    section = lax.axis_index("sec")
    both_sums = lax.psum(stacked, ("sec", "mp"))
    own_emb = lax.dynamic_index_in_dim(both_sums, section, 0, keepdims=False)
    other_emb = lax.dynamic_index_in_dim(both_sums, 1 - section, 0, keepdims=False)
    own_unit, own_norm = unit_rows(own_emb)
    resident_slice = own_unit.astype(jnp.bfloat16)
    other_unit, other_norm = unit_rows(other_emb)
    counterpart_slice = other_unit.astype(jnp.bfloat16)
    sharpness_factor = jnp.exp(natural_log_multiplier[0])
    shift_quantity = logit_bias[0]
    visit_rows = lax.all_gather(counterpart_slice, "blk", axis=0, tiled=True)
    visited_ids = lax.all_gather(match_cluster_labels, "blk", axis=0, tiled=True)
    agreement_scores_matrix = (
        sharpness_factor
        * lax.dot_general(
            resident_slice, visit_rows, (((1,), (1,)), ((), ())), preferred_element_type=jnp.float32
        )
        + shift_quantity
    )
    desired_polarity = jnp.where(
        match_cluster_labels[:, None] == visited_ids[None, :], 1.0, -1.0
    ).astype(jnp.float32)
    row_losses = jnp.sum(jax.nn.softplus(-desired_polarity * agreement_scores_matrix), axis=1)
    penalty_factor = (
        -sharpness_factor
        * desired_polarity
        * jax.nn.sigmoid(-desired_polarity * agreement_scores_matrix)
    ).astype(jnp.bfloat16)
    unit_grad = jnp.dot(penalty_factor, visit_rows, preferred_element_type=jnp.float32)
    unit_grad, row_losses = (unit_grad, row_losses)
    projection = jnp.sum(own_unit * unit_grad, axis=1, keepdims=True)
    own_demb = ((unit_grad - own_unit * projection) / own_norm).astype(jnp.bfloat16)
    both_grads = lax.all_gather(own_demb[None], "sec", axis=0, tiled=True)
    image_grad = lax.dot_general(
        both_grads[0], image_proj, (((1,), (1,)), ((), ())), preferred_element_type=jnp.float32
    ).astype(jnp.bfloat16)
    text_grad = lax.dot_general(
        both_grads[1], text_proj, (((1,), (1,)), ((), ())), preferred_element_type=jnp.float32
    ).astype(jnp.bfloat16)
    return (row_losses[None, :], image_grad, text_grad)


def solution(mesh):
    placed = (
        P("blk", ("sec", "mp")),
        P("blk", ("sec", "mp")),
        P(("sec", "mp"), None),
        P(("sec", "mp"), None),
        P(),
        P(),
        P("blk"),
    )
    return jax.shard_map(
        per_device,
        mesh=mesh,
        in_specs=placed,
        out_specs=(P("sec", "blk"), P("blk", ("sec", "mp")), P("blk", ("sec", "mp"))),
        check_vma=False,
    )
```

profile of v0, /device:TPU:0, one launch (start us, length us, event | category | flops | bytes accessed | tf_op | source)
XLA Modules:
  0.0 155.9 jit_solution(17890607806463199969)
XLA Ops:
  7.2 0.0 copy-start
  7.2 0.0 copy-start.4
  7.2 0.0 copy-start.2
  7.2 0.0 all-reduce.3.cloned.1.call-start
  7.2 1.2 copy-done
  8.4 1.4 convolution_bitcast_fusion
  9.8 0.0 copy-done.4
  9.8 0.0 copy-done.2
  9.8 0.4 convolution_bitcast_fusion.1
  10.2 1.3 pad_maximum_fusion
  11.6 0.0 all-reduce.3.cloned.1.call-update
  11.6 0.0 all-gather.3.cloned.1.call-start
  11.6 48.8 %all-reduce.3.cloned.1.call-done = f32[2,192,1152]{2,1,0:T(8,128)} async-done(((f32[2,192,1152]{2,1,0:T(8,128)}), f32[2,192,1152]{2,1,0:T(8,128)}) %all-reduce.3.cloned.1.call-update) | async-done | bytes 1769488 | tf_op jit(solution)/shard_map/psum | solution.py:25
  60.5 0.0 copy-start.1
  60.5 1.8 %fusion.7 = (f32[192]{0:T(256)S(1)}, f32[192]{0:T(256)S(1)}) fusion(f32[2,192,1152]{2,1,0:T(8,128)} %all-reduce.3.cloned.1.call-done, s32[]{:T(128)S(6)} %select_n.16, s32[]{:T(128)S(6)} %select_n.17), kind=kLoop, calls=%fused_computation.20 | loop fusion | flops 884352 | bytes 1771016 | tf_op jit(solution)/shard_map/reduce_sum | solution.py:8
  62.2 0.0 copy-start.7
  62.3 0.0 copy-start.5
  62.3 0.2 copy-done.1
  62.5 0.9 fusion.6
  63.4 0.0 all-gather.3.cloned.1.call-update
  64.7 0.0 copy-done.7
  64.8 0.6 dynamic-slice
  66.0 0.0 copy-done.5
  66.0 0.3 dynamic-update-slice
  66.3 12.1 %all-reduce = s32[1536]{0:T(1024)S(1)} all-reduce(s32[1536]{0:T(1024)S(1)} %dynamic-update-slice), channel_id=1, replica_groups=mesh['sec'=2,'blk'=8,'mp'=2] {'blk'}, use_global_device_ids=true, to_apply=%add | all-reduce | flops 1536 | bytes 12288
  78.4 50.5 %all-gather.3.cloned.1.call-done = bf16[1536,1152]{1,0:T(8,128)(2,1)} async-done(((bf16[192,1152]{1,0:T(8,128)(2,1)}), bf16[1536,1152]{1,0:T(8,128)(2,1)}) %all-gather.3.cloned.1.call-update) | async-done | bytes 3538960 | tf_op jit(solution)/shard_map/all_gather | solution.py:34
  128.9 0.0 copy-start.6
  128.9 4.7 %fusion.4 = (f32[192]{0:T(256)}, f32[192,1536]{1,0:T(8,128)S(1)}) fusion(f32[]{:T(128)} %bitcast.37, bf16[1536,1152]{1,0:T(8,128)(2,1)} %all-gather.3.cloned.1.call-done, f32[192]{0:T(256)S(1)} %add_sqrt_fusion.1, f32[2,192,1152]{2,1,0:T(8,128)S(1)} %copy-done.1, s32[]{:T(128)S(6)} %select_n.16, f32[]{:T(128)} %bitcast.1, s32[1536]{0:T(1024)S(1)} %all-reduce, ...), kind=kOutput, calls=%fused_computation.11 | convolution fusion | flops 683753280 | bytes 5614348 | tf_op jit(solution)/shard_map/dot_general | solution.py:38
  133.6 0.0 copy-done.6
  133.6 1.1 multiply_reduce_fusion
  134.7 0.2 divide_convert_fusion
  135.0 0.0 copy-start.3
  135.0 11.7 %all-gather = bf16[384,1152]{1,0:T(8,128)(2,1)S(1)} all-gather(bf16[192,1152]{1,0:T(8,128)(2,1)S(1)} %divide_convert_fusion), channel_id=2, replica_groups=mesh['sec'=2,'blk'=8,'mp'=2] {'sec'}, dimensions={0}, use_global_device_ids=true | all-gather | bytes 1327104 | tf_op jit(solution)/shard_map/all_gather | solution.py:56
  146.7 0.0 copy-done.3
  146.7 1.1 convolution_convert_fusion.1
  147.8 1.2 convolution_convert_fusion
  (3 shorter events, 0.0 us)
Async XLA Ops:
  7.2 1.3 copy-start
  7.2 2.6 %copy-start.4 = (bf16[192,384]{1,0:T(8,128)(2,1)S(1)}, bf16[192,384]{1,0:T(8,128)(2,1)}, u32[]{:S(2)}) copy-start(bf16[192,384]{1,0:T(8,128)(2,1)} %param.7) | copy-start | bytes 442372
  7.2 2.6 %copy-start.2 = (bf16[384,1152]{1,0:T(8,128)(2,1)S(1)}, bf16[384,1152]{1,0:T(8,128)(2,1)}, u32[]{:S(2)}) copy-start(bf16[384,1152]{1,0:T(8,128)(2,1)} %param.9) | copy-start | bytes 2654212
  7.2 53.3 %all-reduce.3.cloned.1.call-start = ((), (), s32[]{:S(2)}) async-start(), calls=%async_computation | async-start | bytes 3538944 | tf_op jit(solution)/shard_map/psum | solution.py:25
  11.6 117.3 %all-gather.3.cloned.1.call-start = ((), (), s32[]{:S(2)}) async-start(), calls=%async_computation.1 | async-start | bytes 3981312 | tf_op jit(solution)/shard_map/all_gather | solution.py:34
  60.5 2.0 %copy-start.1 = (f32[2,192,1152]{2,1,0:T(8,128)S(1)}, f32[2,192,1152]{2,1,0:T(8,128)}, u32[]{:S(2)}) copy-start(f32[2,192,1152]{2,1,0:T(8,128)} %all-reduce.3.cloned.1.call-done) | copy-start | bytes 5308420
  62.2 2.5 %copy-start.7 = (u32[32]{0:T(128)S(1)}, u32[32]{0:T(128)}, u32[]{:S(2)}) copy-start(u32[32]{0:T(128)} %constant.31) | copy-start | bytes 388
  62.3 3.8 %copy-start.5 = (s32[192]{0:T(256)S(1)}, s32[192]{0:T(256)}, u32[]{:S(2)}) copy-start(s32[192]{0:T(256)} %param.13) | copy-start | bytes 2308
  128.9 4.7 %copy-start.6 = (bf16[1536,1152]{1,0:T(8,128)(2,1)S(1)}, bf16[1536,1152]{1,0:T(8,128)(2,1)}, u32[]{:S(2)}) copy-start(bf16[1536,1152]{1,0:T(8,128)(2,1)} %all-gather.3.cloned.1.call-done) | copy-start | bytes 10616836
  135.0 11.8 %copy-start.3 = (bf16[384,1152]{1,0:T(8,128)(2,1)S(1)}, bf16[384,1152]{1,0:T(8,128)(2,1)}, u32[]{:S(2)}) copy-start(bf16[384,1152]{1,0:T(8,128)(2,1)} %param.9) | copy-start | bytes 2654212
Sparse Core Ops, SparseCore 0:
  11.7 48.7 all-reduce.2
  63.5 65.3 all-gather.2
where the time goes:
time: 156 us
  waiting for transfers between devices  99.4 us (64%)
  blocking collectives  23.8 us (15%)
  between operations  16.2 us (10%)
  matrix products  9.9 us (6%)
  other arithmetic  4.2 us (3%)
  local copies, waits for them, and re-layouts  2.31 us (1%)
    all_gather x1, waiting for transfers between devices, per_device(): visit_rows = lax.all_gather(counterpart_slice, 'blk', axis=0, tiled=True)  50.5 us
    psum x1, waiting for transfers between devices, per_device(): both_sums = lax.psum(stacked, ('sec', 'mp'))  48.8 us
    unnamed x1, blocking collectives  12.1 us
    all_gather x1, blocking collectives, per_device(): both_grads = lax.all_gather(own_demb[None], 'sec', axis=0, tiled=True)  11.7 us
    dot_general x1, matrix products, per_device(): lax.dot_general(resident_slice, visit_rows, (((1,), (1,)), ((), ())), pre...  4.68 us
  transfers between devices with their start and end apart: 2, of which 2 were waited for; matrix products, arithmetic and copies ran while one was open for 1% of the time, Pallas kernels for 0%

commit v1 on v0

v1 whole, which is shorter than its diff:
```python
import jax
import jax.numpy as jnp
from jax import lax
from jax.experimental import pallas as pl
from jax.experimental.pallas import tpu as pltpu
from jax.sharding import PartitionSpec as P

F32 = jnp.float32
BF16 = jnp.bfloat16
SWAP = [(0, 1), (1, 0)]
NT = (((1,), (1,)), ((), ()))
VMEM_LIMIT = 40 * 1024 * 1024


def local_call(kernel, name, outs, scalars, arrays, scratch=(), flops=0, transcendentals=0):
    nbytes = sum(a.size * a.dtype.itemsize for a in arrays)
    return pl.pallas_call(
        kernel,
        out_shape=outs,
        in_specs=[pl.BlockSpec(memory_space=pltpu.SMEM)] * len(scalars)
        + [pl.BlockSpec(memory_space=pltpu.VMEM)] * len(arrays),
        out_specs=[pl.BlockSpec(memory_space=pltpu.VMEM)] * len(outs),
        scratch_shapes=list(scratch),
        compiler_params=pltpu.CompilerParams(vmem_limit_bytes=VMEM_LIMIT),
        cost_estimate=pl.CostEstimate(
            flops=flops, bytes_accessed=nbytes, transcendentals=transcendentals
        ),
        name=name,
    )(*scalars, *arrays)


def half_embed_kernel(which, dtype):
    def kernel(place, image_pooled, text_pooled, image_proj, text_proj, out):
        half = out.shape[1]
        core = place[2]
        start = pl.multiple_of((core if which == 0 else 1 - core) * half, half)
        rows = pl.ds(start, half)
        out[0] = jnp.dot(
            image_pooled[rows, :], image_proj[...], preferred_element_type=F32
        ).astype(dtype)
        out[1] = jnp.dot(
            text_pooled[rows, :], text_proj[...], preferred_element_type=F32
        ).astype(dtype)

    return kernel


def join_cores_kernel(place, kept, got, own_sum, other_sum, own_send, other_send):
    section = place[0]
    own = kept[section] + got[section].astype(F32)
    own_sum[...] = own
    own_send[...] = own.astype(BF16)
    other = kept[1 - section] + got[1 - section].astype(F32)
    other_sum[...] = other
    other_send[...] = other.astype(BF16)


def unit_kernel(summed, got, unit, unit_b, norm):
    emb = summed[...] + got[...].astype(F32)
    row_norm = jnp.sqrt(jnp.sum(emb * emb, axis=1, keepdims=True) + 1e-06)
    value = emb / row_norm
    unit[...] = value
    unit_b[...] = value.astype(BF16)
    norm[...] = row_norm


def pair_kernel(blocks, first, last):
    def kernel(place, scale_bias, own_a, own_b, own_ids, visit_ids, *refs):
        pieces = refs[: 2 * blocks]
        refs = refs[2 * blocks :]
        if not first:
            grad_in, loss_in = refs[:2]
            refs = refs[2:]
        if last:
            grad_keep, grad_own, grad_near, loss_own, loss_near = refs[:5]
            refs = refs[5:]
        else:
            grad_out, loss_out = refs[:2]
            refs = refs[2:]
        own, visited = refs
        half = own_a.shape[0]
        core = place[2]
        own[pl.ds(0, half), :] = own_a[...]
        own[pl.ds(half, half), :] = own_b[...]
        for block in range(blocks):
            mine = pl.multiple_of(core * half, half) + 2 * half * block
            theirs = pl.multiple_of((1 - core) * half, half) + 2 * half * block
            visited[pl.ds(mine, half), :] = pieces[2 * block][...]
            visited[pl.ds(theirs, half), :] = pieces[2 * block + 1][...]
        scale = scale_bias[0]
        scores = (
            scale * lax.dot_general(own[...], visited[...], NT, preferred_element_type=F32)
            + scale_bias[1]
        )
        sign = jnp.where(own_ids[...] == visit_ids[...], 1.0, -1.0).astype(F32)
        value = -sign * scores
        small = jnp.exp(-jnp.abs(value))
        losses = jnp.maximum(value, 0.0) + jnp.log1p(small)
        sigmoid = jnp.where(value >= 0.0, 1.0, small) / (1.0 + small)
        weight = (-scale * sign * sigmoid).astype(BF16)
        grad = jnp.dot(weight, visited[...], preferred_element_type=F32)
        loss = jnp.sum(losses, axis=1, keepdims=True)
        if not first:
            grad = grad + grad_in[...]
            loss = loss + loss_in[...]
        if last:
            grad_keep[...] = grad[:half]
            grad_own[...] = grad[:half].astype(BF16)
            grad_near[...] = grad[half:].astype(BF16)
            wide = jnp.broadcast_to(loss, (2 * half, 128))
            loss_own[...] = jnp.transpose(wide[:half])[0:1]
            loss_near[...] = jnp.transpose(wide[half:])[0:1]
        else:
            grad_out[...] = grad
            loss_out[...] = loss

    return kernel


def demb_kernel(place, kept, near, across, diagonal, own_unit, own_norm, other_unit, other_norm, out):
    section = place[0]

    def finish(grad, unit, norm):
        value = unit[...]
        along = jnp.sum(value * grad, axis=1, keepdims=True)
        return ((grad - value * along) / norm[...]).astype(BF16)

    out[section] = finish(kept[...] + near[...].astype(F32), own_unit, own_norm)
    out[1 - section] = finish(
        across[...].astype(F32) + diagonal[...].astype(F32), other_unit, other_norm
    )


def grads_kernel(place, mine, theirs, image_proj, text_proj, image_grad, text_grad):
    half = mine.shape[1]
    core = place[2]
    for place_of, source in ((core, mine), (1 - core, theirs)):
        rows = pl.ds(pl.multiple_of(place_of * half, half), half)
        image_grad[rows, :] = lax.dot_general(
            source[0], image_proj[...], NT, preferred_element_type=F32
        ).astype(BF16)
        text_grad[rows, :] = lax.dot_general(
            source[1], text_proj[...], NT, preferred_element_type=F32
        ).astype(BF16)


def make_per_device(mesh):
    sections = mesh.shape["sec"]
    blocks = mesh.shape["blk"]

    def across_blk(value, step):
        return lax.ppermute(value, "blk", [(i, i ^ step) for i in range(blocks)])

    def per_device(
        image_pooled, text_pooled, image_proj, text_proj, log_multiplier, logit_bias, ids
    ):
        section = lax.axis_index("sec")
        core = lax.axis_index("mp")
        place = jnp.stack([section, lax.axis_index("blk"), core]).astype(jnp.int32)
        scale_bias = jnp.concatenate([jnp.exp(log_multiplier), logit_bias])
        rows = image_pooled.shape[0]
        half = rows // 2
        width = image_proj.shape[1]
        block_f32 = jax.ShapeDtypeStruct((half, width), F32)
        block_b16 = jax.ShapeDtypeStruct((half, width), BF16)
        norm_shape = jax.ShapeDtypeStruct((half, 1), F32)
        towers = (image_pooled, text_pooled, image_proj, text_proj)
        embed_flops = 2 * half * width * (image_proj.shape[0] + text_proj.shape[0])

        (sent,) = local_call(
            half_embed_kernel(1, BF16),
            "embed_sent",
            [jax.ShapeDtypeStruct((2, half, width), BF16)],
            [place],
            towers,
            flops=embed_flops,
        )
        got = lax.ppermute(sent, "mp", SWAP)
        (kept,) = local_call(
            half_embed_kernel(0, F32),
            "embed_kept",
            [jax.ShapeDtypeStruct((2, half, width), F32)],
            [place],
            towers,
            flops=embed_flops,
        )
        own_sum, other_sum, own_send, other_send = local_call(
            join_cores_kernel,
            "join_cores",
            [block_f32, block_f32, block_b16, block_b16],
            [place],
            [kept, got],
        )
        other_got = lax.ppermute(own_send, "sec", SWAP)
        own_got = lax.ppermute(other_send, "sec", SWAP)
        other_unit, visit, other_norm = local_call(
            unit_kernel, "other_unit", [block_f32, block_b16, norm_shape], [], [other_sum, other_got]
        )
        own_unit, own_rows, own_norm = local_call(
            unit_kernel, "own_unit", [block_f32, block_b16, norm_shape], [], [own_sum, own_got]
        )

        steps = list(range(0, blocks, 2))
        mine = [visit] + [across_blk(visit, k) for k in steps[1:]]
        near_rows = across_blk(own_rows, 1)
        ids_row = ids[None, :]
        ids_row, _ = lax.optimization_barrier((ids_row, own_rows))
        near_ids = across_blk(ids_row, 1)
        block_ids = [ids_row] + [across_blk(ids_row, k) for k in steps[1:]]
        theirs = [lax.ppermute(v, "mp", SWAP) for v in mine]

        own_ids = jnp.concatenate(
            [
                lax.dynamic_slice_in_dim(ids_row, core * half, half, 1),
                lax.dynamic_slice_in_dim(near_ids, core * half, half, 1),
            ],
            axis=1,
        ).reshape(2 * half, 1)
        groups = [list(range(i, min(i + 2, len(steps)))) for i in range(0, len(steps), 2)]
        state = []
        for index, group in enumerate(groups):
            first, last = index == 0, index == len(groups) - 1
            visit_ids = jnp.concatenate([block_ids[g] for g in group], axis=1)
            pieces = [p for g in group for p in (mine[g], theirs[g])]
            if last:
                outs = [block_f32, block_b16, block_b16]
                outs += [jax.ShapeDtypeStruct((1, half), F32)] * 2
            else:
                outs = [
                    jax.ShapeDtypeStruct((2 * half, width), F32),
                    jax.ShapeDtypeStruct((2 * half, 1), F32),
                ]
            visited_rows = 2 * half * len(group)
            state = local_call(
                pair_kernel(len(group), first, last),
                "pairs",
                outs,
                [place, scale_bias],
                [own_rows, near_rows, own_ids, visit_ids, *pieces, *state],
                scratch=[
                    pltpu.VMEM((2 * half, width), BF16),
                    pltpu.VMEM((visited_rows, width), BF16),
                ],
                flops=8 * half * visited_rows * width,
                transcendentals=6 * half * visited_rows,
            )
        grad_keep, grad_own, grad_near, loss_own, loss_near = state

        pairs = [(s, b) for s in range(sections) for b in range(blocks)]
        diagonal_pairs = [
            (s * blocks + b, (1 - s) * blocks + (b ^ 1)) for s, b in pairs
        ]
        near = across_blk(grad_near, 1)
        diagonal = lax.ppermute(grad_near, ("sec", "blk"), diagonal_pairs)
        across = lax.ppermute(grad_own, "sec", SWAP)
        (demb,) = local_call(
            demb_kernel,
            "demb",
            [jax.ShapeDtypeStruct((2, half, width), BF16)],
            [place],
            [grad_keep, near, across, diagonal, own_unit, own_norm, other_unit, other_norm],
        )
        demb_got = lax.ppermute(demb, "mp", SWAP)
        loss_mine = loss_own + across_blk(loss_near, 1)
        loss_theirs = lax.ppermute(loss_mine, "mp", SWAP)
        pair_loss = jnp.where(
            core == 0,
            jnp.concatenate([loss_mine, loss_theirs], axis=1),
            jnp.concatenate([loss_theirs, loss_mine], axis=1),
        )
        image_grad, text_grad = local_call(
            grads_kernel,
            "grads",
            [
                jax.ShapeDtypeStruct((rows, image_proj.shape[0]), BF16),
                jax.ShapeDtypeStruct((rows, text_proj.shape[0]), BF16),
            ],
            [place],
            [demb, demb_got, image_proj, text_proj],
            flops=2 * embed_flops,
        )
        return (pair_loss, image_grad, text_grad)

    return per_device


def solution(mesh):
    placed = (
        P("blk", ("sec", "mp")),
        P("blk", ("sec", "mp")),
        P(("sec", "mp"), None),
        P(("sec", "mp"), None),
        P(),
        P(),
        P("blk"),
    )
    return jax.shard_map(
        make_per_device(mesh),
        mesh=mesh,
        in_specs=placed,
        out_specs=(P("sec", "blk"), P("blk", ("sec", "mp")), P("blk", ("sec", "mp"))),
        check_vma=False,
    )
```

time: 156 us -> 72.6 us (0.47)
  the two profiles are of different devices: /device:TPU:0 before, /device:TPU:19 now
where the time goes in v1:
time: 72.6 us; the launch traced here: 72.3 us
  waiting for transfers between devices  29.3 us (40%)
  starting transfers between devices  25.6 us (35%)
  Pallas kernels  9.74 us (13%)
  local copies, waits for them, and re-layouts  4.55 us (6%)
  between operations  2.11 us (3%)
  other arithmetic  1.01 us (1%)
    ppermute x10, waiting for transfers between devices, across_blk(): return lax.ppermute(value, 'blk', [(i, i ^ step) for i in range(blocks)])  18.2 us
    pallas_call x9, Pallas kernels, local_call(): pl.pallas_call(kernel, out_shape=outs, in_specs=[pl.BlockSpec(memory_spac...  9.74 us
    ppermute x10, starting transfers between devices, across_blk(): return lax.ppermute(value, 'blk', [(i, i ^ step) for i in range(blocks)])  8.79 us
    ppermute x4, starting transfers between devices, per_device(): theirs = [lax.ppermute(v, 'mp', SWAP) for v in mine]  6.67 us
    ppermute x1, starting transfers between devices, per_device(): demb_got = lax.ppermute(demb, 'mp', SWAP)  4.78 us
    unnamed x14, local copies, waits for them, and re-layouts  4.29 us
    ppermute x1, waiting for transfers between devices, per_device(): own_got = lax.ppermute(other_send, 'sec', SWAP)  3.72 us
    ppermute x1, waiting for transfers between devices, per_device(): diagonal = lax.ppermute(grad_near, ('sec', 'blk'), diagonal_pairs)  3.52 us
  transfers between devices with their start and end apart: 21, of which 10 were waited for; matrix products, arithmetic and copies ran while one was open for 2% of the time, Pallas kernels for 4%

profile of v1, /device:TPU:19, one launch (start us, length us, event | category | flops | bytes accessed | tf_op | source)
XLA Modules:
  0.0 72.3 jit_solution(17475663462116785324)
XLA Ops:
  0.6 0.1 pad_add_fusion.2.place
  0.7 1.3 %copy-done = bf16[512,1152]{1,0:T(8,128)(2,1)S(1)} copy-done((bf16[512,1152]{1,0:T(8,128)(2,1)S(1)}, bf16[512,1152]{1,0:T(8,128)(2,1)}, u32[]{:S(2)}) %copy-start) | copy-done | bytes 1179672
  2.0 1.2 %copy-done.2 = bf16[384,1152]{1,0:T(8,128)(2,1)S(1)} copy-done((bf16[384,1152]{1,0:T(8,128)(2,1)S(1)}, bf16[384,1152]{1,0:T(8,128)(2,1)}, u32[]{:S(2)}) %copy-start.2) | copy-done | bytes 884760
  3.2 0.9 %copy-done.4 = bf16[192,512]{1,0:T(8,128)(2,1)S(1)} copy-done((bf16[192,512]{1,0:T(8,128)(2,1)S(1)}, bf16[192,512]{1,0:T(8,128)(2,1)}, u32[]{:S(2)}) %copy-start.4) | copy-done | bytes 196632
  4.1 0.9 %copy-done.5 = bf16[192,384]{1,0:T(8,128)(2,1)S(1)} copy-done((bf16[192,384]{1,0:T(8,128)(2,1)S(1)}, bf16[192,384]{1,0:T(8,128)(2,1)}, u32[]{:S(2)}) %copy-start.5) | copy-done | bytes 147480
  5.0 1.0 %embed_sent.1 = bf16[2,96,1152]{2,1,0:T(8,128)(2,1)S(1)} custom-call(s32[3]{0:T(128)S(1)} %pad_add_fusion.2.place, bf16[192,384]{1,0:T(8,128)(2,1)S(1)} %copy-done.5, bf16[192,512]{1,0:T(8,128)(2,1)S(1)} %copy-done.4, bf16[384,1152]{1,0:T(8,128)(2,1)S(1)} %copy-done.2, bf16[512,1152]{1,0:T(8,128)(2,1)S(1)} %copy-done), custom_call_target="tpu_custom_call" | custom-call | flops 198180864 | bytes 2408448 | tf_op jit(solution)/shard_map/embed_sent/pallas_call | solution.py:17
  6.0 0.7 %collective-permute-start = (bf16[2,96,1152]{2,1,0:T(8,128)(2,1)S(1)}, bf16[2,96,1152]{2,1,0:T(8,128)(2,1)S(1)}, u32[]{:S(2)}, u32[]{:S(2)}) collective-permute-start(bf16[2,96,1152]{2,1,0:T(8,128)(2,1)S(1)} %embed_sent.1), channel_id=1, source_target_pairs={{0,1},{1,0},{2,3},{3,2},{4,5},{5,4},{6,7},{7,6},{8,9},{9,8},{10,11... | collective-permute-start | bytes 1327112 | tf_op jit(solution)/shard_map/ppermute | solution.py:178
  6.8 1.0 %embed_kept.1.kept = f32[2,96,1152]{2,1,0:T(8,128)S(1)} custom-call(s32[3]{0:T(128)S(1)} %pad_add_fusion.2.place, bf16[192,384]{1,0:T(8,128)(2,1)S(1)} %copy-done.5, bf16[192,512]{1,0:T(8,128)(2,1)S(1)} %copy-done.4, bf16[384,1152]{1,0:T(8,128)(2,1)S(1)} %copy-done.2, bf16[512,1152]{1,0:T(8,128)(2,1)S(1)} %copy-done), custom_call_target="tpu_custom_call" | custom-call | flops 198180864 | bytes 2408448 | tf_op jit(solution)/shard_map/embed_kept/pallas_call | solution.py:17
  7.8 0.4 collective-permute-done.got
  8.2 0.7 join_cores.1
  8.9 0.3 collective-permute-start.1
  9.2 1.2 %collective-permute-start.6 = (bf16[96,1152]{1,0:T(8,128)(2,1)S(1)}, bf16[96,1152]{1,0:T(8,128)(2,1)S(1)}, u32[]{:S(2)}, u32[]{:S(2)}) collective-permute-start(bf16[96,1152]{1,0:T(8,128)(2,1)S(1)} %get-tuple-element.28), channel_id=1, source_target_pairs={{0,16},{16,0},{1,17},{17,1},{2,18},{18,2},{3,19},{19,3},{4,20},{20... | collective-permute-start | bytes 663560 | tf_op jit(solution)/shard_map/ppermute | solution.py:194
  11.8 0.1 pad_maximum_fusion.scale_bias
  11.8 3.7 %collective-permute-done.1.got = bf16[96,1152]{1,0:T(8,128)(2,1)S(1)} collective-permute-done((bf16[96,1152]{1,0:T(8,128)(2,1)S(1)}, bf16[96,1152]{1,0:T(8,128)(2,1)S(1)}, u32[]{:S(2)}, u32[]{:S(2)}) %collective-permute-start.1) | collective-permute-done | bytes 221216 | tf_op jit(solution)/shard_map/ppermute | solution.py:195
  15.5 0.2 own_unit.1
  15.7 1.4 %collective-permute-start.11 = (s32[1,192]{1,0:T(1,128)S(1)}, s32[1,192]{1,0:T(1,128)S(1)}, u32[]{:S(2)}, u32[]{:S(2)}) collective-permute-start(s32[1,192]{1,0:T(1,128)S(1)} %bitcast.6), channel_id=1, source_target_pairs={{0,4},{2,6},{4,0},{6,2},{8,12},{10,14},{12,8},{14,10},{1,5},{3,7},... | collective-permute-start | bytes 2312 | tf_op jit(solution)/shard_map/ppermute | solution.py:152
  17.1 1.2 %collective-permute-start.3 = (s32[1,192]{1,0:T(1,128)S(1)}, s32[1,192]{1,0:T(1,128)S(1)}, u32[]{:S(2)}, u32[]{:S(2)}) collective-permute-start(s32[1,192]{1,0:T(1,128)S(1)} %bitcast.7), channel_id=1, source_target_pairs={{0,2},{2,0},{4,6},{6,4},{8,10},{10,8},{12,14},{14,12},{1,3},{3,1},... | collective-permute-start | bytes 2312 | tf_op jit(solution)/shard_map/ppermute | solution.py:152
  18.4 1.9 %collective-permute-done.6.got = bf16[96,1152]{1,0:T(8,128)(2,1)S(1)} collective-permute-done((bf16[96,1152]{1,0:T(8,128)(2,1)S(1)}, bf16[96,1152]{1,0:T(8,128)(2,1)S(1)}, u32[]{:S(2)}, u32[]{:S(2)}) %collective-permute-start.6) | collective-permute-done | bytes 221216 | tf_op jit(solution)/shard_map/ppermute | solution.py:194
  20.3 0.2 other_unit.1
  20.5 1.4 %collective-permute-start.13 = (bf16[96,1152]{1,0:T(8,128)(2,1)S(1)}, bf16[96,1152]{1,0:T(8,128)(2,1)S(1)}, u32[]{:S(2)}, u32[]{:S(2)}) collective-permute-start(bf16[96,1152]{1,0:T(8,128)(2,1)S(1)} %get-tuple-element.29.refs_0_), channel_id=1, source_target_pairs={{0,4},{2,6},{4,0},{6,2},{8,12},{10,14},{12,8},{14,10},{1,5},{3,7},... | collective-permute-start | bytes 663560 | tf_op jit(solution)/shard_map/ppermute | solution.py:152
  21.9 2.2 %collective-permute-start.7 = (bf16[96,1152]{1,0:T(8,128)(2,1)S(1)}, bf16[96,1152]{1,0:T(8,128)(2,1)S(1)}, u32[]{:S(2)}, u32[]{:S(2)}) collective-permute-start(bf16[96,1152]{1,0:T(8,128)(2,1)S(1)} %get-tuple-element.29.refs_0_), channel_id=1, source_target_pairs={{0,8},{2,10},{4,12},{6,14},{8,0},{10,2},{12,4},{14,6},{1,9},{3,11}... | collective-permute-start | bytes 663560 | tf_op jit(solution)/shard_map/ppermute | solution.py:152
  24.2 0.2 collective-permute-start.5
  24.4 0.1 add_bitcast_fusion
  24.5 0.1 copy.11.own_ids
  24.6 3.3 %collective-permute-start.12 = (bf16[96,1152]{1,0:T(8,128)(2,1)S(1)}, bf16[96,1152]{1,0:T(8,128)(2,1)S(1)}, u32[]{:S(2)}, u32[]{:S(2)}) collective-permute-start(bf16[96,1152]{1,0:T(8,128)(2,1)S(1)} %get-tuple-element.29.refs_0_), channel_id=1, source_target_pairs={{0,1},{1,0},{2,3},{3,2},{4,5},{5,4},{6,7},{7,6},{8,9},{9,8},{10,11... | collective-permute-start | bytes 663560 | tf_op jit(solution)/shard_map/ppermute | solution.py:210
  28.0 13.9 %collective-permute-done.5 = s32[1,192]{1,0:T(1,128)S(1)} collective-permute-done((s32[1,192]{1,0:T(1,128)S(1)}, s32[1,192]{1,0:T(1,128)S(1)}, u32[]{:S(2)}, u32[]{:S(2)}) %collective-permute-start.5) | collective-permute-done | bytes 800 | tf_op jit(solution)/shard_map/ppermute | solution.py:152
  41.9 0.8 %collective-permute-start.2 = (bf16[96,1152]{1,0:T(8,128)(2,1)S(1)}, bf16[96,1152]{1,0:T(8,128)(2,1)S(1)}, u32[]{:S(2)}, u32[]{:S(2)}) collective-permute-start(bf16[96,1152]{1,0:T(8,128)(2,1)S(1)} %get-tuple-element.25.own_a), channel_id=1, source_target_pairs={{0,2},{2,0},{4,6},{6,4},{8,10},{10,8},{12,14},{14,12},{1,3},{3,1},... | collective-permute-start | bytes 663560 | tf_op jit(solution)/shard_map/ppermute | solution.py:152
  42.6 2.8 %collective-permute-start.14 = (bf16[96,1152]{1,0:T(8,128)(2,1)S(1)}, bf16[96,1152]{1,0:T(8,128)(2,1)S(1)}, u32[]{:S(2)}, u32[]{:S(2)}) collective-permute-start(bf16[96,1152]{1,0:T(8,128)(2,1)S(1)} %collective-permute-done.13.refs_2_), channel_id=1, source_target_pairs={{0,1},{1,0},{2,3},{3,2},{4,5},{5,4},{6,7},{7,6},{8,9},{9,8},{10,11... | collective-permute-start | bytes 663560 | tf_op jit(solution)/shard_map/ppermute | solution.py:210
  45.5 0.4 collective-permute-start.8
  46.0 0.1 pad_add_fusion.1.visit_ids
  46.0 0.1 pad_add_fusion.visit_ids
  46.1 0.5 collective-permute-done.2.own_b
  46.7 1.6 %pairs.2 = (f32[192,1152]{1,0:T(8,128)S(1)}, f32[192,1]{1,0:T(8,128)S(1)}) custom-call(s32[3]{0:T(128)S(1)} %pad_add_fusion.2.place, f32[2]{0:T(128)S(1)} %pad_maximum_fusion.scale_bias, bf16[96,1152]{1,0:T(8,128)(2,1)S(1)} %get-tuple-element.25.own_a, bf16[96,1152]{1,0:T(8,128)(2,1)S(1)} %collective-permute-done.2.own_b, s32[192,1]{1,0:T(8,128)S(1)} %copy.11.own_ids, ...), custom_call_target="tpu_custom_call" | custom-call | flops 339738624 | bytes 1329408 | tf_op jit(solution)/shard_map/pairs/pallas_call | solution.py:17
  48.3 1.6 %pairs.3 = (f32[96,1152]{1,0:T(8,128)S(1)}, bf16[96,1152]{1,0:T(8,128)(2,1)S(1)}, bf16[96,1152]{1,0:T(8,128)(2,1)S(1)}, f32[1,96]{1,0:T(1,128)S(1)}, f32[1,96]{1,0:T(1,128)S(1)}) custom-call(s32[3]{0:T(128)S(1)} %pad_add_fusion.2.place, f32[2]{0:T(128)S(1)} %pad_maximum_fusion.scale_bias, bf16[96,1152]{1,0:T(8,128)(2,1)S(1)} %get-tuple-element.25.own_a, ...), custom_call_target="tpu_custom_call" | custom-call | flops 339738624 | bytes 2214912 | tf_op jit(solution)/shard_map/pairs/pallas_call | solution.py:17
  49.9 0.8 %collective-permute-start.17 = (bf16[96,1152]{1,0:T(8,128)(2,1)S(1)}, bf16[96,1152]{1,0:T(8,128)(2,1)S(1)}, u32[]{:S(2)}, u32[]{:S(2)}) collective-permute-start(bf16[96,1152]{1,0:T(8,128)(2,1)S(1)} %get-tuple-element.35), channel_id=1, source_target_pairs={{0,2},{2,0},{4,6},{6,4},{8,10},{10,8},{12,14},{14,12},{1,3},{3,1},... | collective-permute-start | bytes 663560 | tf_op jit(solution)/shard_map/ppermute | solution.py:152
  50.7 0.3 collective-permute-start.18
  51.0 1.6 %collective-permute-start.19 = (bf16[96,1152]{1,0:T(8,128)(2,1)S(1)}, bf16[96,1152]{1,0:T(8,128)(2,1)S(1)}, u32[]{:S(2)}, u32[]{:S(2)}) collective-permute-start(bf16[96,1152]{1,0:T(8,128)(2,1)S(1)} %get-tuple-element.35), channel_id=1, source_target_pairs={{0,18},{2,16},{4,22},{6,20},{8,26},{10,24},{12,30},{14,28},{16,2},... | collective-permute-start | bytes 663560 | tf_op jit(solution)/shard_map/ppermute | solution.py:254
  52.6 2.1 %collective-permute-done.17.near = bf16[96,1152]{1,0:T(8,128)(2,1)S(1)} collective-permute-done((bf16[96,1152]{1,0:T(8,128)(2,1)S(1)}, bf16[96,1152]{1,0:T(8,128)(2,1)S(1)}, u32[]{:S(2)}, u32[]{:S(2)}) %collective-permute-start.17) | collective-permute-done | bytes 221216 | tf_op jit(solution)/shard_map/ppermute | solution.py:152
  54.7 0.8 %collective-permute-done.18.across = bf16[96,1152]{1,0:T(8,128)(2,1)S(1)} collective-permute-done((bf16[96,1152]{1,0:T(8,128)(2,1)S(1)}, bf16[96,1152]{1,0:T(8,128)(2,1)S(1)}, u32[]{:S(2)}, u32[]{:S(2)}) %collective-permute-start.18) | collective-permute-done | bytes 221216 | tf_op jit(solution)/shard_map/ppermute | solution.py:255
  55.5 3.5 %collective-permute-done.19.diagonal = bf16[96,1152]{1,0:T(8,128)(2,1)S(1)} collective-permute-done((bf16[96,1152]{1,0:T(8,128)(2,1)S(1)}, bf16[96,1152]{1,0:T(8,128)(2,1)S(1)}, u32[]{:S(2)}, u32[]{:S(2)}) %collective-permute-start.19) | collective-permute-done | bytes 221216 | tf_op jit(solution)/shard_map/ppermute | solution.py:254
  59.0 0.9 %demb.1.mine = bf16[2,96,1152]{2,1,0:T(8,128)(2,1)S(1)} custom-call(s32[3]{0:T(128)S(1)} %pad_add_fusion.2.place, f32[96,1152]{1,0:T(8,128)S(1)} %get-tuple-element.34.kept, bf16[96,1152]{1,0:T(8,128)(2,1)S(1)} %collective-permute-done.17.near, bf16[96,1152]{1,0:T(8,128)(2,1)S(1)} %collective-permute-done.18.across, ...), custom_call_target="tpu_custom_call" | custom-call | bytes 1991424 | tf_op jit(solution)/shard_map/demb/pallas_call | solution.py:17
  59.9 4.8 %collective-permute-start.20 = (bf16[2,96,1152]{2,1,0:T(8,128)(2,1)S(1)}, bf16[2,96,1152]{2,1,0:T(8,128)(2,1)S(1)}, u32[]{:S(2)}, u32[]{:S(2)}) collective-permute-start(bf16[2,96,1152]{2,1,0:T(8,128)(2,1)S(1)} %demb.1.mine), channel_id=1, source_target_pairs={{0,1},{1,0},{2,3},{3,2},{4,5},{5,4},{6,7},{7,6},{8,9},{9,8},{10,11... | collective-permute-start | bytes 1327112 | tf_op jit(solution)/shard_map/ppermute | solution.py:263
  64.7 0.8 %collective-permute-start.15 = (f32[1,96]{1,0:T(1,128)S(1)}, f32[1,96]{1,0:T(1,128)S(1)}, u32[]{:S(2)}, u32[]{:S(2)}) collective-permute-start(f32[1,96]{1,0:T(1,128)S(1)} %get-tuple-element.33), channel_id=1, source_target_pairs={{0,2},{2,0},{4,6},{6,4},{8,10},{10,8},{12,14},{14,12},{1,3},{3,1},... | collective-permute-start | bytes 1160 | tf_op jit(solution)/shard_map/ppermute | solution.py:152
  65.5 1.6 %collective-permute-done.15 = f32[1,96]{1,0:T(1,128)S(1)} collective-permute-done((f32[1,96]{1,0:T(1,128)S(1)}, f32[1,96]{1,0:T(1,128)S(1)}, u32[]{:S(2)}, u32[]{:S(2)}) %collective-permute-start.15) | collective-permute-done | bytes 416 | tf_op jit(solution)/shard_map/ppermute | solution.py:152
  67.1 1.2 %collective-permute-start.16 = (f32[1,96]{1,0:T(1,128)S(1)}, f32[1,96]{1,0:T(1,128)S(1)}, u32[]{:S(2)}, u32[]{:S(2)}) collective-permute-start(f32[1,96]{1,0:T(1,128)S(1)} %add.8), channel_id=1, source_target_pairs={{0,1},{1,0},{2,3},{3,2},{4,5},{5,4},{6,7},{7,6},{8,9},{9,8},{10,11... | collective-permute-start | bytes 1160 | tf_op jit(solution)/shard_map/ppermute | solution.py:265
  68.3 0.8 %collective-permute-done.16 = f32[1,96]{1,0:T(1,128)S(1)} collective-permute-done((f32[1,96]{1,0:T(1,128)S(1)}, f32[1,96]{1,0:T(1,128)S(1)}, u32[]{:S(2)}, u32[]{:S(2)}) %collective-permute-start.16) | collective-permute-done | bytes 416 | tf_op jit(solution)/shard_map/ppermute | solution.py:265
  69.1 0.6 broadcast_select_fusion
  69.8 2.6 %grads.1 = (bf16[192,384]{1,0:T(8,128)(2,1)}, bf16[192,512]{1,0:T(8,128)(2,1)}) custom-call(s32[3]{0:T(128)S(1)} %pad_add_fusion.2.place, bf16[2,96,1152]{2,1,0:T(8,128)(2,1)S(1)} %demb.1.mine, bf16[2,96,1152]{2,1,0:T(8,128)(2,1)S(1)} %collective-permute-done.20.theirs, bf16[384,1152]{1,0:T(8,128)(2,1)S(1)} %copy-done.3, bf16[512,1152]{1,0:T(8,128)(2,1)S(1)} %copy-done.1), custom_call_target="tpu_custom_call" | custom-call | flops 396361728 | bytes 2949120 | tf_op jit(solution)/shard_map/grads/pallas_call | solution.py:17
  (27 shorter events, 0.3 us)
Async XLA Ops:
  0.7 1.3 %copy-start = (bf16[512,1152]{1,0:T(8,128)(2,1)S(1)}, bf16[512,1152]{1,0:T(8,128)(2,1)}, u32[]{:S(2)}) copy-start(bf16[512,1152]{1,0:T(8,128)(2,1)} %text_proj.5) | copy-start | bytes 3538948
  2.0 1.2 %copy-start.2 = (bf16[384,1152]{1,0:T(8,128)(2,1)S(1)}, bf16[384,1152]{1,0:T(8,128)(2,1)}, u32[]{:S(2)}) copy-start(bf16[384,1152]{1,0:T(8,128)(2,1)} %image_proj.5) | copy-start | bytes 2654212
  3.2 0.9 %copy-start.4 = (bf16[192,512]{1,0:T(8,128)(2,1)S(1)}, bf16[192,512]{1,0:T(8,128)(2,1)}, u32[]{:S(2)}) copy-start(bf16[192,512]{1,0:T(8,128)(2,1)} %text_pooled.3) | copy-start | bytes 589828
  4.1 0.9 %copy-start.5 = (bf16[192,384]{1,0:T(8,128)(2,1)S(1)}, bf16[192,384]{1,0:T(8,128)(2,1)}, u32[]{:S(2)}) copy-start(bf16[192,384]{1,0:T(8,128)(2,1)} %image_pooled.3) | copy-start | bytes 442372
  6.0 2.2 %collective-permute-start = (bf16[2,96,1152]{2,1,0:T(8,128)(2,1)S(1)}, bf16[2,96,1152]{2,1,0:T(8,128)(2,1)S(1)}, u32[]{:S(2)}, u32[]{:S(2)}) collective-permute-start(bf16[2,96,1152]{2,1,0:T(8,128)(2,1)S(1)} %embed_sent.1), channel_id=1, source_target_pairs={{0,1},{1,0},{2,3},{3,2},{4,5},{5,4},{6,7},{7,6},{8,9},{9,8},{10,11... | collective-permute-start | bytes 1327112 | tf_op jit(solution)/shard_map/ppermute | solution.py:178
  7.8 7.9 %copy-start.6 = (s32[192]{0:T(256)S(1)}, s32[192]{0:T(256)}, u32[]{:S(2)}) copy-start(s32[192]{0:T(256)} %param.13) | copy-start | bytes 2308
  8.9 6.7 %collective-permute-start.1 = (bf16[96,1152]{1,0:T(8,128)(2,1)S(1)}, bf16[96,1152]{1,0:T(8,128)(2,1)S(1)}, u32[]{:S(2)}, u32[]{:S(2)}) collective-permute-start(bf16[96,1152]{1,0:T(8,128)(2,1)S(1)} %get-tuple-element.24), channel_id=1, source_target_pairs={{0,16},{16,0},{1,17},{17,1},{2,18},{18,2},{3,19},{19,3},{4,20},{20... | collective-permute-start | bytes 663560 | tf_op jit(solution)/shard_map/ppermute | solution.py:195
  9.2 11.1 %collective-permute-start.6 = (bf16[96,1152]{1,0:T(8,128)(2,1)S(1)}, bf16[96,1152]{1,0:T(8,128)(2,1)S(1)}, u32[]{:S(2)}, u32[]{:S(2)}) collective-permute-start(bf16[96,1152]{1,0:T(8,128)(2,1)S(1)} %get-tuple-element.28), channel_id=1, source_target_pairs={{0,16},{16,0},{1,17},{17,1},{2,18},{18,2},{3,19},{19,3},{4,20},{20... | collective-permute-start | bytes 663560 | tf_op jit(solution)/shard_map/ppermute | solution.py:194
  15.7 8.5 %collective-permute-start.11 = (s32[1,192]{1,0:T(1,128)S(1)}, s32[1,192]{1,0:T(1,128)S(1)}, u32[]{:S(2)}, u32[]{:S(2)}) collective-permute-start(s32[1,192]{1,0:T(1,128)S(1)} %bitcast.6), channel_id=1, source_target_pairs={{0,4},{2,6},{4,0},{6,2},{8,12},{10,14},{12,8},{14,10},{1,5},{3,7},... | collective-permute-start | bytes 2312 | tf_op jit(solution)/shard_map/ppermute | solution.py:152
  17.1 4.8 %collective-permute-start.3 = (s32[1,192]{1,0:T(1,128)S(1)}, s32[1,192]{1,0:T(1,128)S(1)}, u32[]{:S(2)}, u32[]{:S(2)}) collective-permute-start(s32[1,192]{1,0:T(1,128)S(1)} %bitcast.7), channel_id=1, source_target_pairs={{0,2},{2,0},{4,6},{6,4},{8,10},{10,8},{12,14},{14,12},{1,3},{3,1},... | collective-permute-start | bytes 2312 | tf_op jit(solution)/shard_map/ppermute | solution.py:152
  18.3 6.3 %collective-permute-start.4 = (s32[1,192]{1,0:T(1,128)S(1)}, s32[1,192]{1,0:T(1,128)S(1)}, u32[]{:S(2)}, u32[]{:S(2)}) collective-permute-start(s32[1,192]{1,0:T(1,128)S(1)} %bitcast.8), channel_id=1, source_target_pairs={{0,8},{2,10},{4,12},{6,14},{8,0},{10,2},{12,4},{14,6},{1,9},{3,11}... | collective-permute-start | bytes 2312 | tf_op jit(solution)/shard_map/ppermute | solution.py:152
  20.5 22.2 %collective-permute-start.13 = (bf16[96,1152]{1,0:T(8,128)(2,1)S(1)}, bf16[96,1152]{1,0:T(8,128)(2,1)S(1)}, u32[]{:S(2)}, u32[]{:S(2)}) collective-permute-start(bf16[96,1152]{1,0:T(8,128)(2,1)S(1)} %get-tuple-element.29.refs_0_), channel_id=1, source_target_pairs={{0,4},{2,6},{4,0},{6,2},{8,12},{10,14},{12,8},{14,10},{1,5},{3,7},... | collective-permute-start | bytes 663560 | tf_op jit(solution)/shard_map/ppermute | solution.py:152
  21.8 23.6 %collective-permute-start.9 = (bf16[96,1152]{1,0:T(8,128)(2,1)S(1)}, bf16[96,1152]{1,0:T(8,128)(2,1)S(1)}, u32[]{:S(2)}, u32[]{:S(2)}) collective-permute-start(bf16[96,1152]{1,0:T(8,128)(2,1)S(1)} %get-tuple-element.29.refs_0_), channel_id=1, source_target_pairs={{0,12},{2,14},{4,8},{6,10},{8,4},{10,6},{12,0},{14,2},{1,13},{3,15... | collective-permute-start | bytes 663560 | tf_op jit(solution)/shard_map/ppermute | solution.py:152
  21.9 23.6 %collective-permute-start.7 = (bf16[96,1152]{1,0:T(8,128)(2,1)S(1)}, bf16[96,1152]{1,0:T(8,128)(2,1)S(1)}, u32[]{:S(2)}, u32[]{:S(2)}) collective-permute-start(bf16[96,1152]{1,0:T(8,128)(2,1)S(1)} %get-tuple-element.29.refs_0_), channel_id=1, source_target_pairs={{0,8},{2,10},{4,12},{6,14},{8,0},{10,2},{12,4},{14,6},{1,9},{3,11}... | collective-permute-start | bytes 663560 | tf_op jit(solution)/shard_map/ppermute | solution.py:152
  24.2 17.6 %collective-permute-start.5 = (s32[1,192]{1,0:T(1,128)S(1)}, s32[1,192]{1,0:T(1,128)S(1)}, u32[]{:S(2)}, u32[]{:S(2)}) collective-permute-start(s32[1,192]{1,0:T(1,128)S(1)} %bitcast.10), channel_id=1, source_target_pairs={{0,12},{2,14},{4,8},{6,10},{8,4},{10,6},{12,0},{14,2},{1,13},{3,15... | collective-permute-start | bytes 2312 | tf_op jit(solution)/shard_map/ppermute | solution.py:152
  24.6 21.5 %collective-permute-start.12 = (bf16[96,1152]{1,0:T(8,128)(2,1)S(1)}, bf16[96,1152]{1,0:T(8,128)(2,1)S(1)}, u32[]{:S(2)}, u32[]{:S(2)}) collective-permute-start(bf16[96,1152]{1,0:T(8,128)(2,1)S(1)} %get-tuple-element.29.refs_0_), channel_id=1, source_target_pairs={{0,1},{1,0},{2,3},{3,2},{4,5},{5,4},{6,7},{7,6},{8,9},{9,8},{10,11... | collective-permute-start | bytes 663560 | tf_op jit(solution)/shard_map/ppermute | solution.py:210
  41.9 4.8 %collective-permute-start.2 = (bf16[96,1152]{1,0:T(8,128)(2,1)S(1)}, bf16[96,1152]{1,0:T(8,128)(2,1)S(1)}, u32[]{:S(2)}, u32[]{:S(2)}) collective-permute-start(bf16[96,1152]{1,0:T(8,128)(2,1)S(1)} %get-tuple-element.25.own_a), channel_id=1, source_target_pairs={{0,2},{2,0},{4,6},{6,4},{8,10},{10,8},{12,14},{14,12},{1,3},{3,1},... | collective-permute-start | bytes 663560 | tf_op jit(solution)/shard_map/ppermute | solution.py:152
  42.6 4.0 %collective-permute-start.14 = (bf16[96,1152]{1,0:T(8,128)(2,1)S(1)}, bf16[96,1152]{1,0:T(8,128)(2,1)S(1)}, u32[]{:S(2)}, u32[]{:S(2)}) collective-permute-start(bf16[96,1152]{1,0:T(8,128)(2,1)S(1)} %collective-permute-done.13.refs_2_), channel_id=1, source_target_pairs={{0,1},{1,0},{2,3},{3,2},{4,5},{5,4},{6,7},{7,6},{8,9},{9,8},{10,11... | collective-permute-start | bytes 663560 | tf_op jit(solution)/shard_map/ppermute | solution.py:210
  45.5 2.8 %collective-permute-start.10 = (bf16[96,1152]{1,0:T(8,128)(2,1)S(1)}, bf16[96,1152]{1,0:T(8,128)(2,1)S(1)}, u32[]{:S(2)}, u32[]{:S(2)}) collective-permute-start(bf16[96,1152]{1,0:T(8,128)(2,1)S(1)} %collective-permute-done.9.refs_2_), channel_id=1, source_target_pairs={{0,1},{1,0},{2,3},{3,2},{4,5},{5,4},{6,7},{7,6},{8,9},{9,8},{10,11... | collective-permute-start | bytes 663560 | tf_op jit(solution)/shard_map/ppermute | solution.py:210
  45.5 2.7 %collective-permute-start.8 = (bf16[96,1152]{1,0:T(8,128)(2,1)S(1)}, bf16[96,1152]{1,0:T(8,128)(2,1)S(1)}, u32[]{:S(2)}, u32[]{:S(2)}) collective-permute-start(bf16[96,1152]{1,0:T(8,128)(2,1)S(1)} %collective-permute-done.7.refs_0_), channel_id=1, source_target_pairs={{0,1},{1,0},{2,3},{3,2},{4,5},{5,4},{6,7},{7,6},{8,9},{9,8},{10,11... | collective-permute-start | bytes 663560 | tf_op jit(solution)/shard_map/ppermute | solution.py:210
  49.9 4.8 %collective-permute-start.17 = (bf16[96,1152]{1,0:T(8,128)(2,1)S(1)}, bf16[96,1152]{1,0:T(8,128)(2,1)S(1)}, u32[]{:S(2)}, u32[]{:S(2)}) collective-permute-start(bf16[96,1152]{1,0:T(8,128)(2,1)S(1)} %get-tuple-element.35), channel_id=1, source_target_pairs={{0,2},{2,0},{4,6},{6,4},{8,10},{10,8},{12,14},{14,12},{1,3},{3,1},... | collective-permute-start | bytes 663560 | tf_op jit(solution)/shard_map/ppermute | solution.py:152
  50.7 4.8 %collective-permute-start.18 = (bf16[96,1152]{1,0:T(8,128)(2,1)S(1)}, bf16[96,1152]{1,0:T(8,128)(2,1)S(1)}, u32[]{:S(2)}, u32[]{:S(2)}) collective-permute-start(bf16[96,1152]{1,0:T(8,128)(2,1)S(1)} %get-tuple-element.36), channel_id=1, source_target_pairs={{0,16},{16,0},{1,17},{17,1},{2,18},{18,2},{3,19},{19,3},{4,20},{20... | collective-permute-start | bytes 663560 | tf_op jit(solution)/shard_map/ppermute | solution.py:255
  51.0 8.0 %collective-permute-start.19 = (bf16[96,1152]{1,0:T(8,128)(2,1)S(1)}, bf16[96,1152]{1,0:T(8,128)(2,1)S(1)}, u32[]{:S(2)}, u32[]{:S(2)}) collective-permute-start(bf16[96,1152]{1,0:T(8,128)(2,1)S(1)} %get-tuple-element.35), channel_id=1, source_target_pairs={{0,18},{2,16},{4,22},{6,20},{8,26},{10,24},{12,30},{14,28},{16,2},... | collective-permute-start | bytes 663560 | tf_op jit(solution)/shard_map/ppermute | solution.py:254
  59.0 10.8 %copy-start.1 = (bf16[512,1152]{1,0:T(8,128)(2,1)S(1)}, bf16[512,1152]{1,0:T(8,128)(2,1)}, u32[]{:S(2)}) copy-start(bf16[512,1152]{1,0:T(8,128)(2,1)} %text_proj.5) | copy-start | bytes 3538948
  59.0 10.8 %copy-start.3 = (bf16[384,1152]{1,0:T(8,128)(2,1)S(1)}, bf16[384,1152]{1,0:T(8,128)(2,1)}, u32[]{:S(2)}) copy-start(bf16[384,1152]{1,0:T(8,128)(2,1)} %image_proj.5) | copy-start | bytes 2654212
  59.9 9.9 %collective-permute-start.20 = (bf16[2,96,1152]{2,1,0:T(8,128)(2,1)S(1)}, bf16[2,96,1152]{2,1,0:T(8,128)(2,1)S(1)}, u32[]{:S(2)}, u32[]{:S(2)}) collective-permute-start(bf16[2,96,1152]{2,1,0:T(8,128)(2,1)S(1)} %demb.1.mine), channel_id=1, source_target_pairs={{0,1},{1,0},{2,3},{3,2},{4,5},{5,4},{6,7},{7,6},{8,9},{9,8},{10,11... | collective-permute-start | bytes 1327112 | tf_op jit(solution)/shard_map/ppermute | solution.py:263
  64.7 2.4 %collective-permute-start.15 = (f32[1,96]{1,0:T(1,128)S(1)}, f32[1,96]{1,0:T(1,128)S(1)}, u32[]{:S(2)}, u32[]{:S(2)}) collective-permute-start(f32[1,96]{1,0:T(1,128)S(1)} %get-tuple-element.33), channel_id=1, source_target_pairs={{0,2},{2,0},{4,6},{6,4},{8,10},{10,8},{12,14},{14,12},{1,3},{3,1},... | collective-permute-start | bytes 1160 | tf_op jit(solution)/shard_map/ppermute | solution.py:152
  67.1 2.0 %collective-permute-start.16 = (f32[1,96]{1,0:T(1,128)S(1)}, f32[1,96]{1,0:T(1,128)S(1)}, u32[]{:S(2)}, u32[]{:S(2)}) collective-permute-start(f32[1,96]{1,0:T(1,128)S(1)} %add.8), channel_id=1, source_target_pairs={{0,1},{1,0},{2,3},{3,2},{4,5},{5,4},{6,7},{7,6},{8,9},{9,8},{10,11... | collective-permute-start | bytes 1160 | tf_op jit(solution)/shard_map/ppermute | solution.py:265

commit v2 on v1

v2 whole, which is shorter than its diff:
```python
import jax
import jax.numpy as jnp
from jax import lax
from jax.experimental import pallas as pl
from jax.experimental.pallas import tpu as pltpu
from jax.sharding import PartitionSpec as P

F32 = jnp.float32
BF16 = jnp.bfloat16
SWAP = [(0, 1), (1, 0)]
NT = (((1,), (1,)), ((), ()))
VMEM_LIMIT = 16 * 1024 * 1024
LANES = 128
EXTRA = 8


def local_call(
    kernel, name, outs, scalars, arrays, scratch=(), flops=0, transcendentals=0, held=(),
):
    nbytes = sum(a.size * a.dtype.itemsize for a in (*arrays, *held))
    return pl.pallas_call(
        kernel,
        out_shape=outs,
        in_specs=[pl.BlockSpec(memory_space=pltpu.SMEM)] * len(scalars)
        + [pl.BlockSpec(memory_space=pltpu.VMEM)] * len(arrays)
        + [pl.BlockSpec(memory_space=pltpu.HBM)] * len(held),
        out_specs=[pl.BlockSpec(memory_space=pltpu.VMEM)] * len(outs),
        scratch_shapes=list(scratch),
        compiler_params=pltpu.CompilerParams(vmem_limit_bytes=VMEM_LIMIT),
        cost_estimate=pl.CostEstimate(
            flops=flops, bytes_accessed=nbytes, transcendentals=transcendentals
        ),
        name=name,
    )(*scalars, *arrays, *held)


def cuts(rows):
    size = 128 if rows % 128 == 0 else rows
    return [(start, size) for start in range(0, rows, size)]


def embed_rows(which, place, image_pooled, text_pooled, image_proj, text_proj, out, before):
    half = out.shape[1]
    core = place[2]
    start = pl.multiple_of((core if which == 0 else 1 - core) * half, half)
    rows = pl.ds(start, half)
    for index, (pooled, proj) in enumerate(
        ((image_pooled, image_proj), (text_pooled, text_proj))
    ):
        for copy in before[index]:
            copy.wait()
        out[index] = jnp.dot(pooled[rows, :], proj[...], preferred_element_type=F32).astype(
            out.dtype
        )


def embed_sent_kernel(place, *refs):
    sources, sent, held, sems = refs[:4], refs[4], refs[5:9], refs[9]
    before = [[], []]
    count = 0
    for index in (0, 2, 1, 3):
        source, target = sources[index], held[index]
        for start, size in cuts(source.shape[0]):
            rows = pl.ds(start, size)
            copy = pltpu.make_async_copy(source.at[rows], target.at[rows], sems.at[count])
            copy.start()
            before[index % 2].append(copy)
            count += 1
    embed_rows(1, place, *held, sent, before)


def embed_kept_kernel(place, *refs):
    embed_rows(0, place, *refs[:4], refs[4], [[], []])


def join_cores_kernel(place, kept, got, own_send, other_send):
    section = place[0]
    own_send[...] = (kept[section] + got[section].astype(F32)).astype(BF16)
    other_send[...] = (kept[1 - section] + got[1 - section].astype(F32)).astype(BF16)


def write_block(block, value, extra):
    half, width = value.shape
    for c in range(width // LANES):
        block[pl.ds(c * half, half), :] = value[:, c * LANES : (c + 1) * LANES].astype(BF16)
    block[pl.ds(half * (width // LANES), EXTRA), :] = extra.astype(BF16)


def read_block(block, target, start, half):
    for c in range(target.shape[1] // LANES):
        target[pl.ds(start, half), pl.ds(c * LANES, LANES)] = block[pl.ds(c * half, half), :]


def extra_rows(block):
    return block[pl.ds(block.shape[0] - EXTRA, EXTRA), :].astype(F32)


def block_ids(block):
    extra = extra_rows(block)
    return extra[0:1] * 128.0 + extra[1:2]


def split_rows(row, extra):
    high = row.astype(BF16).astype(F32)
    rest = row - high
    middle = rest.astype(BF16).astype(F32)
    extra[...] = jnp.zeros_like(extra)
    for index, part in enumerate((high, middle, rest - middle)):
        extra[index : index + 1, 0 : row.shape[1]] = part


def unit_kernel(own):
    def kernel(place, kept, got, summed, extra, unit, block, norm):
        section = place[0] if own else 1 - place[0]
        emb = kept[section] + got[section].astype(F32) + summed[...].astype(F32)
        row_norm = jnp.sqrt(jnp.sum(emb * emb, axis=1, keepdims=True) + 1e-06)
        value = emb / row_norm
        unit[...] = value
        norm[...] = row_norm
        write_block(block, value, extra[...].astype(F32))

    return kernel


def pair_kernel(blocks, first, last):
    def kernel(scale_bias, own_block, near_block, own_ids, *refs):
        pieces = refs[: 2 * blocks]
        refs = refs[2 * blocks :]
        if not first:
            grad_in, loss_in = refs[:2]
            refs = refs[2:]
        if last:
            grad_keep, grad_own, grad_near, loss_own = refs[:4]
            refs = refs[4:]
        else:
            grad_out, loss_out = refs[:2]
            refs = refs[2:]
        own, visited, visit_ids, extra = refs
        half = own.shape[0] // 2
        read_block(own_block, own, 0, half)
        read_block(near_block, own, half, half)
        for index, piece in enumerate(pieces):
            read_block(piece, visited, index * half, half)
            visit_ids[0:1, pl.ds(index * half, half)] = block_ids(piece)[:, :half]
        near_ids = jnp.transpose(jnp.broadcast_to(block_ids(near_block), (LANES, LANES)))
        ids = jnp.concatenate([own_ids[...], near_ids[:half, 0:1]], axis=0)
        scale = scale_bias[0]
        scores = (
            scale * lax.dot_general(own[...], visited[...], NT, preferred_element_type=F32)
            + scale_bias[1]
        )
        sign = jnp.where(ids == visit_ids[0:1, :], 1.0, -1.0).astype(F32)
        value = -sign * scores
        small = jnp.exp(-jnp.abs(value))
        losses = jnp.maximum(value, 0.0) + jnp.log1p(small)
        sigmoid = jnp.where(value >= 0.0, 1.0, small) / (1.0 + small)
        weight = (-scale * sign * sigmoid).astype(BF16)
        grad = jnp.dot(weight, visited[...], preferred_element_type=F32)
        loss = jnp.sum(losses, axis=1, keepdims=True)
        if not first:
            grad = grad + grad_in[...]
            loss = loss + loss_in[...]
        if last:
            grad_keep[...] = grad[:half]
            grad_own[...] = grad[:half].astype(BF16)
            wide = jnp.broadcast_to(loss, (2 * half, LANES))
            loss_own[...] = jnp.transpose(wide[:half])[0:1]
            split_rows(jnp.transpose(wide[half:])[0:1], extra)
            write_block(grad_near, grad[half:], extra[...])
        else:
            grad_out[...] = grad
            loss_out[...] = loss

    return kernel


def demb_kernel(
    place, kept, near, across, diagonal, own_unit, own_norm, other_unit, other_norm, loss_own,
    out, loss_mine, joined, extra,
):
    section = place[0]
    half, width = own_unit.shape

    def finish(grad, unit, norm):
        value = unit[...]
        along = jnp.sum(value * grad, axis=1, keepdims=True)
        return ((grad - value * along) / norm[...]).astype(BF16)

    rows = pl.ds(0, half)
    read_block(diagonal, joined, 0, half)
    out[1 - section, rows, :] = finish(
        across[...].astype(F32) + joined[...].astype(F32), other_unit, other_norm
    )
    read_block(near, joined, 0, half)
    out[section, rows, :] = finish(kept[...] + joined[...].astype(F32), own_unit, own_norm)
    parts = extra_rows(near)
    loss = loss_own[...] + (parts[0:1] + parts[1:2] + parts[2:3])[:, :half]
    loss_mine[...] = loss
    split_rows(loss, extra)
    out[:, pl.ds(half, EXTRA), :] = jnp.zeros((2, EXTRA, width), BF16)
    out[0, pl.ds(half, EXTRA), pl.ds(0, LANES)] = extra[...].astype(BF16)


def grads_kernel(
    place, mine, theirs, loss_mine, image_proj, text_proj, pair_loss, image_grad, text_grad, joined
):
    half = joined.shape[0] // 2
    core = place[2]
    for index, (proj, grad) in enumerate(((image_proj, image_grad), (text_proj, text_grad))):
        for spot, source in ((core, mine), (1 - core, theirs)):
            rows = pl.ds(pl.multiple_of(spot * half, half), half)
            joined[rows, :] = source[index, pl.ds(0, half), :]
        grad[...] = lax.dot_general(
            joined[...], proj[...], NT, preferred_element_type=F32
        ).astype(BF16)
    parts = theirs[0, pl.ds(half, EXTRA), pl.ds(0, LANES)].astype(F32)
    loss = loss_mine[...]
    loss_theirs = (parts[0:1] + parts[1:2] + parts[2:3])[:, :half]
    pair_loss[0:1, 0:half] = jnp.where(core == 0, loss, loss_theirs)
    pair_loss[0:1, half : 2 * half] = jnp.where(core == 0, loss_theirs, loss)


def make_per_device(mesh):
    sections = mesh.shape["sec"]
    blocks = mesh.shape["blk"]

    def across_blk(value, step):
        return lax.ppermute(value, "blk", [(i, i ^ step) for i in range(blocks)])

    def per_device(
        image_pooled, text_pooled, image_proj, text_proj, log_multiplier, logit_bias, ids
    ):
        section = lax.axis_index("sec")
        core = lax.axis_index("mp")
        place = jnp.stack([section, lax.axis_index("blk"), core]).astype(jnp.int32)
        scale_bias = jnp.concatenate([jnp.exp(log_multiplier), logit_bias])
        rows = image_pooled.shape[0]
        half = rows // 2
        width = image_proj.shape[1]
        block_rows = half * (width // LANES) + EXTRA
        whole_f32 = jax.ShapeDtypeStruct((half, width), F32)
        whole_b16 = jax.ShapeDtypeStruct((half, width), BF16)
        block_b16 = jax.ShapeDtypeStruct((block_rows, LANES), BF16)
        norm_shape = jax.ShapeDtypeStruct((half, 1), F32)
        loss_shape = jax.ShapeDtypeStruct((1, half), F32)
        towers = (image_pooled, text_pooled, image_proj, text_proj)
        embed_flops = 2 * half * width * (image_proj.shape[0] + text_proj.shape[0])

        half_ids = lax.dynamic_slice_in_dim(ids, core * half, half)
        digits = jnp.stack([half_ids >> 7, half_ids & 127]).astype(BF16)
        extra = jnp.pad(digits, ((0, EXTRA - 2), (0, LANES - half)))
        own_ids = half_ids.astype(F32).reshape(half, 1)

        copies = sum(len(cuts(t.shape[0])) for t in towers)
        sent, *towers = local_call(
            embed_sent_kernel,
            "embed_sent",
            [jax.ShapeDtypeStruct((2, half, width), BF16)]
            + [jax.ShapeDtypeStruct(t.shape, t.dtype) for t in towers],
            [place],
            [],
            scratch=[pltpu.SemaphoreType.DMA((copies,))],
            flops=embed_flops,
            held=[pltpu.with_memory_space_constraint(t, pltpu.HBM) for t in towers],
        )
        image_proj, text_proj = towers[2:]
        got = lax.ppermute(sent, "mp", SWAP)
        (kept,) = local_call(
            embed_kept_kernel,
            "embed_kept",
            [jax.ShapeDtypeStruct((2, half, width), F32)],
            [place],
            towers,
            flops=embed_flops,
        )
        own_send, other_send = local_call(
            join_cores_kernel, "join_cores", [whole_b16, whole_b16], [place], [kept, got]
        )
        other_got = lax.ppermute(own_send, "sec", SWAP)
        own_got = lax.ppermute(other_send, "sec", SWAP)
        other_unit, visit, other_norm = local_call(
            unit_kernel(False),
            "other_unit",
            [whole_f32, block_b16, norm_shape],
            [place],
            [kept, got, other_got, extra],
        )
        own_unit, own_block, own_norm = local_call(
            unit_kernel(True),
            "own_unit",
            [whole_f32, block_b16, norm_shape],
            [place],
            [kept, got, own_got, extra],
        )

        steps = list(range(0, blocks, 2))
        mine = [visit] + [across_blk(visit, k) for k in steps[1:]]
        near_block = across_blk(own_block, 1)
        mine = [visit] + [lax.optimization_barrier((v, own_block))[0] for v in mine[1:]]
        theirs = [lax.ppermute(v, "mp", SWAP) for v in mine]

        groups = [list(range(i, min(i + 2, len(steps)))) for i in range(0, len(steps), 2)]
        state = []
        for index, group in enumerate(groups):
            first, last = index == 0, index == len(groups) - 1
            pieces = [p for g in group for p in (mine[g], theirs[g])]
            if last:
                outs = [whole_f32, whole_b16, block_b16, loss_shape]
            else:
                outs = [
                    jax.ShapeDtypeStruct((2 * half, width), F32),
                    jax.ShapeDtypeStruct((2 * half, 1), F32),
                ]
            visited_rows = 2 * half * len(group)
            state = local_call(
                pair_kernel(len(group), first, last),
                "pairs",
                outs,
                [scale_bias],
                [own_block, near_block, own_ids, *pieces, *state],
                scratch=[
                    pltpu.VMEM((2 * half, width), BF16),
                    pltpu.VMEM((visited_rows, width), BF16),
                    pltpu.VMEM((8, visited_rows), F32),
                    pltpu.VMEM((EXTRA, LANES), F32),
                ],
                flops=8 * half * visited_rows * width,
                transcendentals=6 * half * visited_rows,
            )
        grad_keep, grad_own, grad_near, loss_own = state

        pairs = [(s, b) for s in range(sections) for b in range(blocks)]
        diagonal_pairs = [
            (s * blocks + b, (1 - s) * blocks + (b ^ 1)) for s, b in pairs
        ]
        diagonal = lax.ppermute(grad_near, ("sec", "blk"), diagonal_pairs)
        near = across_blk(grad_near, 1)
        across = lax.ppermute(grad_own, "sec", SWAP)
        demb, loss_mine = local_call(
            demb_kernel,
            "demb",
            [jax.ShapeDtypeStruct((2, half + EXTRA, width), BF16), loss_shape],
            [place],
            [
                grad_keep, near, across, diagonal,
                own_unit, own_norm, other_unit, other_norm, loss_own,
            ],
            scratch=[pltpu.VMEM((half, width), BF16), pltpu.VMEM((EXTRA, LANES), F32)],
        )
        demb_got = lax.ppermute(demb, "mp", SWAP)
        return local_call(
            grads_kernel,
            "grads",
            [
                jax.ShapeDtypeStruct((1, rows), F32),
                jax.ShapeDtypeStruct((rows, image_proj.shape[0]), BF16),
                jax.ShapeDtypeStruct((rows, text_proj.shape[0]), BF16),
            ],
            [place],
            [demb, demb_got, loss_mine, image_proj, text_proj],
            scratch=[pltpu.VMEM((rows, width), BF16)],
            flops=2 * embed_flops,
        )

    return per_device


def solution(mesh):
    placed = (
        P("blk", ("sec", "mp")),
        P("blk", ("sec", "mp")),
        P(("sec", "mp"), None),
        P(("sec", "mp"), None),
        P(),
        P(),
        P("blk"),
    )
    return jax.shard_map(
        make_per_device(mesh),
        mesh=mesh,
        in_specs=placed,
        out_specs=(P("sec", "blk"), P("blk", ("sec", "mp")), P("blk", ("sec", "mp"))),
        check_vma=False,
    )
```

time: 72.6 us -> 65.3 us (0.90)
  the two profiles are of different devices: /device:TPU:19 before, /device:TPU:0 now
where the time goes in v2:
time: 65.3 us; the launch traced here: 65.1 us
  waiting for transfers between devices  34 us (52%)
  starting transfers between devices  14.6 us (22%)
  Pallas kernels  13.3 us (20%)
  between operations  2.1 us (3%)
  local copies, waits for them, and re-layouts  0.87 us (1%)
    ppermute x5, waiting for transfers between devices, across_blk(): return lax.ppermute(value, 'blk', [(i, i ^ step) for i in range(blocks)])  13.5 us
    pallas_call x9, Pallas kernels, local_call(): pl.pallas_call(kernel, out_shape=outs, in_specs=[pl.BlockSpec(memory_spac...  13.3 us
    ppermute x1, waiting for transfers between devices, per_device(): across = lax.ppermute(grad_own, 'sec', SWAP)  10.4 us
    ppermute x5, starting transfers between devices, across_blk(): return lax.ppermute(value, 'blk', [(i, i ^ step) for i in range(blocks)])  7.59 us
    ppermute x1, waiting for transfers between devices, per_device(): other_got = lax.ppermute(own_send, 'sec', SWAP)  5.63 us
    ppermute x1, starting transfers between devices, per_device(): other_got = lax.ppermute(own_send, 'sec', SWAP)  2.92 us
    ppermute x1, waiting for transfers between devices, per_device(): own_got = lax.ppermute(other_send, 'sec', SWAP)  2.28 us
    ppermute x1, waiting for transfers between devices, per_device(): demb_got = lax.ppermute(demb, 'mp', SWAP)  1.83 us
  transfers between devices with their start and end apart: 15, of which 7 were waited for; matrix products, arithmetic and copies ran while one was open for 0% of the time, Pallas kernels for 6%

profile of v2, /device:TPU:0, one launch (start us, length us, event | category | flops | bytes accessed | tf_op | source)
XLA Modules:
  0.0 65.1 jit_solution(12100502493950295077)
XLA Ops:
  0.6 0.1 pad_add_fusion.place
  0.7 2.6 %embed_sent.1 = (bf16[2,96,1152]{2,1,0:T(8,128)(2,1)S(1)}, bf16[192,384]{1,0:T(8,128)(2,1)S(1)}, bf16[192,512]{1,0:T(8,128)(2,1)S(1)}, bf16[384,1152]{1,0:T(8,128)(2,1)S(1)}, bf16[512,1152]{1,0:T(8,128)(2,1)S(1)}) custom-call(s32[3]{0:T(128)S(1)} %pad_add_fusion.place, bf16[192,384]{1,0:T(8,128)(2,1)} %refs_0_.1, bf16[192,512]{1,0:T(8,128)(2,1)} %refs_1_.1, ...), custom_call_target="tpu_custom_call" | custom-call | flops 198180864 | bytes 2408448 | tf_op jit(solution)/shard_map/embed_sent/pallas_call | solution.py:21
  3.3 0.5 collective-permute-start
  3.8 1.0 %embed_kept.1.kept = f32[2,96,1152]{2,1,0:T(8,128)S(1)} custom-call(s32[3]{0:T(128)S(1)} %pad_add_fusion.place, bf16[192,384]{1,0:T(8,128)(2,1)S(1)} %get-tuple-element.27.refs_0_, bf16[192,512]{1,0:T(8,128)(2,1)S(1)} %get-tuple-element.28.refs_1_, bf16[384,1152]{1,0:T(8,128)(2,1)S(1)} %get-tuple-element.29.refs_2_.image_proj, ...), custom_call_target="tpu_custom_call" | custom-call | flops 198180864 | bytes 2408448 | tf_op jit(solution)/shard_map/embed_kept/pallas_call | solution.py:21
  4.9 0.0 copy-start.2
  4.9 0.4 collective-permute-done.got
  5.2 0.6 join_cores.1
  5.9 2.9 %collective-permute-start.3 = (bf16[96,1152]{1,0:T(8,128)(2,1)S(1)}, bf16[96,1152]{1,0:T(8,128)(2,1)S(1)}, u32[]{:S(2)}, u32[]{:S(2)}) collective-permute-start(bf16[96,1152]{1,0:T(8,128)(2,1)S(1)} %get-tuple-element.34), channel_id=1, source_target_pairs={{0,16},{16,0},{1,17},{17,1},{2,18},{18,2},{3,19},{19,3},{4,20},{20... | collective-permute-start | bytes 663560 | tf_op jit(solution)/shard_map/ppermute | solution.py:279
  8.8 0.0 copy-done.2
  8.8 0.1 convert_bitcast_fusion
  8.9 5.6 %collective-permute-done.3.summed = bf16[96,1152]{1,0:T(8,128)(2,1)S(1)} collective-permute-done((bf16[96,1152]{1,0:T(8,128)(2,1)S(1)}, bf16[96,1152]{1,0:T(8,128)(2,1)S(1)}, u32[]{:S(2)}, u32[]{:S(2)}) %collective-permute-start.3) | collective-permute-done | bytes 221216 | tf_op jit(solution)/shard_map/ppermute | solution.py:279
  14.6 0.7 %other_unit.1 = (f32[96,1152]{1,0:T(8,128)S(1)}, bf16[872,128]{1,0:T(8,128)(2,1)S(1)}, f32[96,1]{1,0:T(8,128)S(1)}) custom-call(s32[3]{0:T(128)S(1)} %pad_add_fusion.place, f32[2,96,1152]{2,1,0:T(8,128)S(1)} %embed_kept.1.kept, bf16[2,96,1152]{2,1,0:T(8,128)(2,1)S(1)} %collective-permute-done.got, bf16[96,1152]{1,0:T(8,128)(2,1)S(1)} %collective-permute-done.3.summed, ...), custom_call_target="tpu_custom_call" | custom-call | bytes 1550336 | tf_op jit(solution)/shard_map/other_unit/pallas_call | solution.py:21
  15.3 1.9 %collective-permute-start.9 = (bf16[872,128]{1,0:T(8,128)(2,1)S(1)}, bf16[872,128]{1,0:T(8,128)(2,1)}, u32[]{:S(2)}, u32[]{:S(2)}) collective-permute-start(bf16[872,128]{1,0:T(8,128)(2,1)S(1)} %get-tuple-element.35.refs_0_), channel_id=1, source_target_pairs={{0,4},{2,6},{4,0},{6,2},{8,12},{10,14},{12,8},{14,10},{1,5},{3,7},... | collective-permute-start | bytes 669704 | tf_op jit(solution)/shard_map/ppermute | solution.py:228
  17.2 1.5 %collective-permute-start.1 = (bf16[96,1152]{1,0:T(8,128)(2,1)S(1)}, bf16[96,1152]{1,0:T(8,128)(2,1)S(1)}, u32[]{:S(2)}, u32[]{:S(2)}) collective-permute-start(bf16[96,1152]{1,0:T(8,128)(2,1)S(1)} %get-tuple-element.32), channel_id=1, source_target_pairs={{0,16},{16,0},{1,17},{17,1},{2,18},{18,2},{3,19},{19,3},{4,20},{20... | collective-permute-start | bytes 663560 | tf_op jit(solution)/shard_map/ppermute | solution.py:280
  18.7 2.5 %collective-permute-start.6 = (bf16[872,128]{1,0:T(8,128)(2,1)S(1)}, bf16[872,128]{1,0:T(8,128)(2,1)}, u32[]{:S(2)}, u32[]{:S(2)}) collective-permute-start(bf16[872,128]{1,0:T(8,128)(2,1)S(1)} %get-tuple-element.35.refs_0_), channel_id=1, source_target_pairs={{0,12},{2,14},{4,8},{6,10},{8,4},{10,6},{12,0},{14,2},{1,13},{3,15... | collective-permute-start | bytes 669704 | tf_op jit(solution)/shard_map/ppermute | solution.py:228
  21.1 0.1 collective-permute-start.4
  21.3 0.0 collective-permute-start.8
  21.3 2.3 %collective-permute-done.1.summed = bf16[96,1152]{1,0:T(8,128)(2,1)S(1)} collective-permute-done((bf16[96,1152]{1,0:T(8,128)(2,1)S(1)}, bf16[96,1152]{1,0:T(8,128)(2,1)S(1)}, u32[]{:S(2)}, u32[]{:S(2)}) %collective-permute-start.1) | collective-permute-done | bytes 221216 | tf_op jit(solution)/shard_map/ppermute | solution.py:280
  23.5 0.7 %own_unit.1 = (f32[96,1152]{1,0:T(8,128)S(1)}, bf16[872,128]{1,0:T(8,128)(2,1)S(1)}, f32[96,1]{1,0:T(8,128)S(1)}) custom-call(s32[3]{0:T(128)S(1)} %pad_add_fusion.place, f32[2,96,1152]{2,1,0:T(8,128)S(1)} %embed_kept.1.kept, bf16[2,96,1152]{2,1,0:T(8,128)(2,1)S(1)} %collective-permute-done.got, bf16[96,1152]{1,0:T(8,128)(2,1)S(1)} %collective-permute-done.1.summed, ...), custom_call_target="tpu_custom_call" | custom-call | bytes 1550336 | tf_op jit(solution)/shard_map/own_unit/pallas_call | solution.py:21
  24.3 0.0 copy-start
  24.3 0.8 %copy-done = f32[96,1152]{1,0:T(8,128)} copy-done((f32[96,1152]{1,0:T(8,128)}, f32[96,1152]{1,0:T(8,128)S(1)}, u32[]{:S(2)}) %copy-start) | copy-done | bytes 442392
  25.0 1.5 %collective-permute-start.2 = (bf16[872,128]{1,0:T(8,128)(2,1)S(1)}, bf16[872,128]{1,0:T(8,128)(2,1)S(1)}, u32[]{:S(2)}, u32[]{:S(2)}) collective-permute-start(bf16[872,128]{1,0:T(8,128)(2,1)S(1)} %get-tuple-element.33.own_block), channel_id=1, source_target_pairs={{0,2},{2,0},{4,6},{6,4},{8,10},{10,8},{12,14},{14,12},{1,3},{3,1},... | collective-permute-start | bytes 669704 | tf_op jit(solution)/shard_map/ppermute | solution.py:228
  26.6 0.0 collective-permute-done.9.refs_2_
  26.6 0.0 collective-permute-start.10
  26.6 4.4 %collective-permute-done.6.refs_2_ = bf16[872,128]{1,0:T(8,128)(2,1)} collective-permute-done((bf16[872,128]{1,0:T(8,128)(2,1)S(1)}, bf16[872,128]{1,0:T(8,128)(2,1)}, u32[]{:S(2)}, u32[]{:S(2)}) %collective-permute-start.6) | collective-permute-done | bytes 223264 | tf_op jit(solution)/shard_map/ppermute | solution.py:228
  31.0 0.0 collective-permute-start.7
  31.0 9.1 %collective-permute-done.4.refs_0_ = bf16[872,128]{1,0:T(8,128)(2,1)} collective-permute-done((bf16[872,128]{1,0:T(8,128)(2,1)S(1)}, bf16[872,128]{1,0:T(8,128)(2,1)}, u32[]{:S(2)}, u32[]{:S(2)}) %collective-permute-start.4) | collective-permute-done | bytes 223264 | tf_op jit(solution)/shard_map/ppermute | solution.py:228
  40.1 0.0 collective-permute-start.5
  40.1 0.1 copy.11.own_ids
  41.5 0.1 pad_maximum_fusion.scale_bias
  41.6 0.0 collective-permute-done.8.refs_1_
  41.6 0.0 collective-permute-done.2.near_block
  41.6 0.0 collective-permute-done.10.refs_3_
  41.6 2.2 %pairs.2 = (f32[192,1152]{1,0:T(8,128)S(1)}, f32[192,1]{1,0:T(8,128)S(1)}) custom-call(f32[2]{0:T(128)S(1)} %pad_maximum_fusion.scale_bias, bf16[872,128]{1,0:T(8,128)(2,1)S(1)} %get-tuple-element.33.own_block, bf16[872,128]{1,0:T(8,128)(2,1)S(1)} %collective-permute-done.2.near_block, f32[96,1]{1,0:T(8,128)S(1)} %copy.11.own_ids, ...), custom_call_target="tpu_custom_call" | custom-call | flops 339738624 | bytes 1339776 | tf_op jit(solution)/shard_map/pairs/pallas_call | solution.py:21
  43.9 0.0 collective-permute-done.7.refs_3_
  43.9 0.0 collective-permute-done.5.refs_1_
  43.9 0.0 copy-start.1
  43.9 2.4 %pairs.3 = (f32[96,1152]{1,0:T(8,128)S(1)}, bf16[96,1152]{1,0:T(8,128)(2,1)S(1)}, bf16[872,128]{1,0:T(8,128)(2,1)S(1)}, f32[1,96]{1,0:T(1,128)S(1)}) custom-call(f32[2]{0:T(128)S(1)} %pad_maximum_fusion.scale_bias, bf16[872,128]{1,0:T(8,128)(2,1)S(1)} %get-tuple-element.33.own_block, bf16[872,128]{1,0:T(8,128)(2,1)S(1)} %collective-permute-done.2.near_block, ...), custom_call_target="tpu_custom_call" | custom-call | flops 339738624 | bytes 2225280 | tf_op jit(solution)/shard_map/pairs/pallas_call | solution.py:21
  46.3 1.6 %collective-permute-start.11 = (bf16[872,128]{1,0:T(8,128)(2,1)S(1)}, bf16[872,128]{1,0:T(8,128)(2,1)S(1)}, u32[]{:S(2)}, u32[]{:S(2)}) collective-permute-start(bf16[872,128]{1,0:T(8,128)(2,1)S(1)} %get-tuple-element.42), channel_id=1, source_target_pairs={{0,2},{2,0},{4,6},{6,4},{8,10},{10,8},{12,14},{14,12},{1,3},{3,1},... | collective-permute-start | bytes 669704 | tf_op jit(solution)/shard_map/ppermute | solution.py:228
  47.9 0.5 collective-permute-start.13
  48.3 1.5 %collective-permute-start.12 = (bf16[96,1152]{1,0:T(8,128)(2,1)S(1)}, bf16[96,1152]{1,0:T(8,128)(2,1)S(1)}, u32[]{:S(2)}, u32[]{:S(2)}) collective-permute-start(bf16[96,1152]{1,0:T(8,128)(2,1)S(1)} %get-tuple-element.43), channel_id=1, source_target_pairs={{0,16},{16,0},{1,17},{17,1},{2,18},{18,2},{3,19},{19,3},{4,20},{20... | collective-permute-start | bytes 663560 | tf_op jit(solution)/shard_map/ppermute | solution.py:338
  49.8 10.4 %collective-permute-done.12.across = bf16[96,1152]{1,0:T(8,128)(2,1)S(1)} collective-permute-done((bf16[96,1152]{1,0:T(8,128)(2,1)S(1)}, bf16[96,1152]{1,0:T(8,128)(2,1)S(1)}, u32[]{:S(2)}, u32[]{:S(2)}) %collective-permute-start.12) | collective-permute-done | bytes 221216 | tf_op jit(solution)/shard_map/ppermute | solution.py:338
  60.2 0.0 collective-permute-done.11.near
  60.2 0.0 collective-permute-done.13.diagonal
  60.2 1.0 %demb.1 = (bf16[2,104,1152]{2,1,0:T(8,128)(2,1)S(1)}, f32[1,96]{1,0:T(1,128)S(1)}) custom-call(s32[3]{0:T(128)S(1)} %pad_add_fusion.place, f32[96,1152]{1,0:T(8,128)S(1)} %get-tuple-element.41.kept, bf16[872,128]{1,0:T(8,128)(2,1)S(1)} %collective-permute-done.11.near, bf16[96,1152]{1,0:T(8,128)(2,1)S(1)} %collective-permute-done.12.across, ...), custom_call_target="tpu_custom_call" | custom-call | bytes 1995904 | tf_op jit(solution)/shard_map/demb/pallas_call | solution.py:21
  61.2 0.1 collective-permute-start.14
  61.2 1.8 %collective-permute-done.14.theirs = bf16[2,104,1152]{2,1,0:T(8,128)(2,1)S(1)} collective-permute-done((bf16[2,104,1152]{2,1,0:T(8,128)(2,1)S(1)}, bf16[2,104,1152]{2,1,0:T(8,128)(2,1)S(1)}, u32[]{:S(2)}, u32[]{:S(2)}) %collective-permute-start.14) | collective-permute-done | bytes 479264 | tf_op jit(solution)/shard_map/ppermute | solution.py:350
  63.1 2.0 %grads.1 = (f32[1,192]{1,0:T(1,128)}, bf16[192,384]{1,0:T(8,128)(2,1)}, bf16[192,512]{1,0:T(8,128)(2,1)}) custom-call(s32[3]{0:T(128)S(1)} %pad_add_fusion.place, bf16[2,104,1152]{2,1,0:T(8,128)(2,1)S(1)} %get-tuple-element.49.mine, bf16[2,104,1152]{2,1,0:T(8,128)(2,1)S(1)} %collective-permute-done.14.theirs, f32[1,96]{1,0:T(1,128)S(1)} %get-tuple-element.50.loss_mine, ...), custom_call_target="tpu_custom_call" | custom-call | flops 396361728 | bytes 3023232 | tf_op jit(solution)/shard_map/grads/pallas_call | solution.py:21
  (2 shorter events, 0.0 us)
Async XLA Ops:
  3.3 1.9 %collective-permute-start = (bf16[2,96,1152]{2,1,0:T(8,128)(2,1)S(1)}, bf16[2,96,1152]{2,1,0:T(8,128)(2,1)S(1)}, u32[]{:S(2)}, u32[]{:S(2)}) collective-permute-start(bf16[2,96,1152]{2,1,0:T(8,128)(2,1)S(1)} %get-tuple-element.31), channel_id=1, source_target_pairs={{0,1},{1,0},{2,3},{3,2},{4,5},{5,4},{6,7},{7,6},{8,9},{9,8},{10,11... | collective-permute-start | bytes 1327112 | tf_op jit(solution)/shard_map/ppermute | solution.py:267
  4.9 4.0 %copy-start.2 = (s32[192]{0:T(256)S(1)}, s32[192]{0:T(256)}, u32[]{:S(2)}) copy-start(s32[192]{0:T(256)} %param.13) | copy-start | bytes 2308
  5.9 8.7 %collective-permute-start.3 = (bf16[96,1152]{1,0:T(8,128)(2,1)S(1)}, bf16[96,1152]{1,0:T(8,128)(2,1)S(1)}, u32[]{:S(2)}, u32[]{:S(2)}) collective-permute-start(bf16[96,1152]{1,0:T(8,128)(2,1)S(1)} %get-tuple-element.34), channel_id=1, source_target_pairs={{0,16},{16,0},{1,17},{17,1},{2,18},{18,2},{3,19},{19,3},{4,20},{20... | collective-permute-start | bytes 663560 | tf_op jit(solution)/shard_map/ppermute | solution.py:279
  15.3 11.3 %collective-permute-start.9 = (bf16[872,128]{1,0:T(8,128)(2,1)S(1)}, bf16[872,128]{1,0:T(8,128)(2,1)}, u32[]{:S(2)}, u32[]{:S(2)}) collective-permute-start(bf16[872,128]{1,0:T(8,128)(2,1)S(1)} %get-tuple-element.35.refs_0_), channel_id=1, source_target_pairs={{0,4},{2,6},{4,0},{6,2},{8,12},{10,14},{12,8},{14,10},{1,5},{3,7},... | collective-permute-start | bytes 669704 | tf_op jit(solution)/shard_map/ppermute | solution.py:228
  17.2 6.4 %collective-permute-start.1 = (bf16[96,1152]{1,0:T(8,128)(2,1)S(1)}, bf16[96,1152]{1,0:T(8,128)(2,1)S(1)}, u32[]{:S(2)}, u32[]{:S(2)}) collective-permute-start(bf16[96,1152]{1,0:T(8,128)(2,1)S(1)} %get-tuple-element.32), channel_id=1, source_target_pairs={{0,16},{16,0},{1,17},{17,1},{2,18},{18,2},{3,19},{19,3},{4,20},{20... | collective-permute-start | bytes 663560 | tf_op jit(solution)/shard_map/ppermute | solution.py:280
  18.7 12.4 %collective-permute-start.6 = (bf16[872,128]{1,0:T(8,128)(2,1)S(1)}, bf16[872,128]{1,0:T(8,128)(2,1)}, u32[]{:S(2)}, u32[]{:S(2)}) collective-permute-start(bf16[872,128]{1,0:T(8,128)(2,1)S(1)} %get-tuple-element.35.refs_0_), channel_id=1, source_target_pairs={{0,12},{2,14},{4,8},{6,10},{8,4},{10,6},{12,0},{14,2},{1,13},{3,15... | collective-permute-start | bytes 669704 | tf_op jit(solution)/shard_map/ppermute | solution.py:228
  21.1 18.9 %collective-permute-start.4 = (bf16[872,128]{1,0:T(8,128)(2,1)S(1)}, bf16[872,128]{1,0:T(8,128)(2,1)}, u32[]{:S(2)}, u32[]{:S(2)}) collective-permute-start(bf16[872,128]{1,0:T(8,128)(2,1)S(1)} %get-tuple-element.35.refs_0_), channel_id=1, source_target_pairs={{0,8},{2,10},{4,12},{6,14},{8,0},{10,2},{12,4},{14,6},{1,9},{3,11}... | collective-permute-start | bytes 669704 | tf_op jit(solution)/shard_map/ppermute | solution.py:228
  21.3 20.4 %collective-permute-start.8 = (bf16[872,128]{1,0:T(8,128)(2,1)S(1)}, bf16[872,128]{1,0:T(8,128)(2,1)}, u32[]{:S(2)}, u32[]{:S(2)}) collective-permute-start(bf16[872,128]{1,0:T(8,128)(2,1)S(1)} %get-tuple-element.35.refs_0_), channel_id=1, source_target_pairs={{0,1},{1,0},{2,3},{3,2},{4,5},{5,4},{6,7},{7,6},{8,9},{9,8},{10,11... | collective-permute-start | bytes 669704 | tf_op jit(solution)/shard_map/ppermute | solution.py:300
  24.3 0.8 %copy-start = (f32[96,1152]{1,0:T(8,128)}, f32[96,1152]{1,0:T(8,128)S(1)}, u32[]{:S(2)}) copy-start(f32[96,1152]{1,0:T(8,128)S(1)} %get-tuple-element.44.own_unit) | copy-start | bytes 1327108
  25.0 16.6 %collective-permute-start.2 = (bf16[872,128]{1,0:T(8,128)(2,1)S(1)}, bf16[872,128]{1,0:T(8,128)(2,1)S(1)}, u32[]{:S(2)}, u32[]{:S(2)}) collective-permute-start(bf16[872,128]{1,0:T(8,128)(2,1)S(1)} %get-tuple-element.33.own_block), channel_id=1, source_target_pairs={{0,2},{2,0},{4,6},{6,4},{8,10},{10,8},{12,14},{14,12},{1,3},{3,1},... | collective-permute-start | bytes 669704 | tf_op jit(solution)/shard_map/ppermute | solution.py:228
  26.6 15.1 %collective-permute-start.10 = (bf16[872,128]{1,0:T(8,128)(2,1)}, bf16[872,128]{1,0:T(8,128)(2,1)}, u32[]{:S(2)}, u32[]{:S(2)}) collective-permute-start(bf16[872,128]{1,0:T(8,128)(2,1)} %collective-permute-done.9.refs_2_), channel_id=1, source_target_pairs={{0,1},{1,0},{2,3},{3,2},{4,5},{5,4},{6,7},{7,6},{8,9},{9,8},{10,11... | collective-permute-start | bytes 669704 | tf_op jit(solution)/shard_map/ppermute | solution.py:300
  31.0 12.8 %collective-permute-start.7 = (bf16[872,128]{1,0:T(8,128)(2,1)}, bf16[872,128]{1,0:T(8,128)(2,1)}, u32[]{:S(2)}, u32[]{:S(2)}) collective-permute-start(bf16[872,128]{1,0:T(8,128)(2,1)} %collective-permute-done.6.refs_2_), channel_id=1, source_target_pairs={{0,1},{1,0},{2,3},{3,2},{4,5},{5,4},{6,7},{7,6},{8,9},{9,8},{10,11... | collective-permute-start | bytes 669704 | tf_op jit(solution)/shard_map/ppermute | solution.py:300
  40.1 3.8 %collective-permute-start.5 = (bf16[872,128]{1,0:T(8,128)(2,1)}, bf16[872,128]{1,0:T(8,128)(2,1)}, u32[]{:S(2)}, u32[]{:S(2)}) collective-permute-start(bf16[872,128]{1,0:T(8,128)(2,1)} %collective-permute-done.4.refs_0_), channel_id=1, source_target_pairs={{0,1},{1,0},{2,3},{3,2},{4,5},{5,4},{6,7},{7,6},{8,9},{9,8},{10,11... | collective-permute-start | bytes 669704 | tf_op jit(solution)/shard_map/ppermute | solution.py:300
  43.9 16.3 %copy-start.1 = (f32[96,1152]{1,0:T(8,128)S(1)}, f32[96,1152]{1,0:T(8,128)}, u32[]{:S(2)}) copy-start(f32[96,1152]{1,0:T(8,128)} %copy-done) | copy-start | bytes 1327108
  46.3 13.9 %collective-permute-start.11 = (bf16[872,128]{1,0:T(8,128)(2,1)S(1)}, bf16[872,128]{1,0:T(8,128)(2,1)S(1)}, u32[]{:S(2)}, u32[]{:S(2)}) collective-permute-start(bf16[872,128]{1,0:T(8,128)(2,1)S(1)} %get-tuple-element.42), channel_id=1, source_target_pairs={{0,2},{2,0},{4,6},{6,4},{8,10},{10,8},{12,14},{14,12},{1,3},{3,1},... | collective-permute-start | bytes 669704 | tf_op jit(solution)/shard_map/ppermute | solution.py:228
  47.9 12.3 %collective-permute-start.13 = (bf16[872,128]{1,0:T(8,128)(2,1)S(1)}, bf16[872,128]{1,0:T(8,128)(2,1)S(1)}, u32[]{:S(2)}, u32[]{:S(2)}) collective-permute-start(bf16[872,128]{1,0:T(8,128)(2,1)S(1)} %get-tuple-element.42), channel_id=1, source_target_pairs={{0,18},{2,16},{4,22},{6,20},{8,26},{10,24},{12,30},{14,28},{16,2},... | collective-permute-start | bytes 669704 | tf_op jit(solution)/shard_map/ppermute | solution.py:336
  48.3 11.9 %collective-permute-start.12 = (bf16[96,1152]{1,0:T(8,128)(2,1)S(1)}, bf16[96,1152]{1,0:T(8,128)(2,1)S(1)}, u32[]{:S(2)}, u32[]{:S(2)}) collective-permute-start(bf16[96,1152]{1,0:T(8,128)(2,1)S(1)} %get-tuple-element.43), channel_id=1, source_target_pairs={{0,16},{16,0},{1,17},{17,1},{2,18},{18,2},{3,19},{19,3},{4,20},{20... | collective-permute-start | bytes 663560 | tf_op jit(solution)/shard_map/ppermute | solution.py:338
  61.2 1.9 %collective-permute-start.14 = (bf16[2,104,1152]{2,1,0:T(8,128)(2,1)S(1)}, bf16[2,104,1152]{2,1,0:T(8,128)(2,1)S(1)}, u32[]{:S(2)}, u32[]{:S(2)}) collective-permute-start(bf16[2,104,1152]{2,1,0:T(8,128)(2,1)S(1)} %get-tuple-element.49.mine), channel_id=1, source_target_pairs={{0,1},{1,0},{2,3},{3,2},{4,5},{5,4},{6,7},{7,6},{8,9},{9,8},{10,11... | collective-permute-start | bytes 1437704 | tf_op jit(solution)/shard_map/ppermute | solution.py:350

commit v3 on v2

--- a/solution.py
+++ b/solution.py
@@ -15,14 +15,13 @@
 
 
 def local_call(
-    kernel, name, outs, scalars, arrays, scratch=(), flops=0, transcendentals=0, held=(),
+    kernel, name, outs, arrays, scratch=(), flops=0, transcendentals=0, held=(),
 ):
     nbytes = sum(a.size * a.dtype.itemsize for a in (*arrays, *held))
     return pl.pallas_call(
         kernel,
         out_shape=outs,
-        in_specs=[pl.BlockSpec(memory_space=pltpu.SMEM)] * len(scalars)
-        + [pl.BlockSpec(memory_space=pltpu.VMEM)] * len(arrays)
+        in_specs=[pl.BlockSpec(memory_space=pltpu.VMEM)] * len(arrays)
         + [pl.BlockSpec(memory_space=pltpu.HBM)] * len(held),
         out_specs=[pl.BlockSpec(memory_space=pltpu.VMEM)] * len(outs),
         scratch_shapes=list(scratch),
@@ -31,7 +30,7 @@
             flops=flops, bytes_accessed=nbytes, transcendentals=transcendentals
         ),
         name=name,
-    )(*scalars, *arrays, *held)
+    )(*arrays, *held)
 
 
 def cuts(rows):
@@ -39,9 +38,9 @@
     return [(start, size) for start in range(0, rows, size)]
 
 
-def embed_rows(which, place, image_pooled, text_pooled, image_proj, text_proj, out, before):
+def embed_rows(which, image_pooled, text_pooled, image_proj, text_proj, out, before):
     half = out.shape[1]
-    core = place[2]
+    core = lax.axis_index("mp")
     start = pl.multiple_of((core if which == 0 else 1 - core) * half, half)
     rows = pl.ds(start, half)
     for index, (pooled, proj) in enumerate(
@@ -54,7 +53,7 @@
         )
 
 
-def embed_sent_kernel(place, *refs):
+def embed_sent_kernel(*refs):
     sources, sent, held, sems = refs[:4], refs[4], refs[5:9], refs[9]
     before = [[], []]
     count = 0
@@ -66,15 +65,15 @@
             copy.start()
             before[index % 2].append(copy)
             count += 1
-    embed_rows(1, place, *held, sent, before)
-
-
-def embed_kept_kernel(place, *refs):
-    embed_rows(0, place, *refs[:4], refs[4], [[], []])
-
-
-def join_cores_kernel(place, kept, got, own_send, other_send):
-    section = place[0]
+    embed_rows(1, *held, sent, before)
+
+
+def embed_kept_kernel(*refs):
+    embed_rows(0, *refs[:4], refs[4], [[], []])
+
+
+def join_cores_kernel(kept, got, own_send, other_send):
+    section = lax.axis_index("sec")
     own_send[...] = (kept[section] + got[section].astype(F32)).astype(BF16)
     other_send[...] = (kept[1 - section] + got[1 - section].astype(F32)).astype(BF16)
 
@@ -110,20 +109,31 @@
 
 
 def unit_kernel(own):
-    def kernel(place, kept, got, summed, extra, unit, block, norm):
-        section = place[0] if own else 1 - place[0]
+    def kernel(kept, got, summed, ids, unit, block, norm, extra):
+        half = summed.shape[0]
+        core = lax.axis_index("mp")
+        half_ids = jnp.where(core == 0, ids[0:1, :half], ids[0:1, half : 2 * half])
+        extra[...] = jnp.zeros_like(extra)
+        extra[0:1, 0:half] = (half_ids >> 7).astype(F32)
+        extra[1:2, 0:half] = (half_ids & 127).astype(F32)
+        section = lax.axis_index("sec")
+        section = section if own else 1 - section
         emb = kept[section] + got[section].astype(F32) + summed[...].astype(F32)
         row_norm = jnp.sqrt(jnp.sum(emb * emb, axis=1, keepdims=True) + 1e-06)
         value = emb / row_norm
         unit[...] = value
         norm[...] = row_norm
-        write_block(block, value, extra[...].astype(F32))
+        write_block(block, value, extra[...])
 
     return kernel
 
 
+def relay_kernel(block, out):
+    out[...] = block[...]
+
+
 def pair_kernel(blocks, first, last):
-    def kernel(scale_bias, own_block, near_block, own_ids, *refs):
+    def kernel(scale_bias, own_block, near_block, *refs):
         pieces = refs[: 2 * blocks]
         refs = refs[2 * blocks :]
         if not first:
@@ -142,12 +152,17 @@
         for index, piece in enumerate(pieces):
             read_block(piece, visited, index * half, half)
             visit_ids[0:1, pl.ds(index * half, half)] = block_ids(piece)[:, :half]
-        near_ids = jnp.transpose(jnp.broadcast_to(block_ids(near_block), (LANES, LANES)))
-        ids = jnp.concatenate([own_ids[...], near_ids[:half, 0:1]], axis=0)
-        scale = scale_bias[0]
+        ids = jnp.concatenate(
+            [
+                jnp.transpose(jnp.broadcast_to(block_ids(b), (LANES, LANES)))[:half, 0:1]
+                for b in (own_block, near_block)
+            ],
+            axis=0,
+        )
+        scale = scale_bias[0:1, 0:1]
         scores = (
             scale * lax.dot_general(own[...], visited[...], NT, preferred_element_type=F32)
-            + scale_bias[1]
+            + scale_bias[0:1, 1:2]
         )
         sign = jnp.where(ids == visit_ids[0:1, :], 1.0, -1.0).astype(F32)
         value = -sign * scores
@@ -175,10 +190,10 @@
 
 
 def demb_kernel(
-    place, kept, near, across, diagonal, own_unit, own_norm, other_unit, other_norm, loss_own,
+    kept, near, across, diagonal, own_unit, own_norm, other_unit, other_norm, loss_own,
     out, loss_mine, joined, extra,
 ):
-    section = place[0]
+    section = lax.axis_index("sec")
     half, width = own_unit.shape
 
     def finish(grad, unit, norm):
@@ -187,12 +202,12 @@
         return ((grad - value * along) / norm[...]).astype(BF16)
 
     rows = pl.ds(0, half)
-    read_block(diagonal, joined, 0, half)
+    read_block(diagonal, joined.at[0], 0, half)
     out[1 - section, rows, :] = finish(
-        across[...].astype(F32) + joined[...].astype(F32), other_unit, other_norm
+        across[...].astype(F32) + joined[0].astype(F32), other_unit, other_norm
     )
-    read_block(near, joined, 0, half)
-    out[section, rows, :] = finish(kept[...] + joined[...].astype(F32), own_unit, own_norm)
+    read_block(near, joined.at[1], 0, half)
+    out[section, rows, :] = finish(kept[...] + joined[1].astype(F32), own_unit, own_norm)
     parts = extra_rows(near)
     loss = loss_own[...] + (parts[0:1] + parts[1:2] + parts[2:3])[:, :half]
     loss_mine[...] = loss
@@ -202,16 +217,16 @@
 
 
 def grads_kernel(
-    place, mine, theirs, loss_mine, image_proj, text_proj, pair_loss, image_grad, text_grad, joined
+    mine, theirs, loss_mine, image_proj, text_proj, pair_loss, image_grad, text_grad, joined
 ):
-    half = joined.shape[0] // 2
-    core = place[2]
+    half = joined.shape[1] // 2
+    core = lax.axis_index("mp")
     for index, (proj, grad) in enumerate(((image_proj, image_grad), (text_proj, text_grad))):
         for spot, source in ((core, mine), (1 - core, theirs)):
             rows = pl.ds(pl.multiple_of(spot * half, half), half)
-            joined[rows, :] = source[index, pl.ds(0, half), :]
+            joined[index, rows, :] = source[index, pl.ds(0, half), :]
         grad[...] = lax.dot_general(
-            joined[...], proj[...], NT, preferred_element_type=F32
+            joined[index], proj[...], NT, preferred_element_type=F32
         ).astype(BF16)
     parts = theirs[0, pl.ds(half, EXTRA), pl.ds(0, LANES)].astype(F32)
     loss = loss_mine[...]
@@ -230,10 +245,7 @@
     def per_device(
         image_pooled, text_pooled, image_proj, text_proj, log_multiplier, logit_bias, ids
     ):
-        section = lax.axis_index("sec")
-        core = lax.axis_index("mp")
-        place = jnp.stack([section, lax.axis_index("blk"), core]).astype(jnp.int32)
-        scale_bias = jnp.concatenate([jnp.exp(log_multiplier), logit_bias])
+        scale_bias = jnp.concatenate([jnp.exp(log_multiplier), logit_bias])[None, :]
         rows = image_pooled.shape[0]
         half = rows // 2
         width = image_proj.shape[1]
@@ -246,18 +258,13 @@
         towers = (image_pooled, text_pooled, image_proj, text_proj)
         embed_flops = 2 * half * width * (image_proj.shape[0] + text_proj.shape[0])
 
-        half_ids = lax.dynamic_slice_in_dim(ids, core * half, half)
-        digits = jnp.stack([half_ids >> 7, half_ids & 127]).astype(BF16)
-        extra = jnp.pad(digits, ((0, EXTRA - 2), (0, LANES - half)))
-        own_ids = half_ids.astype(F32).reshape(half, 1)
-
+        ids_row = ids[None, :]
         copies = sum(len(cuts(t.shape[0])) for t in towers)
         sent, *towers = local_call(
             embed_sent_kernel,
             "embed_sent",
             [jax.ShapeDtypeStruct((2, half, width), BF16)]
             + [jax.ShapeDtypeStruct(t.shape, t.dtype) for t in towers],
-            [place],
             [],
             scratch=[pltpu.SemaphoreType.DMA((copies,))],
             flops=embed_flops,
@@ -269,12 +276,11 @@
             embed_kept_kernel,
             "embed_kept",
             [jax.ShapeDtypeStruct((2, half, width), F32)],
-            [place],
             towers,
             flops=embed_flops,
         )
         own_send, other_send = local_call(
-            join_cores_kernel, "join_cores", [whole_b16, whole_b16], [place], [kept, got]
+            join_cores_kernel, "join_cores", [whole_b16, whole_b16], [kept, got]
         )
         other_got = lax.ppermute(own_send, "sec", SWAP)
         own_got = lax.ppermute(other_send, "sec", SWAP)
@@ -282,24 +288,26 @@
             unit_kernel(False),
             "other_unit",
             [whole_f32, block_b16, norm_shape],
-            [place],
-            [kept, got, other_got, extra],
+            [kept, got, other_got, ids_row],
+            scratch=[pltpu.VMEM((EXTRA, LANES), F32)],
         )
         own_unit, own_block, own_norm = local_call(
             unit_kernel(True),
             "own_unit",
             [whole_f32, block_b16, norm_shape],
-            [place],
-            [kept, got, own_got, extra],
+            [kept, got, own_got, ids_row],
+            scratch=[pltpu.VMEM((EXTRA, LANES), F32)],
         )
 
         steps = list(range(0, blocks, 2))
         mine = [visit] + [across_blk(visit, k) for k in steps[1:]]
         near_block = across_blk(own_block, 1)
         mine = [visit] + [lax.optimization_barrier((v, own_block))[0] for v in mine[1:]]
+        mine[-1:] = local_call(relay_kernel, "relay", [block_b16], [mine[-1]], flops=10**9)
         theirs = [lax.ppermute(v, "mp", SWAP) for v in mine]
 
-        groups = [list(range(i, min(i + 2, len(steps)))) for i in range(0, len(steps), 2)]
+        early = list(range(len(steps) - 1))
+        groups = [early[i : i + 3] for i in range(0, len(early), 3)] + [[len(steps) - 1]]
         state = []
         for index, group in enumerate(groups):
             first, last = index == 0, index == len(groups) - 1
@@ -316,8 +324,7 @@
                 pair_kernel(len(group), first, last),
                 "pairs",
                 outs,
-                [scale_bias],
-                [own_block, near_block, own_ids, *pieces, *state],
+                [scale_bias, own_block, near_block, *pieces, *state],
                 scratch=[
                     pltpu.VMEM((2 * half, width), BF16),
                     pltpu.VMEM((visited_rows, width), BF16),
@@ -340,12 +347,11 @@
             demb_kernel,
             "demb",
             [jax.ShapeDtypeStruct((2, half + EXTRA, width), BF16), loss_shape],
-            [place],
             [
                 grad_keep, near, across, diagonal,
                 own_unit, own_norm, other_unit, other_norm, loss_own,
             ],
-            scratch=[pltpu.VMEM((half, width), BF16), pltpu.VMEM((EXTRA, LANES), F32)],
+            scratch=[pltpu.VMEM((2, half, width), BF16), pltpu.VMEM((EXTRA, LANES), F32)],
         )
         demb_got = lax.ppermute(demb, "mp", SWAP)
         return local_call(
@@ -356,9 +362,8 @@
                 jax.ShapeDtypeStruct((rows, image_proj.shape[0]), BF16),
                 jax.ShapeDtypeStruct((rows, text_proj.shape[0]), BF16),
             ],
-            [place],
             [demb, demb_got, loss_mine, image_proj, text_proj],
-            scratch=[pltpu.VMEM((rows, width), BF16)],
+            scratch=[pltpu.VMEM((2, rows, width), BF16)],
             flops=2 * embed_flops,
         )
 

time: 65.3 us -> 56.6 us (0.87)
  the two profiles are of different devices: /device:TPU:0 before, /device:TPU:19 now
where the time goes in v3:
time: 56.6 us; the launch traced here: 56.4 us
  waiting for transfers between devices  29.7 us (52%)
  starting transfers between devices  17.1 us (30%)
  Pallas kernels  7.42 us (13%)
  between operations  2.06 us (4%)
    ppermute x1, waiting for transfers between devices, per_device(): across = lax.ppermute(grad_own, 'sec', SWAP)  10.1 us
    ppermute x5, waiting for transfers between devices, across_blk(): return lax.ppermute(value, 'blk', [(i, i ^ step) for i in range(blocks)])  8.37 us
    ppermute x4, starting transfers between devices, per_device(): theirs = [lax.ppermute(v, 'mp', SWAP) for v in mine]  7.91 us
    pallas_call x10, Pallas kernels, local_call(): pl.pallas_call(kernel, out_shape=outs, in_specs=[pl.BlockSpec(memory_spac...  7.42 us
    ppermute x1, waiting for transfers between devices, per_device(): other_got = lax.ppermute(own_send, 'sec', SWAP)  6.39 us
    ppermute x5, starting transfers between devices, across_blk(): return lax.ppermute(value, 'blk', [(i, i ^ step) for i in range(blocks)])  5.33 us
    ppermute x1, waiting for transfers between devices, per_device(): own_got = lax.ppermute(other_send, 'sec', SWAP)  2.5 us
    ppermute x1, waiting for transfers between devices, per_device(): demb_got = lax.ppermute(demb, 'mp', SWAP)  1.47 us
  transfers between devices with their start and end apart: 15, of which 6 were waited for; matrix products, arithmetic and copies ran while one was open for 0% of the time, Pallas kernels for 4%

profile of v3, /device:TPU:19, one launch (start us, length us, event | category | flops | bytes accessed | tf_op | source)
XLA Modules:
  0.0 56.4 jit_solution(8462913999915115798)
XLA Ops:
  0.6 2.1 %embed_sent.1 = (bf16[2,96,1152]{2,1,0:T(8,128)(2,1)S(1)}, bf16[192,384]{1,0:T(8,128)(2,1)S(1)}, bf16[192,512]{1,0:T(8,128)(2,1)S(1)}, bf16[384,1152]{1,0:T(8,128)(2,1)S(1)}, bf16[512,1152]{1,0:T(8,128)(2,1)S(1)}) custom-call(bf16[192,384]{1,0:T(8,128)(2,1)} %refs_0_.1, bf16[192,512]{1,0:T(8,128)(2,1)} %refs_1_.1, bf16[384,1152]{1,0:T(8,128)(2,1)} %refs_2_.1, ...), custom_call_target="tpu_custom_call" | custom-call | flops 198180864 | bytes 2408448 | tf_op jit(solution)/shard_map/embed_sent/pallas_call | solution.py:21
  2.7 0.7 %collective-permute-start = (bf16[2,96,1152]{2,1,0:T(8,128)(2,1)S(1)}, bf16[2,96,1152]{2,1,0:T(8,128)(2,1)S(1)}, u32[]{:S(2)}, u32[]{:S(2)}) collective-permute-start(bf16[2,96,1152]{2,1,0:T(8,128)(2,1)S(1)} %get-tuple-element.31), channel_id=1, source_target_pairs={{0,1},{1,0},{2,3},{3,2},{4,5},{5,4},{6,7},{7,6},{8,9},{9,8},{10,11... | collective-permute-start | bytes 1327112 | tf_op jit(solution)/shard_map/ppermute | solution.py:274
  3.4 0.5 embed_kept.1.kept
  3.9 0.0 copy-start
  3.9 0.9 %collective-permute-done.got = bf16[2,96,1152]{2,1,0:T(8,128)(2,1)S(1)} collective-permute-done((bf16[2,96,1152]{2,1,0:T(8,128)(2,1)S(1)}, bf16[2,96,1152]{2,1,0:T(8,128)(2,1)S(1)}, u32[]{:S(2)}, u32[]{:S(2)}) %collective-permute-start) | collective-permute-done | bytes 442400 | tf_op jit(solution)/shard_map/ppermute | solution.py:274
  4.9 0.1 join_cores.1
  4.9 0.3 collective-permute-start.3
  5.3 6.4 %collective-permute-done.3.summed = bf16[96,1152]{1,0:T(8,128)(2,1)S(1)} collective-permute-done((bf16[96,1152]{1,0:T(8,128)(2,1)S(1)}, bf16[96,1152]{1,0:T(8,128)(2,1)S(1)}, u32[]{:S(2)}, u32[]{:S(2)}) %collective-permute-start.3) | collective-permute-done | bytes 221216 | tf_op jit(solution)/shard_map/ppermute | solution.py:285
  11.7 0.0 copy-done
  11.7 0.2 other_unit.1
  11.9 0.1 collective-permute-start.9
  12.0 1.3 %collective-permute-start.7 = (bf16[872,128]{1,0:T(8,128)(2,1)S(1)}, bf16[872,128]{1,0:T(8,128)(2,1)S(1)}, u32[]{:S(2)}, u32[]{:S(2)}) collective-permute-start(bf16[872,128]{1,0:T(8,128)(2,1)S(1)} %get-tuple-element.35.refs_0_), channel_id=1, source_target_pairs={{0,4},{2,6},{4,0},{6,2},{8,12},{10,14},{12,8},{14,10},{1,5},{3,7},... | collective-permute-start | bytes 669704 | tf_op jit(solution)/shard_map/ppermute | solution.py:243
  13.3 1.3 %collective-permute-start.4 = (bf16[872,128]{1,0:T(8,128)(2,1)S(1)}, bf16[872,128]{1,0:T(8,128)(2,1)S(1)}, u32[]{:S(2)}, u32[]{:S(2)}) collective-permute-start(bf16[872,128]{1,0:T(8,128)(2,1)S(1)} %get-tuple-element.35.refs_0_), channel_id=1, source_target_pairs={{0,12},{2,14},{4,8},{6,10},{8,4},{10,6},{12,0},{14,2},{1,13},{3,15... | collective-permute-start | bytes 669704 | tf_op jit(solution)/shard_map/ppermute | solution.py:243
  14.6 0.3 collective-permute-start.1
  14.8 2.3 %collective-permute-start.6 = (bf16[872,128]{1,0:T(8,128)(2,1)S(1)}, bf16[872,128]{1,0:T(8,128)(2,1)S(1)}, u32[]{:S(2)}, u32[]{:S(2)}) collective-permute-start(bf16[872,128]{1,0:T(8,128)(2,1)S(1)} %get-tuple-element.35.refs_0_), channel_id=1, source_target_pairs={{0,1},{1,0},{2,3},{3,2},{4,5},{5,4},{6,7},{7,6},{8,9},{9,8},{10,11... | collective-permute-start | bytes 669704 | tf_op jit(solution)/shard_map/ppermute | solution.py:307
  17.2 2.5 %collective-permute-done.1.summed = bf16[96,1152]{1,0:T(8,128)(2,1)S(1)} collective-permute-done((bf16[96,1152]{1,0:T(8,128)(2,1)S(1)}, bf16[96,1152]{1,0:T(8,128)(2,1)S(1)}, u32[]{:S(2)}, u32[]{:S(2)}) %collective-permute-start.1) | collective-permute-done | bytes 221216 | tf_op jit(solution)/shard_map/ppermute | solution.py:286
  19.7 0.2 own_unit.1
  19.9 1.3 %collective-permute-start.2 = (bf16[872,128]{1,0:T(8,128)(2,1)S(1)}, bf16[872,128]{1,0:T(8,128)(2,1)S(1)}, u32[]{:S(2)}, u32[]{:S(2)}) collective-permute-start(bf16[872,128]{1,0:T(8,128)(2,1)S(1)} %get-tuple-element.33.own_block), channel_id=1, source_target_pairs={{0,2},{2,0},{4,6},{6,4},{8,10},{10,8},{12,14},{14,12},{1,3},{3,1},... | collective-permute-start | bytes 669704 | tf_op jit(solution)/shard_map/ppermute | solution.py:243
  21.2 0.0 collective-permute-done.9.refs_4_
  21.2 3.8 %collective-permute-start.10 = (bf16[872,128]{1,0:T(8,128)(2,1)S(1)}, bf16[872,128]{1,0:T(8,128)(2,1)S(1)}, u32[]{:S(2)}, u32[]{:S(2)}) collective-permute-start(bf16[872,128]{1,0:T(8,128)(2,1)S(1)} %collective-permute-done.9.refs_4_), channel_id=1, source_target_pairs={{0,1},{1,0},{2,3},{3,2},{4,5},{5,4},{6,7},{7,6},{8,9},{9,8},{10,11... | collective-permute-start | bytes 669704 | tf_op jit(solution)/shard_map/ppermute | solution.py:307
  24.9 0.0 collective-permute-done.7.refs_2_
  24.9 1.3 %collective-permute-start.8 = (bf16[872,128]{1,0:T(8,128)(2,1)S(1)}, bf16[872,128]{1,0:T(8,128)(2,1)S(1)}, u32[]{:S(2)}, u32[]{:S(2)}) collective-permute-start(bf16[872,128]{1,0:T(8,128)(2,1)S(1)} %collective-permute-done.7.refs_2_), channel_id=1, source_target_pairs={{0,1},{1,0},{2,3},{3,2},{4,5},{5,4},{6,7},{7,6},{8,9},{9,8},{10,11... | collective-permute-start | bytes 669704 | tf_op jit(solution)/shard_map/ppermute | solution.py:307
  26.2 8.4 %collective-permute-done.4.block = bf16[872,128]{1,0:T(8,128)(2,1)S(1)} collective-permute-done((bf16[872,128]{1,0:T(8,128)(2,1)S(1)}, bf16[872,128]{1,0:T(8,128)(2,1)S(1)}, u32[]{:S(2)}, u32[]{:S(2)}) %collective-permute-start.4) | collective-permute-done | bytes 223264 | tf_op jit(solution)/shard_map/ppermute | solution.py:243
  34.6 0.6 collective-permute-start.5
  36.5 0.1 maximum_bitcast_fusion.scale_bias
  36.6 0.0 collective-permute-done.2.near_block
  36.6 0.0 collective-permute-done.6.refs_1_
  36.6 0.0 collective-permute-done.10.refs_5_
  36.6 0.0 collective-permute-done.8.refs_3_
  36.6 1.5 %pairs.2 = (f32[192,1152]{1,0:T(8,128)S(1)}, f32[192,1]{1,0:T(8,128)S(1)}) custom-call(f32[1,2]{1,0:T(1,128)S(1)} %maximum_bitcast_fusion.scale_bias, bf16[872,128]{1,0:T(8,128)(2,1)S(1)} %get-tuple-element.33.own_block, bf16[872,128]{1,0:T(8,128)(2,1)S(1)} %collective-permute-done.2.near_block, bf16[872,128]{1,0:T(8,128)(2,1)S(1)} %get-tuple-element.35.refs_0_, ...), custom_call_target="tpu_custom_call" | custom-call | flops 509607936 | bytes 1785864 | tf_op jit(solution)/shard_map/pairs/pallas_call | solution.py:21
  38.1 0.0 collective-permute-done.5.refs_1_
  38.1 0.9 %pairs.3 = (f32[96,1152]{1,0:T(8,128)S(1)}, bf16[96,1152]{1,0:T(8,128)(2,1)S(1)}, bf16[872,128]{1,0:T(8,128)(2,1)S(1)}, f32[1,96]{1,0:T(1,128)S(1)}) custom-call(f32[1,2]{1,0:T(1,128)S(1)} %maximum_bitcast_fusion.scale_bias, bf16[872,128]{1,0:T(8,128)(2,1)S(1)} %get-tuple-element.33.own_block, bf16[872,128]{1,0:T(8,128)(2,1)S(1)} %collective-permute-done.2.near_block, ...), custom_call_target="tpu_custom_call" | custom-call | flops 169869312 | bytes 1778440 | tf_op jit(solution)/shard_map/pairs/pallas_call | solution.py:21
  39.0 1.3 %collective-permute-start.11 = (bf16[872,128]{1,0:T(8,128)(2,1)S(1)}, bf16[872,128]{1,0:T(8,128)(2,1)S(1)}, u32[]{:S(2)}, u32[]{:S(2)}) collective-permute-start(bf16[872,128]{1,0:T(8,128)(2,1)S(1)} %get-tuple-element.42), channel_id=1, source_target_pairs={{0,2},{2,0},{4,6},{6,4},{8,10},{10,8},{12,14},{14,12},{1,3},{3,1},... | collective-permute-start | bytes 669704 | tf_op jit(solution)/shard_map/ppermute | solution.py:243
  40.3 0.2 collective-permute-start.13
  40.5 1.2 %collective-permute-start.12 = (bf16[96,1152]{1,0:T(8,128)(2,1)S(1)}, bf16[96,1152]{1,0:T(8,128)(2,1)S(1)}, u32[]{:S(2)}, u32[]{:S(2)}) collective-permute-start(bf16[96,1152]{1,0:T(8,128)(2,1)S(1)} %get-tuple-element.43), channel_id=1, source_target_pairs={{0,16},{16,0},{1,17},{17,1},{2,18},{18,2},{3,19},{19,3},{4,20},{20... | collective-permute-start | bytes 663560 | tf_op jit(solution)/shard_map/ppermute | solution.py:345
  41.7 10.1 %collective-permute-done.12.across = bf16[96,1152]{1,0:T(8,128)(2,1)S(1)} collective-permute-done((bf16[96,1152]{1,0:T(8,128)(2,1)S(1)}, bf16[96,1152]{1,0:T(8,128)(2,1)S(1)}, u32[]{:S(2)}, u32[]{:S(2)}) %collective-permute-start.12) | collective-permute-done | bytes 221216 | tf_op jit(solution)/shard_map/ppermute | solution.py:345
  51.8 0.0 collective-permute-done.11.near
  51.8 0.0 collective-permute-done.13.diagonal
  51.8 0.4 demb.1
  52.2 1.2 %collective-permute-start.14 = (bf16[2,104,1152]{2,1,0:T(8,128)(2,1)S(1)}, bf16[2,104,1152]{2,1,0:T(8,128)(2,1)S(1)}, u32[]{:S(2)}, u32[]{:S(2)}) collective-permute-start(bf16[2,104,1152]{2,1,0:T(8,128)(2,1)S(1)} %get-tuple-element.49.mine), channel_id=1, source_target_pairs={{0,1},{1,0},{2,3},{3,2},{4,5},{5,4},{6,7},{7,6},{8,9},{9,8},{10,11... | collective-permute-start | bytes 1437704 | tf_op jit(solution)/shard_map/ppermute | solution.py:356
  53.4 1.5 %collective-permute-done.14.theirs = bf16[2,104,1152]{2,1,0:T(8,128)(2,1)S(1)} collective-permute-done((bf16[2,104,1152]{2,1,0:T(8,128)(2,1)S(1)}, bf16[2,104,1152]{2,1,0:T(8,128)(2,1)S(1)}, u32[]{:S(2)}, u32[]{:S(2)}) %collective-permute-start.14) | collective-permute-done | bytes 479264 | tf_op jit(solution)/shard_map/ppermute | solution.py:356
  54.9 1.6 %grads.1 = (f32[1,192]{1,0:T(1,128)}, bf16[192,384]{1,0:T(8,128)(2,1)}, bf16[192,512]{1,0:T(8,128)(2,1)}) custom-call(bf16[2,104,1152]{2,1,0:T(8,128)(2,1)S(1)} %get-tuple-element.49.mine, bf16[2,104,1152]{2,1,0:T(8,128)(2,1)S(1)} %collective-permute-done.14.theirs, f32[1,96]{1,0:T(1,128)S(1)} %get-tuple-element.50.loss_mine, ...), custom_call_target="tpu_custom_call" | custom-call | flops 396361728 | bytes 3023232 | tf_op jit(solution)/shard_map/grads/pallas_call | solution.py:21
  (1 shorter events, 0.0 us)
Async XLA Ops:
  2.7 2.2 %collective-permute-start = (bf16[2,96,1152]{2,1,0:T(8,128)(2,1)S(1)}, bf16[2,96,1152]{2,1,0:T(8,128)(2,1)S(1)}, u32[]{:S(2)}, u32[]{:S(2)}) collective-permute-start(bf16[2,96,1152]{2,1,0:T(8,128)(2,1)S(1)} %get-tuple-element.31), channel_id=1, source_target_pairs={{0,1},{1,0},{2,3},{3,2},{4,5},{5,4},{6,7},{7,6},{8,9},{9,8},{10,11... | collective-permute-start | bytes 1327112 | tf_op jit(solution)/shard_map/ppermute | solution.py:274
  3.9 7.7 %copy-start = (s32[192]{0:T(256)S(1)}, s32[192]{0:T(256)}, u32[]{:S(2)}) copy-start(s32[192]{0:T(256)} %param.13) | copy-start | bytes 2308
  4.9 6.7 %collective-permute-start.3 = (bf16[96,1152]{1,0:T(8,128)(2,1)S(1)}, bf16[96,1152]{1,0:T(8,128)(2,1)S(1)}, u32[]{:S(2)}, u32[]{:S(2)}) collective-permute-start(bf16[96,1152]{1,0:T(8,128)(2,1)S(1)} %get-tuple-element.34), channel_id=1, source_target_pairs={{0,16},{16,0},{1,17},{17,1},{2,18},{18,2},{3,19},{19,3},{4,20},{20... | collective-permute-start | bytes 663560 | tf_op jit(solution)/shard_map/ppermute | solution.py:285
  11.9 9.3 %collective-permute-start.9 = (bf16[872,128]{1,0:T(8,128)(2,1)S(1)}, bf16[872,128]{1,0:T(8,128)(2,1)S(1)}, u32[]{:S(2)}, u32[]{:S(2)}) collective-permute-start(bf16[872,128]{1,0:T(8,128)(2,1)S(1)} %get-tuple-element.35.refs_0_), channel_id=1, source_target_pairs={{0,8},{2,10},{4,12},{6,14},{8,0},{10,2},{12,4},{14,6},{1,9},{3,11}... | collective-permute-start | bytes 669704 | tf_op jit(solution)/shard_map/ppermute | solution.py:243
  12.0 13.0 %collective-permute-start.7 = (bf16[872,128]{1,0:T(8,128)(2,1)S(1)}, bf16[872,128]{1,0:T(8,128)(2,1)S(1)}, u32[]{:S(2)}, u32[]{:S(2)}) collective-permute-start(bf16[872,128]{1,0:T(8,128)(2,1)S(1)} %get-tuple-element.35.refs_0_), channel_id=1, source_target_pairs={{0,4},{2,6},{4,0},{6,2},{8,12},{10,14},{12,8},{14,10},{1,5},{3,7},... | collective-permute-start | bytes 669704 | tf_op jit(solution)/shard_map/ppermute | solution.py:243
  13.3 21.3 %collective-permute-start.4 = (bf16[872,128]{1,0:T(8,128)(2,1)S(1)}, bf16[872,128]{1,0:T(8,128)(2,1)S(1)}, u32[]{:S(2)}, u32[]{:S(2)}) collective-permute-start(bf16[872,128]{1,0:T(8,128)(2,1)S(1)} %get-tuple-element.35.refs_0_), channel_id=1, source_target_pairs={{0,12},{2,14},{4,8},{6,10},{8,4},{10,6},{12,0},{14,2},{1,13},{3,15... | collective-permute-start | bytes 669704 | tf_op jit(solution)/shard_map/ppermute | solution.py:243
  14.6 5.1 %collective-permute-start.1 = (bf16[96,1152]{1,0:T(8,128)(2,1)S(1)}, bf16[96,1152]{1,0:T(8,128)(2,1)S(1)}, u32[]{:S(2)}, u32[]{:S(2)}) collective-permute-start(bf16[96,1152]{1,0:T(8,128)(2,1)S(1)} %get-tuple-element.32), channel_id=1, source_target_pairs={{0,16},{16,0},{1,17},{17,1},{2,18},{18,2},{3,19},{19,3},{4,20},{20... | collective-permute-start | bytes 663560 | tf_op jit(solution)/shard_map/ppermute | solution.py:286
  14.8 21.7 %collective-permute-start.6 = (bf16[872,128]{1,0:T(8,128)(2,1)S(1)}, bf16[872,128]{1,0:T(8,128)(2,1)S(1)}, u32[]{:S(2)}, u32[]{:S(2)}) collective-permute-start(bf16[872,128]{1,0:T(8,128)(2,1)S(1)} %get-tuple-element.35.refs_0_), channel_id=1, source_target_pairs={{0,1},{1,0},{2,3},{3,2},{4,5},{5,4},{6,7},{7,6},{8,9},{9,8},{10,11... | collective-permute-start | bytes 669704 | tf_op jit(solution)/shard_map/ppermute | solution.py:307
  19.9 16.7 %collective-permute-start.2 = (bf16[872,128]{1,0:T(8,128)(2,1)S(1)}, bf16[872,128]{1,0:T(8,128)(2,1)S(1)}, u32[]{:S(2)}, u32[]{:S(2)}) collective-permute-start(bf16[872,128]{1,0:T(8,128)(2,1)S(1)} %get-tuple-element.33.own_block), channel_id=1, source_target_pairs={{0,2},{2,0},{4,6},{6,4},{8,10},{10,8},{12,14},{14,12},{1,3},{3,1},... | collective-permute-start | bytes 669704 | tf_op jit(solution)/shard_map/ppermute | solution.py:243
  21.2 15.4 %collective-permute-start.10 = (bf16[872,128]{1,0:T(8,128)(2,1)S(1)}, bf16[872,128]{1,0:T(8,128)(2,1)S(1)}, u32[]{:S(2)}, u32[]{:S(2)}) collective-permute-start(bf16[872,128]{1,0:T(8,128)(2,1)S(1)} %collective-permute-done.9.refs_4_), channel_id=1, source_target_pairs={{0,1},{1,0},{2,3},{3,2},{4,5},{5,4},{6,7},{7,6},{8,9},{9,8},{10,11... | collective-permute-start | bytes 669704 | tf_op jit(solution)/shard_map/ppermute | solution.py:307
  24.9 11.7 %collective-permute-start.8 = (bf16[872,128]{1,0:T(8,128)(2,1)S(1)}, bf16[872,128]{1,0:T(8,128)(2,1)S(1)}, u32[]{:S(2)}, u32[]{:S(2)}) collective-permute-start(bf16[872,128]{1,0:T(8,128)(2,1)S(1)} %collective-permute-done.7.refs_2_), channel_id=1, source_target_pairs={{0,1},{1,0},{2,3},{3,2},{4,5},{5,4},{6,7},{7,6},{8,9},{9,8},{10,11... | collective-permute-start | bytes 669704 | tf_op jit(solution)/shard_map/ppermute | solution.py:307
  34.6 3.5 %collective-permute-start.5 = (bf16[872,128]{1,0:T(8,128)(2,1)S(1)}, bf16[872,128]{1,0:T(8,128)(2,1)S(1)}, u32[]{:S(2)}, u32[]{:S(2)}) collective-permute-start(bf16[872,128]{1,0:T(8,128)(2,1)S(1)} %relay.1.refs_0_), channel_id=1, source_target_pairs={{0,1},{1,0},{2,3},{3,2},{4,5},{5,4},{6,7},{7,6},{8,9},{9,8},{10,11... | collective-permute-start | bytes 669704 | tf_op jit(solution)/shard_map/ppermute | solution.py:307
  39.0 12.8 %collective-permute-start.11 = (bf16[872,128]{1,0:T(8,128)(2,1)S(1)}, bf16[872,128]{1,0:T(8,128)(2,1)S(1)}, u32[]{:S(2)}, u32[]{:S(2)}) collective-permute-start(bf16[872,128]{1,0:T(8,128)(2,1)S(1)} %get-tuple-element.42), channel_id=1, source_target_pairs={{0,2},{2,0},{4,6},{6,4},{8,10},{10,8},{12,14},{14,12},{1,3},{3,1},... | collective-permute-start | bytes 669704 | tf_op jit(solution)/shard_map/ppermute | solution.py:243
  40.3 11.5 %collective-permute-start.13 = (bf16[872,128]{1,0:T(8,128)(2,1)S(1)}, bf16[872,128]{1,0:T(8,128)(2,1)S(1)}, u32[]{:S(2)}, u32[]{:S(2)}) collective-permute-start(bf16[872,128]{1,0:T(8,128)(2,1)S(1)} %get-tuple-element.42), channel_id=1, source_target_pairs={{0,18},{2,16},{4,22},{6,20},{8,26},{10,24},{12,30},{14,28},{16,2},... | collective-permute-start | bytes 669704 | tf_op jit(solution)/shard_map/ppermute | solution.py:343
  40.5 11.3 %collective-permute-start.12 = (bf16[96,1152]{1,0:T(8,128)(2,1)S(1)}, bf16[96,1152]{1,0:T(8,128)(2,1)S(1)}, u32[]{:S(2)}, u32[]{:S(2)}) collective-permute-start(bf16[96,1152]{1,0:T(8,128)(2,1)S(1)} %get-tuple-element.43), channel_id=1, source_target_pairs={{0,16},{16,0},{1,17},{17,1},{2,18},{18,2},{3,19},{19,3},{4,20},{20... | collective-permute-start | bytes 663560 | tf_op jit(solution)/shard_map/ppermute | solution.py:345
  52.2 2.7 %collective-permute-start.14 = (bf16[2,104,1152]{2,1,0:T(8,128)(2,1)S(1)}, bf16[2,104,1152]{2,1,0:T(8,128)(2,1)S(1)}, u32[]{:S(2)}, u32[]{:S(2)}) collective-permute-start(bf16[2,104,1152]{2,1,0:T(8,128)(2,1)S(1)} %get-tuple-element.49.mine), channel_id=1, source_target_pairs={{0,1},{1,0},{2,3},{3,2},{4,5},{5,4},{6,7},{7,6},{8,9},{9,8},{10,11... | collective-permute-start | bytes 1437704 | tf_op jit(solution)/shard_map/ppermute | solution.py:356

commit v4 on v3

--- a/solution.py
+++ b/solution.py
@@ -109,7 +109,13 @@
 
 
 def unit_kernel(own):
-    def kernel(kept, got, summed, ids, unit, block, norm, extra):
+    def kernel(kept, got, summed, ids, *refs):
+        if own:
+            multiplier, bias, unit, block, norm, params, extra = refs
+            params[0:1, :] = jnp.broadcast_to(jnp.exp(multiplier[...]), (1, LANES))
+            params[1:2, :] = jnp.broadcast_to(bias[...], (1, LANES))
+        else:
+            unit, block, norm, extra = refs
         half = summed.shape[0]
         core = lax.axis_index("mp")
         half_ids = jnp.where(core == 0, ids[0:1, :half], ids[0:1, half : 2 * half])
@@ -132,37 +138,27 @@
     out[...] = block[...]
 
 
-def pair_kernel(blocks, first, last):
-    def kernel(scale_bias, own_block, near_block, *refs):
-        pieces = refs[: 2 * blocks]
-        refs = refs[2 * blocks :]
+def pair_kernel(blocks, sides, first, last):
+    def kernel(params, *refs):
+        sources, refs = refs[: len(sides)], refs[len(sides) :]
+        pieces, refs = refs[: 2 * blocks], refs[2 * blocks :]
         if not first:
-            grad_in, loss_in = refs[:2]
-            refs = refs[2:]
-        if last:
-            grad_keep, grad_own, grad_near, loss_own = refs[:4]
-            refs = refs[4:]
-        else:
-            grad_out, loss_out = refs[:2]
-            refs = refs[2:]
-        own, visited, visit_ids, extra = refs
-        half = own.shape[0] // 2
-        read_block(own_block, own, 0, half)
-        read_block(near_block, own, half, half)
+            (grad_in, loss_in), refs = refs[:2], refs[2:]
+        outs, (own, visited, visit_ids, extra) = refs[:-4], refs[-4:]
+        half = own.shape[0] // len(sides)
+        columns = []
+        for index, source in enumerate(sources):
+            read_block(source, own, index * half, half)
+            square = jnp.broadcast_to(block_ids(source), (LANES, LANES))
+            columns.append(jnp.transpose(square)[:half, 0:1])
+        ids = jnp.concatenate(columns, axis=0) if len(sides) > 1 else columns[0]
         for index, piece in enumerate(pieces):
             read_block(piece, visited, index * half, half)
             visit_ids[0:1, pl.ds(index * half, half)] = block_ids(piece)[:, :half]
-        ids = jnp.concatenate(
-            [
-                jnp.transpose(jnp.broadcast_to(block_ids(b), (LANES, LANES)))[:half, 0:1]
-                for b in (own_block, near_block)
-            ],
-            axis=0,
-        )
-        scale = scale_bias[0:1, 0:1]
+        scale = params[0:1, 0:1]
         scores = (
             scale * lax.dot_general(own[...], visited[...], NT, preferred_element_type=F32)
-            + scale_bias[0:1, 1:2]
+            + params[1:2, 0:1]
         )
         sign = jnp.where(ids == visit_ids[0:1, :], 1.0, -1.0).astype(F32)
         value = -sign * scores
@@ -173,62 +169,75 @@
         grad = jnp.dot(weight, visited[...], preferred_element_type=F32)
         loss = jnp.sum(losses, axis=1, keepdims=True)
         if not first:
-            grad = grad + grad_in[...]
-            loss = loss + loss_in[...]
-        if last:
-            grad_keep[...] = grad[:half]
-            grad_own[...] = grad[:half].astype(BF16)
-            wide = jnp.broadcast_to(loss, (2 * half, LANES))
-            loss_own[...] = jnp.transpose(wide[:half])[0:1]
-            split_rows(jnp.transpose(wide[half:])[0:1], extra)
-            write_block(grad_near, grad[half:], extra[...])
+            rows = pl.ds(half * sides[0], half * len(sides))
+            grad = grad + grad_in[rows, :]
+            loss = loss + loss_in[rows, :]
+        if not last:
+            outs[0][...] = grad
+            outs[1][...] = loss
+            return
+        loss_row = jnp.transpose(jnp.broadcast_to(loss, (half, LANES)))[0:1]
+        if sides[0] == 0:
+            grad_keep, grad_own, loss_own = outs
+            grad_keep[...] = grad
+            grad_own[...] = grad.astype(BF16)
+            loss_own[...] = loss_row
         else:
-            grad_out[...] = grad
-            loss_out[...] = loss
+            split_rows(loss_row, extra)
+            write_block(outs[0], grad, extra[...])
 
     return kernel
 
 
-def demb_kernel(
-    kept, near, across, diagonal, own_unit, own_norm, other_unit, other_norm, loss_own,
-    out, loss_mine, joined, extra,
-):
-    section = lax.axis_index("sec")
-    half, width = own_unit.shape
-
-    def finish(grad, unit, norm):
-        value = unit[...]
-        along = jnp.sum(value * grad, axis=1, keepdims=True)
-        return ((grad - value * along) / norm[...]).astype(BF16)
-
-    rows = pl.ds(0, half)
-    read_block(diagonal, joined.at[0], 0, half)
-    out[1 - section, rows, :] = finish(
-        across[...].astype(F32) + joined[0].astype(F32), other_unit, other_norm
-    )
-    read_block(near, joined.at[1], 0, half)
-    out[section, rows, :] = finish(kept[...] + joined[1].astype(F32), own_unit, own_norm)
+def finish(grad, unit, norm):
+    value = unit[...]
+    along = jnp.sum(value * grad, axis=1, keepdims=True)
+    return ((grad - value * along) / norm[...]).astype(BF16)
+
+
+def own_demb_kernel(kept, near, unit, norm, loss_own, out, loss_mine, joined, extra):
+    half, width = unit.shape
+    read_block(near, joined, 0, half)
+    out[pl.ds(0, half), :] = finish(kept[...] + joined[...].astype(F32), unit, norm)
     parts = extra_rows(near)
     loss = loss_own[...] + (parts[0:1] + parts[1:2] + parts[2:3])[:, :half]
     loss_mine[...] = loss
     split_rows(loss, extra)
-    out[:, pl.ds(half, EXTRA), :] = jnp.zeros((2, EXTRA, width), BF16)
-    out[0, pl.ds(half, EXTRA), pl.ds(0, LANES)] = extra[...].astype(BF16)
+    out[pl.ds(half, EXTRA), :] = jnp.zeros((EXTRA, width), BF16)
+    out[pl.ds(half, EXTRA), pl.ds(0, LANES)] = extra[...].astype(BF16)
+
+
+def other_demb_kernel(across, diagonal, unit, norm, out, joined):
+    read_block(diagonal, joined, 0, unit.shape[0])
+    out[...] = finish(across[...].astype(F32) + joined[...].astype(F32), unit, norm)
 
 
 def grads_kernel(
-    mine, theirs, loss_mine, image_proj, text_proj, pair_loss, image_grad, text_grad, joined
+    own, own_got, other, other_got, loss_mine, image_proj, text_proj,
+    pair_loss, image_grad, text_grad, joined,
 ):
     half = joined.shape[1] // 2
     core = lax.axis_index("mp")
-    for index, (proj, grad) in enumerate(((image_proj, image_grad), (text_proj, text_grad))):
-        for spot, source in ((core, mine), (1 - core, theirs)):
-            rows = pl.ds(pl.multiple_of(spot * half, half), half)
-            joined[index, rows, :] = source[index, pl.ds(0, half), :]
+
+    def tower(index, mine, theirs, proj, grad):
+        mine, theirs = mine[pl.ds(0, half), :], theirs[pl.ds(0, half), :]
+        joined[index, pl.ds(0, half), :] = jnp.where(core == 0, mine, theirs)
+        joined[index, pl.ds(half, half), :] = jnp.where(core == 0, theirs, mine)
         grad[...] = lax.dot_general(
             joined[index], proj[...], NT, preferred_element_type=F32
         ).astype(BF16)
-    parts = theirs[0, pl.ds(half, EXTRA), pl.ds(0, LANES)].astype(F32)
+
+    @pl.when(lax.axis_index("sec") == 0)
+    def _():
+        tower(0, own, own_got, image_proj, image_grad)
+        tower(1, other, other_got, text_proj, text_grad)
+
+    @pl.when(lax.axis_index("sec") != 0)
+    def _():
+        tower(1, own, own_got, text_proj, text_grad)
+        tower(0, other, other_got, image_proj, image_grad)
+
+    parts = own_got[pl.ds(half, EXTRA), pl.ds(0, LANES)].astype(F32)
     loss = loss_mine[...]
     loss_theirs = (parts[0:1] + parts[1:2] + parts[2:3])[:, :half]
     pair_loss[0:1, 0:half] = jnp.where(core == 0, loss, loss_theirs)
@@ -245,7 +254,7 @@
     def per_device(
         image_pooled, text_pooled, image_proj, text_proj, log_multiplier, logit_bias, ids
     ):
-        scale_bias = jnp.concatenate([jnp.exp(log_multiplier), logit_bias])[None, :]
+        multiplier, bias = log_multiplier[None, :], logit_bias[None, :]
         rows = image_pooled.shape[0]
         half = rows // 2
         width = image_proj.shape[1]
@@ -291,11 +300,11 @@
             [kept, got, other_got, ids_row],
             scratch=[pltpu.VMEM((EXTRA, LANES), F32)],
         )
-        own_unit, own_block, own_norm = local_call(
+        own_unit, own_block, own_norm, params = local_call(
             unit_kernel(True),
             "own_unit",
-            [whole_f32, block_b16, norm_shape],
-            [kept, got, own_got, ids_row],
+            [whole_f32, block_b16, norm_shape, jax.ShapeDtypeStruct((2, LANES), F32)],
+            [kept, got, own_got, ids_row, multiplier, bias],
             scratch=[pltpu.VMEM((EXTRA, LANES), F32)],
         )
 
@@ -312,29 +321,36 @@
         for index, group in enumerate(groups):
             first, last = index == 0, index == len(groups) - 1
             pieces = [p for g in group for p in (mine[g], theirs[g])]
+            visited_rows = 2 * half * len(group)
+
+            def score(sides, outs):
+                sources = [(own_block, near_block)[side] for side in sides]
+                return local_call(
+                    pair_kernel(len(group), sides, first, last),
+                    "pairs",
+                    outs,
+                    [params, *sources, *pieces, *state],
+                    scratch=[
+                        pltpu.VMEM((len(sides) * half, width), BF16),
+                        pltpu.VMEM((visited_rows, width), BF16),
+                        pltpu.VMEM((8, visited_rows), F32),
+                        pltpu.VMEM((EXTRA, LANES), F32),
+                    ],
+                    flops=4 * len(sides) * half * visited_rows * width,
+                    transcendentals=3 * len(sides) * half * visited_rows,
+                )
+
             if last:
-                outs = [whole_f32, whole_b16, block_b16, loss_shape]
+                grad_keep, grad_own, loss_own = score((0,), [whole_f32, whole_b16, loss_shape])
+                (grad_near,) = score((1,), [block_b16])
             else:
-                outs = [
-                    jax.ShapeDtypeStruct((2 * half, width), F32),
-                    jax.ShapeDtypeStruct((2 * half, 1), F32),
-                ]
-            visited_rows = 2 * half * len(group)
-            state = local_call(
-                pair_kernel(len(group), first, last),
-                "pairs",
-                outs,
-                [scale_bias, own_block, near_block, *pieces, *state],
-                scratch=[
-                    pltpu.VMEM((2 * half, width), BF16),
-                    pltpu.VMEM((visited_rows, width), BF16),
-                    pltpu.VMEM((8, visited_rows), F32),
-                    pltpu.VMEM((EXTRA, LANES), F32),
-                ],
-                flops=8 * half * visited_rows * width,
-                transcendentals=6 * half * visited_rows,
-            )
-        grad_keep, grad_own, grad_near, loss_own = state
+                state = score(
+                    (0, 1),
+                    [
+                        jax.ShapeDtypeStruct((2 * half, width), F32),
+                        jax.ShapeDtypeStruct((2 * half, 1), F32),
+                    ],
+                )
 
         pairs = [(s, b) for s in range(sections) for b in range(blocks)]
         diagonal_pairs = [
@@ -343,17 +359,22 @@
         diagonal = lax.ppermute(grad_near, ("sec", "blk"), diagonal_pairs)
         near = across_blk(grad_near, 1)
         across = lax.ppermute(grad_own, "sec", SWAP)
-        demb, loss_mine = local_call(
-            demb_kernel,
-            "demb",
-            [jax.ShapeDtypeStruct((2, half + EXTRA, width), BF16), loss_shape],
-            [
-                grad_keep, near, across, diagonal,
-                own_unit, own_norm, other_unit, other_norm, loss_own,
-            ],
-            scratch=[pltpu.VMEM((2, half, width), BF16), pltpu.VMEM((EXTRA, LANES), F32)],
-        )
-        demb_got = lax.ppermute(demb, "mp", SWAP)
+        own_demb, loss_mine = local_call(
+            own_demb_kernel,
+            "own_demb",
+            [jax.ShapeDtypeStruct((half + EXTRA, width), BF16), loss_shape],
+            [grad_keep, near, own_unit, own_norm, loss_own],
+            scratch=[pltpu.VMEM((half, width), BF16), pltpu.VMEM((EXTRA, LANES), F32)],
+        )
+        own_got = lax.ppermute(own_demb, "mp", SWAP)
+        (other_demb,) = local_call(
+            other_demb_kernel,
+            "other_demb",
+            [whole_b16],
+            [across, diagonal, other_unit, other_norm],
+            scratch=[pltpu.VMEM((half, width), BF16)],
+        )
+        other_got = lax.ppermute(other_demb, "mp", SWAP)
         return local_call(
             grads_kernel,
             "grads",
@@ -362,7 +383,7 @@
                 jax.ShapeDtypeStruct((rows, image_proj.shape[0]), BF16),
                 jax.ShapeDtypeStruct((rows, text_proj.shape[0]), BF16),
             ],
-            [demb, demb_got, loss_mine, image_proj, text_proj],
+            [own_demb, own_got, other_demb, other_got, loss_mine, image_proj, text_proj],
             scratch=[pltpu.VMEM((2, rows, width), BF16)],
             flops=2 * embed_flops,
         )

time: 56.6 us -> 54.5 us (0.963)
  waiting for transfers between devices: 29.7 us -> 26.4 us
  starting transfers between devices: 17.1 us -> 17.9 us
  Pallas kernels: 7.42 us -> 8.03 us
    ppermute x1, waiting for transfers between devices: 10.1 us -> 0.01 us  [per_device(): across = lax.ppermute(grad_own, 'sec', SWAP)]
    ppermute x5, waiting for transfers between devices: 8.37 us -> 16.8 us  [across_blk(): return lax.ppermute(value, 'blk', [(i, i ^ step) for i in range(blocks)])]
    ppermute x1, waiting for transfers between devices: 2.5 us -> 1.13 us  [per_device(): own_got = lax.ppermute(other_send, 'sec', SWAP)]
    ppermute x1 -> x2, starting transfers between devices: 1.18 us -> 1.81 us  [the longest x1 0.93 us: per_device(): other_got = lax.ppermute(other_demb, 'mp', SWAP)]
    pallas_call x10 -> x12, Pallas kernels: 7.42 us -> 8.03 us  [local_call(): pl.pallas_call(kernel, out_shape=outs, in_specs=[pl.BlockSpec(memory_spac...]
    ppermute x1 -> x2, waiting for transfers between devices: 1.47 us -> 1.11 us  [the longest x1 1.1 us: per_device(): other_got = lax.ppermute(other_demb, 'mp', SWAP)]
  transfers between devices with their start and end apart: 15 -> 16, of which waited for: 6 -> 6; matrix products, arithmetic and copies ran while one was open for 0% -> 0% of each run, Pallas kernels for 4% -> 6%
where the time goes in v4:
time: 54.5 us; the launch traced here: 54.3 us
  waiting for transfers between devices  26.4 us (48%)
  starting transfers between devices  17.9 us (33%)
  Pallas kernels  8.03 us (15%)
  between operations  2.03 us (4%)
    ppermute x5, waiting for transfers between devices, across_blk(): return lax.ppermute(value, 'blk', [(i, i ^ step) for i in range(blocks)])  16.8 us
    pallas_call x12, Pallas kernels, local_call(): pl.pallas_call(kernel, out_shape=outs, in_specs=[pl.BlockSpec(memory_spac...  8.03 us
    ppermute x4, starting transfers between devices, per_device(): theirs = [lax.ppermute(v, 'mp', SWAP) for v in mine]  7.95 us
    ppermute x1, waiting for transfers between devices, per_device(): other_got = lax.ppermute(own_send, 'sec', SWAP)  6.39 us
    ppermute x5, starting transfers between devices, across_blk(): return lax.ppermute(value, 'blk', [(i, i ^ step) for i in range(blocks)])  5.32 us
    ppermute x1, starting transfers between devices, per_device(): across = lax.ppermute(grad_own, 'sec', SWAP)  1.27 us
    ppermute x1, waiting for transfers between devices, per_device(): own_got = lax.ppermute(other_send, 'sec', SWAP)  1.13 us
    ppermute x1, waiting for transfers between devices, per_device(): other_got = lax.ppermute(other_demb, 'mp', SWAP)  1.1 us
  transfers between devices with their start and end apart: 16, of which 6 were waited for; matrix products, arithmetic and copies ran while one was open for 0% of the time, Pallas kernels for 6%

profile of v4, /device:TPU:19, one launch (start us, length us, event | category | flops | bytes accessed | tf_op | source)
XLA Modules:
  0.0 54.3 jit_solution(13503478917097642850)
XLA Ops:
  0.6 2.1 %embed_sent.1 = (bf16[2,96,1152]{2,1,0:T(8,128)(2,1)S(1)}, bf16[192,384]{1,0:T(8,128)(2,1)S(1)}, bf16[192,512]{1,0:T(8,128)(2,1)S(1)}, bf16[384,1152]{1,0:T(8,128)(2,1)S(1)}, bf16[512,1152]{1,0:T(8,128)(2,1)S(1)}) custom-call(bf16[192,384]{1,0:T(8,128)(2,1)} %refs_0_.1, bf16[192,512]{1,0:T(8,128)(2,1)} %refs_1_.1, bf16[384,1152]{1,0:T(8,128)(2,1)} %refs_2_.1, ...), custom_call_target="tpu_custom_call" | custom-call | flops 198180864 | bytes 2408448 | tf_op jit(solution)/shard_map/embed_sent/pallas_call | solution.py:21
  2.7 0.7 %collective-permute-start = (bf16[2,96,1152]{2,1,0:T(8,128)(2,1)S(1)}, bf16[2,96,1152]{2,1,0:T(8,128)(2,1)S(1)}, u32[]{:S(2)}, u32[]{:S(2)}) collective-permute-start(bf16[2,96,1152]{2,1,0:T(8,128)(2,1)S(1)} %get-tuple-element.31), channel_id=1, source_target_pairs={{0,1},{1,0},{2,3},{3,2},{4,5},{5,4},{6,7},{7,6},{8,9},{9,8},{10,11... | collective-permute-start | bytes 1327112 | tf_op jit(solution)/shard_map/ppermute | solution.py:283
  3.4 0.5 embed_kept.1.kept
  3.9 0.0 copy-start
  3.9 0.9 %collective-permute-done.got = bf16[2,96,1152]{2,1,0:T(8,128)(2,1)S(1)} collective-permute-done((bf16[2,96,1152]{2,1,0:T(8,128)(2,1)S(1)}, bf16[2,96,1152]{2,1,0:T(8,128)(2,1)S(1)}, u32[]{:S(2)}, u32[]{:S(2)}) %collective-permute-start) | collective-permute-done | bytes 442400 | tf_op jit(solution)/shard_map/ppermute | solution.py:283
  4.9 0.1 join_cores.1
  4.9 0.3 collective-permute-start.2
  5.3 6.4 %collective-permute-done.2.summed = bf16[96,1152]{1,0:T(8,128)(2,1)S(1)} collective-permute-done((bf16[96,1152]{1,0:T(8,128)(2,1)S(1)}, bf16[96,1152]{1,0:T(8,128)(2,1)S(1)}, u32[]{:S(2)}, u32[]{:S(2)}) %collective-permute-start.2) | collective-permute-done | bytes 221216 | tf_op jit(solution)/shard_map/ppermute | solution.py:294
  11.7 0.0 copy-done
  11.7 0.2 other_unit.1
  11.9 0.1 collective-permute-start.9
  12.0 1.3 %collective-permute-start.7 = (bf16[872,128]{1,0:T(8,128)(2,1)S(1)}, bf16[872,128]{1,0:T(8,128)(2,1)S(1)}, u32[]{:S(2)}, u32[]{:S(2)}) collective-permute-start(bf16[872,128]{1,0:T(8,128)(2,1)S(1)} %get-tuple-element.36.refs_2_), channel_id=1, source_target_pairs={{0,4},{2,6},{4,0},{6,2},{8,12},{10,14},{12,8},{14,10},{1,5},{3,7},... | collective-permute-start | bytes 669704 | tf_op jit(solution)/shard_map/ppermute | solution.py:252
  13.3 1.3 %collective-permute-start.3 = (bf16[872,128]{1,0:T(8,128)(2,1)S(1)}, bf16[872,128]{1,0:T(8,128)(2,1)S(1)}, u32[]{:S(2)}, u32[]{:S(2)}) collective-permute-start(bf16[872,128]{1,0:T(8,128)(2,1)S(1)} %get-tuple-element.36.refs_2_), channel_id=1, source_target_pairs={{0,12},{2,14},{4,8},{6,10},{8,4},{10,6},{12,0},{14,2},{1,13},{3,15... | collective-permute-start | bytes 669704 | tf_op jit(solution)/shard_map/ppermute | solution.py:252
  14.6 0.3 collective-permute-start.1
  16.1 2.4 %collective-permute-start.6 = (bf16[872,128]{1,0:T(8,128)(2,1)S(1)}, bf16[872,128]{1,0:T(8,128)(2,1)S(1)}, u32[]{:S(2)}, u32[]{:S(2)}) collective-permute-start(bf16[872,128]{1,0:T(8,128)(2,1)S(1)} %get-tuple-element.36.refs_2_), channel_id=1, source_target_pairs={{0,1},{1,0},{2,3},{3,2},{4,5},{5,4},{6,7},{7,6},{8,9},{9,8},{10,11... | collective-permute-start | bytes 669704 | tf_op jit(solution)/shard_map/ppermute | solution.py:316
  18.5 1.1 %collective-permute-done.1.summed = bf16[96,1152]{1,0:T(8,128)(2,1)S(1)} collective-permute-done((bf16[96,1152]{1,0:T(8,128)(2,1)S(1)}, bf16[96,1152]{1,0:T(8,128)(2,1)S(1)}, u32[]{:S(2)}, u32[]{:S(2)}) %collective-permute-start.1) | collective-permute-done | bytes 221216 | tf_op jit(solution)/shard_map/ppermute | solution.py:295
  19.7 0.2 own_unit.1
  19.9 1.3 %collective-permute-start.5 = (bf16[872,128]{1,0:T(8,128)(2,1)S(1)}, bf16[872,128]{1,0:T(8,128)(2,1)S(1)}, u32[]{:S(2)}, u32[]{:S(2)}) collective-permute-start(bf16[872,128]{1,0:T(8,128)(2,1)S(1)} %get-tuple-element.34.refs_0_), channel_id=1, source_target_pairs={{0,2},{2,0},{4,6},{6,4},{8,10},{10,8},{12,14},{14,12},{1,3},{3,1},... | collective-permute-start | bytes 669704 | tf_op jit(solution)/shard_map/ppermute | solution.py:252
  21.2 0.0 collective-permute-done.9.refs_6_
  21.2 3.7 %collective-permute-start.10 = (bf16[872,128]{1,0:T(8,128)(2,1)S(1)}, bf16[872,128]{1,0:T(8,128)(2,1)S(1)}, u32[]{:S(2)}, u32[]{:S(2)}) collective-permute-start(bf16[872,128]{1,0:T(8,128)(2,1)S(1)} %collective-permute-done.9.refs_6_), channel_id=1, source_target_pairs={{0,1},{1,0},{2,3},{3,2},{4,5},{5,4},{6,7},{7,6},{8,9},{9,8},{10,11... | collective-permute-start | bytes 669704 | tf_op jit(solution)/shard_map/ppermute | solution.py:316
  24.9 0.0 collective-permute-done.7.refs_4_
  24.9 1.3 %collective-permute-start.8 = (bf16[872,128]{1,0:T(8,128)(2,1)S(1)}, bf16[872,128]{1,0:T(8,128)(2,1)S(1)}, u32[]{:S(2)}, u32[]{:S(2)}) collective-permute-start(bf16[872,128]{1,0:T(8,128)(2,1)S(1)} %collective-permute-done.7.refs_4_), channel_id=1, source_target_pairs={{0,1},{1,0},{2,3},{3,2},{4,5},{5,4},{6,7},{7,6},{8,9},{9,8},{10,11... | collective-permute-start | bytes 669704 | tf_op jit(solution)/shard_map/ppermute | solution.py:316
  26.2 8.4 %collective-permute-done.3.block = bf16[872,128]{1,0:T(8,128)(2,1)S(1)} collective-permute-done((bf16[872,128]{1,0:T(8,128)(2,1)S(1)}, bf16[872,128]{1,0:T(8,128)(2,1)S(1)}, u32[]{:S(2)}, u32[]{:S(2)}) %collective-permute-start.3) | collective-permute-done | bytes 223264 | tf_op jit(solution)/shard_map/ppermute | solution.py:252
  34.6 0.6 %collective-permute-start.4 = (bf16[872,128]{1,0:T(8,128)(2,1)S(1)}, bf16[872,128]{1,0:T(8,128)(2,1)S(1)}, u32[]{:S(2)}, u32[]{:S(2)}) collective-permute-start(bf16[872,128]{1,0:T(8,128)(2,1)S(1)} %relay.1.refs_1_), channel_id=1, source_target_pairs={{0,1},{1,0},{2,3},{3,2},{4,5},{5,4},{6,7},{7,6},{8,9},{9,8},{10,11... | collective-permute-start | bytes 669704 | tf_op jit(solution)/shard_map/ppermute | solution.py:316
  35.2 0.0 collective-permute-done.5.refs_1_.refs_0_
  35.2 0.0 collective-permute-done.6.refs_3_
  35.2 0.0 collective-permute-done.10.refs_7_
  35.2 0.0 collective-permute-done.8.refs_5_
  35.2 1.5 %pairs.3 = (f32[192,1152]{1,0:T(8,128)S(1)}, f32[192,1]{1,0:T(8,128)S(1)}) custom-call(f32[2,128]{1,0:T(2,128)S(1)} %get-tuple-element.33.params, bf16[872,128]{1,0:T(8,128)(2,1)S(1)} %get-tuple-element.34.refs_0_, bf16[872,128]{1,0:T(8,128)(2,1)S(1)} %collective-permute-done.5.refs_1_.refs_0_, bf16[872,128]{1,0:T(8,128)(2,1)S(1)} %get-tuple-element.36.refs_2_, ...), custom_call_target="tpu_custom_call" | custom-call | flops 509607936 | bytes 1786880 | tf_op jit(solution)/shard_map/pairs/pallas_call | solution.py:21
  36.7 0.0 collective-permute-done.4.refs_2_
  36.7 0.7 %pairs.5 = bf16[872,128]{1,0:T(8,128)(2,1)S(1)} custom-call(f32[2,128]{1,0:T(2,128)S(1)} %get-tuple-element.33.params, bf16[872,128]{1,0:T(8,128)(2,1)S(1)} %collective-permute-done.5.refs_1_.refs_0_, bf16[872,128]{1,0:T(8,128)(2,1)S(1)} %relay.1.refs_1_, bf16[872,128]{1,0:T(8,128)(2,1)S(1)} %collective-permute-done.4.refs_2_, ...), custom_call_target="tpu_custom_call" | custom-call | flops 84934656 | bytes 1556224 | tf_op jit(solution)/shard_map/pairs/pallas_call | solution.py:21
  37.4 1.3 %collective-permute-start.11 = (bf16[872,128]{1,0:T(8,128)(2,1)S(1)}, bf16[872,128]{1,0:T(8,128)(2,1)S(1)}, u32[]{:S(2)}, u32[]{:S(2)}) collective-permute-start(bf16[872,128]{1,0:T(8,128)(2,1)S(1)} %pairs.5), channel_id=1, source_target_pairs={{0,2},{2,0},{4,6},{6,4},{8,10},{10,8},{12,14},{14,12},{1,3},{3,1},... | collective-permute-start | bytes 669704 | tf_op jit(solution)/shard_map/ppermute | solution.py:252
  38.7 0.2 collective-permute-start.14
  38.9 0.7 %pairs.4 = (f32[96,1152]{1,0:T(8,128)S(1)}, bf16[96,1152]{1,0:T(8,128)(2,1)S(1)}, f32[1,96]{1,0:T(1,128)S(1)}) custom-call(f32[2,128]{1,0:T(2,128)S(1)} %get-tuple-element.33.params, bf16[872,128]{1,0:T(8,128)(2,1)S(1)} %get-tuple-element.34.refs_0_, bf16[872,128]{1,0:T(8,128)(2,1)S(1)} %relay.1.refs_1_, ...), custom_call_target="tpu_custom_call" | custom-call | flops 84934656 | bytes 1556224 | tf_op jit(solution)/shard_map/pairs/pallas_call | solution.py:21
  39.6 1.3 %collective-permute-start.13 = (bf16[96,1152]{1,0:T(8,128)(2,1)S(1)}, bf16[96,1152]{1,0:T(8,128)(2,1)S(1)}, u32[]{:S(2)}, u32[]{:S(2)}) collective-permute-start(bf16[96,1152]{1,0:T(8,128)(2,1)S(1)} %get-tuple-element.47), channel_id=1, source_target_pairs={{0,16},{16,0},{1,17},{17,1},{2,18},{18,2},{3,19},{19,3},{4,20},{20... | collective-permute-start | bytes 663560 | tf_op jit(solution)/shard_map/ppermute | solution.py:361
  40.9 8.5 %collective-permute-done.11.near = bf16[872,128]{1,0:T(8,128)(2,1)S(1)} collective-permute-done((bf16[872,128]{1,0:T(8,128)(2,1)S(1)}, bf16[872,128]{1,0:T(8,128)(2,1)S(1)}, u32[]{:S(2)}, u32[]{:S(2)}) %collective-permute-start.11) | collective-permute-done | bytes 223264 | tf_op jit(solution)/shard_map/ppermute | solution.py:252
  49.3 0.2 own_demb.1
  49.6 0.9 %collective-permute-start.12 = (bf16[104,1152]{1,0:T(8,128)(2,1)S(1)}, bf16[104,1152]{1,0:T(8,128)(2,1)S(1)}, u32[]{:S(2)}, u32[]{:S(2)}) collective-permute-start(bf16[104,1152]{1,0:T(8,128)(2,1)S(1)} %get-tuple-element.46.own), channel_id=1, source_target_pairs={{0,1},{1,0},{2,3},{3,2},{4,5},{5,4},{6,7},{7,6},{8,9},{9,8},{10,11... | collective-permute-start | bytes 718856 | tf_op jit(solution)/shard_map/ppermute | solution.py:369
  50.5 0.0 collective-permute-done.13.across
  50.5 0.0 collective-permute-done.14.diagonal
  50.5 0.3 other_demb.1.other
  50.7 0.9 %collective-permute-start.15 = (bf16[96,1152]{1,0:T(8,128)(2,1)S(1)}, bf16[96,1152]{1,0:T(8,128)(2,1)S(1)}, u32[]{:S(2)}, u32[]{:S(2)}) collective-permute-start(bf16[96,1152]{1,0:T(8,128)(2,1)S(1)} %other_demb.1.other), channel_id=1, source_target_pairs={{0,1},{1,0},{2,3},{3,2},{4,5},{5,4},{6,7},{7,6},{8,9},{9,8},{10,11... | collective-permute-start | bytes 663560 | tf_op jit(solution)/shard_map/ppermute | solution.py:377
  51.7 1.1 %collective-permute-done.15.other_got = bf16[96,1152]{1,0:T(8,128)(2,1)S(1)} collective-permute-done((bf16[96,1152]{1,0:T(8,128)(2,1)S(1)}, bf16[96,1152]{1,0:T(8,128)(2,1)S(1)}, u32[]{:S(2)}, u32[]{:S(2)}) %collective-permute-start.15) | collective-permute-done | bytes 221216 | tf_op jit(solution)/shard_map/ppermute | solution.py:377
  52.8 0.0 collective-permute-done.12.own_got
  52.8 1.6 %grads.1 = (f32[1,192]{1,0:T(1,128)}, bf16[192,384]{1,0:T(8,128)(2,1)}, bf16[192,512]{1,0:T(8,128)(2,1)}) custom-call(bf16[104,1152]{1,0:T(8,128)(2,1)S(1)} %get-tuple-element.46.own, bf16[104,1152]{1,0:T(8,128)(2,1)S(1)} %collective-permute-done.12.own_got, bf16[96,1152]{1,0:T(8,128)(2,1)S(1)} %other_demb.1.other, ...), custom_call_target="tpu_custom_call" | custom-call | flops 396361728 | bytes 2986368 | tf_op jit(solution)/shard_map/grads/pallas_call | solution.py:21
  (1 shorter events, 0.0 us)
Async XLA Ops:
  2.7 2.2 %collective-permute-start = (bf16[2,96,1152]{2,1,0:T(8,128)(2,1)S(1)}, bf16[2,96,1152]{2,1,0:T(8,128)(2,1)S(1)}, u32[]{:S(2)}, u32[]{:S(2)}) collective-permute-start(bf16[2,96,1152]{2,1,0:T(8,128)(2,1)S(1)} %get-tuple-element.31), channel_id=1, source_target_pairs={{0,1},{1,0},{2,3},{3,2},{4,5},{5,4},{6,7},{7,6},{8,9},{9,8},{10,11... | collective-permute-start | bytes 1327112 | tf_op jit(solution)/shard_map/ppermute | solution.py:283
  3.9 7.7 %copy-start = (s32[192]{0:T(256)S(1)}, s32[192]{0:T(256)}, u32[]{:S(2)}) copy-start(s32[192]{0:T(256)} %param.13) | copy-start | bytes 2308
  4.9 6.7 %collective-permute-start.2 = (bf16[96,1152]{1,0:T(8,128)(2,1)S(1)}, bf16[96,1152]{1,0:T(8,128)(2,1)S(1)}, u32[]{:S(2)}, u32[]{:S(2)}) collective-permute-start(bf16[96,1152]{1,0:T(8,128)(2,1)S(1)} %get-tuple-element.35), channel_id=1, source_target_pairs={{0,16},{16,0},{1,17},{17,1},{2,18},{18,2},{3,19},{19,3},{4,20},{20... | collective-permute-start | bytes 663560 | tf_op jit(solution)/shard_map/ppermute | solution.py:294
  11.9 9.3 %collective-permute-start.9 = (bf16[872,128]{1,0:T(8,128)(2,1)S(1)}, bf16[872,128]{1,0:T(8,128)(2,1)S(1)}, u32[]{:S(2)}, u32[]{:S(2)}) collective-permute-start(bf16[872,128]{1,0:T(8,128)(2,1)S(1)} %get-tuple-element.36.refs_2_), channel_id=1, source_target_pairs={{0,8},{2,10},{4,12},{6,14},{8,0},{10,2},{12,4},{14,6},{1,9},{3,11}... | collective-permute-start | bytes 669704 | tf_op jit(solution)/shard_map/ppermute | solution.py:252
  12.0 13.0 %collective-permute-start.7 = (bf16[872,128]{1,0:T(8,128)(2,1)S(1)}, bf16[872,128]{1,0:T(8,128)(2,1)S(1)}, u32[]{:S(2)}, u32[]{:S(2)}) collective-permute-start(bf16[872,128]{1,0:T(8,128)(2,1)S(1)} %get-tuple-element.36.refs_2_), channel_id=1, source_target_pairs={{0,4},{2,6},{4,0},{6,2},{8,12},{10,14},{12,8},{14,10},{1,5},{3,7},... | collective-permute-start | bytes 669704 | tf_op jit(solution)/shard_map/ppermute | solution.py:252
  13.3 21.3 %collective-permute-start.3 = (bf16[872,128]{1,0:T(8,128)(2,1)S(1)}, bf16[872,128]{1,0:T(8,128)(2,1)S(1)}, u32[]{:S(2)}, u32[]{:S(2)}) collective-permute-start(bf16[872,128]{1,0:T(8,128)(2,1)S(1)} %get-tuple-element.36.refs_2_), channel_id=1, source_target_pairs={{0,12},{2,14},{4,8},{6,10},{8,4},{10,6},{12,0},{14,2},{1,13},{3,15... | collective-permute-start | bytes 669704 | tf_op jit(solution)/shard_map/ppermute | solution.py:252
  14.6 5.1 %collective-permute-start.1 = (bf16[96,1152]{1,0:T(8,128)(2,1)S(1)}, bf16[96,1152]{1,0:T(8,128)(2,1)S(1)}, u32[]{:S(2)}, u32[]{:S(2)}) collective-permute-start(bf16[96,1152]{1,0:T(8,128)(2,1)S(1)} %get-tuple-element.32), channel_id=1, source_target_pairs={{0,16},{16,0},{1,17},{17,1},{2,18},{18,2},{3,19},{19,3},{4,20},{20... | collective-permute-start | bytes 663560 | tf_op jit(solution)/shard_map/ppermute | solution.py:295
  16.1 19.0 %collective-permute-start.6 = (bf16[872,128]{1,0:T(8,128)(2,1)S(1)}, bf16[872,128]{1,0:T(8,128)(2,1)S(1)}, u32[]{:S(2)}, u32[]{:S(2)}) collective-permute-start(bf16[872,128]{1,0:T(8,128)(2,1)S(1)} %get-tuple-element.36.refs_2_), channel_id=1, source_target_pairs={{0,1},{1,0},{2,3},{3,2},{4,5},{5,4},{6,7},{7,6},{8,9},{9,8},{10,11... | collective-permute-start | bytes 669704 | tf_op jit(solution)/shard_map/ppermute | solution.py:316
  19.9 15.3 %collective-permute-start.5 = (bf16[872,128]{1,0:T(8,128)(2,1)S(1)}, bf16[872,128]{1,0:T(8,128)(2,1)S(1)}, u32[]{:S(2)}, u32[]{:S(2)}) collective-permute-start(bf16[872,128]{1,0:T(8,128)(2,1)S(1)} %get-tuple-element.34.refs_0_), channel_id=1, source_target_pairs={{0,2},{2,0},{4,6},{6,4},{8,10},{10,8},{12,14},{14,12},{1,3},{3,1},... | collective-permute-start | bytes 669704 | tf_op jit(solution)/shard_map/ppermute | solution.py:252
  21.2 14.0 %collective-permute-start.10 = (bf16[872,128]{1,0:T(8,128)(2,1)S(1)}, bf16[872,128]{1,0:T(8,128)(2,1)S(1)}, u32[]{:S(2)}, u32[]{:S(2)}) collective-permute-start(bf16[872,128]{1,0:T(8,128)(2,1)S(1)} %collective-permute-done.9.refs_6_), channel_id=1, source_target_pairs={{0,1},{1,0},{2,3},{3,2},{4,5},{5,4},{6,7},{7,6},{8,9},{9,8},{10,11... | collective-permute-start | bytes 669704 | tf_op jit(solution)/shard_map/ppermute | solution.py:316
  24.9 10.2 %collective-permute-start.8 = (bf16[872,128]{1,0:T(8,128)(2,1)S(1)}, bf16[872,128]{1,0:T(8,128)(2,1)S(1)}, u32[]{:S(2)}, u32[]{:S(2)}) collective-permute-start(bf16[872,128]{1,0:T(8,128)(2,1)S(1)} %collective-permute-done.7.refs_4_), channel_id=1, source_target_pairs={{0,1},{1,0},{2,3},{3,2},{4,5},{5,4},{6,7},{7,6},{8,9},{9,8},{10,11... | collective-permute-start | bytes 669704 | tf_op jit(solution)/shard_map/ppermute | solution.py:316
  34.6 2.1 %collective-permute-start.4 = (bf16[872,128]{1,0:T(8,128)(2,1)S(1)}, bf16[872,128]{1,0:T(8,128)(2,1)S(1)}, u32[]{:S(2)}, u32[]{:S(2)}) collective-permute-start(bf16[872,128]{1,0:T(8,128)(2,1)S(1)} %relay.1.refs_1_), channel_id=1, source_target_pairs={{0,1},{1,0},{2,3},{3,2},{4,5},{5,4},{6,7},{7,6},{8,9},{9,8},{10,11... | collective-permute-start | bytes 669704 | tf_op jit(solution)/shard_map/ppermute | solution.py:316
  37.4 11.9 %collective-permute-start.11 = (bf16[872,128]{1,0:T(8,128)(2,1)S(1)}, bf16[872,128]{1,0:T(8,128)(2,1)S(1)}, u32[]{:S(2)}, u32[]{:S(2)}) collective-permute-start(bf16[872,128]{1,0:T(8,128)(2,1)S(1)} %pairs.5), channel_id=1, source_target_pairs={{0,2},{2,0},{4,6},{6,4},{8,10},{10,8},{12,14},{14,12},{1,3},{3,1},... | collective-permute-start | bytes 669704 | tf_op jit(solution)/shard_map/ppermute | solution.py:252
  38.7 11.8 %collective-permute-start.14 = (bf16[872,128]{1,0:T(8,128)(2,1)S(1)}, bf16[872,128]{1,0:T(8,128)(2,1)S(1)}, u32[]{:S(2)}, u32[]{:S(2)}) collective-permute-start(bf16[872,128]{1,0:T(8,128)(2,1)S(1)} %pairs.5), channel_id=1, source_target_pairs={{0,18},{2,16},{4,22},{6,20},{8,26},{10,24},{12,30},{14,28},{16,2},... | collective-permute-start | bytes 669704 | tf_op jit(solution)/shard_map/ppermute | solution.py:359
  39.6 10.9 %collective-permute-start.13 = (bf16[96,1152]{1,0:T(8,128)(2,1)S(1)}, bf16[96,1152]{1,0:T(8,128)(2,1)S(1)}, u32[]{:S(2)}, u32[]{:S(2)}) collective-permute-start(bf16[96,1152]{1,0:T(8,128)(2,1)S(1)} %get-tuple-element.47), channel_id=1, source_target_pairs={{0,16},{16,0},{1,17},{17,1},{2,18},{18,2},{3,19},{19,3},{4,20},{20... | collective-permute-start | bytes 663560 | tf_op jit(solution)/shard_map/ppermute | solution.py:361
  49.6 3.2 %collective-permute-start.12 = (bf16[104,1152]{1,0:T(8,128)(2,1)S(1)}, bf16[104,1152]{1,0:T(8,128)(2,1)S(1)}, u32[]{:S(2)}, u32[]{:S(2)}) collective-permute-start(bf16[104,1152]{1,0:T(8,128)(2,1)S(1)} %get-tuple-element.46.own), channel_id=1, source_target_pairs={{0,1},{1,0},{2,3},{3,2},{4,5},{5,4},{6,7},{7,6},{8,9},{9,8},{10,11... | collective-permute-start | bytes 718856 | tf_op jit(solution)/shard_map/ppermute | solution.py:369
  50.7 2.0 %collective-permute-start.15 = (bf16[96,1152]{1,0:T(8,128)(2,1)S(1)}, bf16[96,1152]{1,0:T(8,128)(2,1)S(1)}, u32[]{:S(2)}, u32[]{:S(2)}) collective-permute-start(bf16[96,1152]{1,0:T(8,128)(2,1)S(1)} %other_demb.1.other), channel_id=1, source_target_pairs={{0,1},{1,0},{2,3},{3,2},{4,5},{5,4},{6,7},{7,6},{8,9},{9,8},{10,11... | collective-permute-start | bytes 663560 | tf_op jit(solution)/shard_map/ppermute | solution.py:377

commit v5 on v4

--- a/solution.py
+++ b/solution.py
@@ -78,24 +78,31 @@
     other_send[...] = (kept[1 - section] + got[1 - section].astype(F32)).astype(BF16)
 
 
-def write_block(block, value, extra):
+def block_rows(half, width):
+    return half * (width // LANES) + EXTRA
+
+
+def write_block(block, value, extra, base=0):
     half, width = value.shape
     for c in range(width // LANES):
-        block[pl.ds(c * half, half), :] = value[:, c * LANES : (c + 1) * LANES].astype(BF16)
-    block[pl.ds(half * (width // LANES), EXTRA), :] = extra.astype(BF16)
-
-
-def read_block(block, target, start, half):
+        rows = pl.ds(base + c * half, half)
+        block[rows, :] = value[:, c * LANES : (c + 1) * LANES].astype(BF16)
+    block[pl.ds(base + half * (width // LANES), EXTRA), :] = extra.astype(BF16)
+
+
+def read_block(block, target, start, half, base=0):
     for c in range(target.shape[1] // LANES):
-        target[pl.ds(start, half), pl.ds(c * LANES, LANES)] = block[pl.ds(c * half, half), :]
-
-
-def extra_rows(block):
-    return block[pl.ds(block.shape[0] - EXTRA, EXTRA), :].astype(F32)
-
-
-def block_ids(block):
-    extra = extra_rows(block)
+        rows = pl.ds(base + c * half, half)
+        target[pl.ds(start, half), pl.ds(c * LANES, LANES)] = block[rows, :]
+
+
+def extra_rows(block, end=None):
+    end = block.shape[0] if end is None else end
+    return block[pl.ds(end - EXTRA, EXTRA), :].astype(F32)
+
+
+def block_ids(block, end=None):
+    extra = extra_rows(block, end)
     return extra[0:1] * 128.0 + extra[1:2]
 
 
@@ -116,12 +123,8 @@
             params[1:2, :] = jnp.broadcast_to(bias[...], (1, LANES))
         else:
             unit, block, norm, extra = refs
-        half = summed.shape[0]
+        half, width = summed.shape
         core = lax.axis_index("mp")
-        half_ids = jnp.where(core == 0, ids[0:1, :half], ids[0:1, half : 2 * half])
-        extra[...] = jnp.zeros_like(extra)
-        extra[0:1, 0:half] = (half_ids >> 7).astype(F32)
-        extra[1:2, 0:half] = (half_ids & 127).astype(F32)
         section = lax.axis_index("sec")
         section = section if own else 1 - section
         emb = kept[section] + got[section].astype(F32) + summed[...].astype(F32)
@@ -129,19 +132,38 @@
         value = emb / row_norm
         unit[...] = value
         norm[...] = row_norm
-        write_block(block, value, extra[...])
+        half_ids = jnp.where(core == 0, ids[0:1, :half], ids[0:1, half : 2 * half])
+        size = half if own else half // 2
+        for index, start in enumerate(range(0, half, size)):
+            some = half_ids[:, start : start + size]
+            extra[index] = jnp.zeros_like(extra[index])
+            extra[index, 0:1, 0:size] = (some >> 7).astype(F32)
+            extra[index, 1:2, 0:size] = (some & 127).astype(F32)
+            base = index * block_rows(size, width)
+            write_block(block, value[start : start + size], extra[index], base)
 
     return kernel
 
 
-def relay_kernel(block, out):
-    out[...] = block[...]
+def join_far_kernel(parts):
+    def kernel(*refs):
+        size = refs[0].shape[0]
+        out = refs[-1]
+        if parts == 1:
+            out[...] = refs[0][...]
+            return
+        inner, first, direct, passed = lax.axis_index("blk"), refs[0], refs[1], refs[2]
+        inner = jnp.logical_and(inner >= 2, inner < 6)
+        out[pl.ds(0, size), :] = first[...]
+        out[pl.ds(size, size), :] = jnp.where(inner, direct[...], passed[...])
+
+    return kernel
 
 
 def pair_kernel(blocks, sides, first, last):
     def kernel(params, *refs):
         sources, refs = refs[: len(sides)], refs[len(sides) :]
-        pieces, refs = refs[: 2 * blocks], refs[2 * blocks :]
+        pieces, refs = refs[:blocks], refs[blocks:]
         if not first:
             (grad_in, loss_in), refs = refs[:2], refs[2:]
         outs, (own, visited, visit_ids, extra) = refs[:-4], refs[-4:]
@@ -152,9 +174,15 @@
             square = jnp.broadcast_to(block_ids(source), (LANES, LANES))
             columns.append(jnp.transpose(square)[:half, 0:1])
         ids = jnp.concatenate(columns, axis=0) if len(sides) > 1 else columns[0]
-        for index, piece in enumerate(pieces):
-            read_block(piece, visited, index * half, half)
-            visit_ids[0:1, pl.ds(index * half, half)] = block_ids(piece)[:, :half]
+        part = half // 2
+        size = block_rows(part, own.shape[1])
+        start = 0
+        for piece in pieces:
+            for base in range(0, piece.shape[0], size):
+                read_block(piece, visited, start, part, base)
+                ids_row = block_ids(piece, base + size)
+                visit_ids[0:1, pl.ds(start, part)] = ids_row[:, :part]
+                start += part
         scale = params[0:1, 0:1]
         scores = (
             scale * lax.dot_general(own[...], visited[...], NT, preferred_element_type=F32)
@@ -258,10 +286,11 @@
         rows = image_pooled.shape[0]
         half = rows // 2
         width = image_proj.shape[1]
-        block_rows = half * (width // LANES) + EXTRA
+        part_rows = block_rows(half // 2, width)
         whole_f32 = jax.ShapeDtypeStruct((half, width), F32)
         whole_b16 = jax.ShapeDtypeStruct((half, width), BF16)
-        block_b16 = jax.ShapeDtypeStruct((block_rows, LANES), BF16)
+        block_b16 = jax.ShapeDtypeStruct((block_rows(half, width), LANES), BF16)
+        visit_b16 = jax.ShapeDtypeStruct((2 * part_rows, LANES), BF16)
         norm_shape = jax.ShapeDtypeStruct((half, 1), F32)
         loss_shape = jax.ShapeDtypeStruct((1, half), F32)
         towers = (image_pooled, text_pooled, image_proj, text_proj)
@@ -296,23 +325,34 @@
         other_unit, visit, other_norm = local_call(
             unit_kernel(False),
             "other_unit",
-            [whole_f32, block_b16, norm_shape],
+            [whole_f32, visit_b16, norm_shape],
             [kept, got, other_got, ids_row],
-            scratch=[pltpu.VMEM((EXTRA, LANES), F32)],
+            scratch=[pltpu.VMEM((2, EXTRA, LANES), F32)],
         )
         own_unit, own_block, own_norm, params = local_call(
             unit_kernel(True),
             "own_unit",
             [whole_f32, block_b16, norm_shape, jax.ShapeDtypeStruct((2, LANES), F32)],
             [kept, got, own_got, ids_row, multiplier, bias],
-            scratch=[pltpu.VMEM((EXTRA, LANES), F32)],
+            scratch=[pltpu.VMEM((1, EXTRA, LANES), F32)],
         )
 
         steps = list(range(0, blocks, 2))
-        mine = [visit] + [across_blk(visit, k) for k in steps[1:]]
+        mine = [across_blk(visit, k) for k in steps[1:-1]]
+        if blocks == 8:
+            first = across_blk(visit[:part_rows], 6)
+            second = visit[part_rows:]
+            direct = lax.ppermute(second, "blk", [(2, 4), (4, 2), (3, 5), (5, 3)])
+            passed = mine[1][part_rows:]
+            passed = lax.ppermute(passed, "blk", [(4, 6), (5, 7), (2, 0), (3, 1)])
+            far = [first, direct, passed]
+        else:
+            far = [across_blk(visit, steps[-1])]
         near_block = across_blk(own_block, 1)
-        mine = [visit] + [lax.optimization_barrier((v, own_block))[0] for v in mine[1:]]
-        mine[-1:] = local_call(relay_kernel, "relay", [block_b16], [mine[-1]], flops=10**9)
+        mine = [lax.optimization_barrier((v, own_block))[0] for v in mine]
+        far = [lax.optimization_barrier((v, own_block))[0] for v in far]
+        mine = [visit, *mine]
+        mine += local_call(join_far_kernel(len(far)), "join_far", [visit_b16], far, flops=10**9)
         theirs = [lax.ppermute(v, "mp", SWAP) for v in mine]
 
         early = list(range(len(steps) - 1))
@@ -326,7 +366,7 @@
             def score(sides, outs):
                 sources = [(own_block, near_block)[side] for side in sides]
                 return local_call(
-                    pair_kernel(len(group), sides, first, last),
+                    pair_kernel(len(pieces), sides, first, last),
                     "pairs",
                     outs,
                     [params, *sources, *pieces, *state],

time: 54.5 us -> 59.7 us (1.095)
  starting transfers between devices: 17.9 us -> 26 us
  waiting for transfers between devices: 26.4 us -> 23.3 us
    ppermute x0 -> x2, starting transfers between devices: none -> 11.8 us  [the longest x1 8.65 us: per_device(): passed = lax.ppermute(passed, 'blk', [(4, 6), (5, 7), (2, 0), (3, 1)])]
    ppermute x4, starting transfers between devices: 7.95 us -> 3.24 us  [per_device(): theirs = [lax.ppermute(v, 'mp', SWAP) for v in mine]]
    ppermute x1, waiting for transfers between devices: 6.39 us -> 5.14 us  [per_device(): other_got = lax.ppermute(own_send, 'sec', SWAP)]
    ppermute x1, waiting for transfers between devices: 1.13 us -> 0.01 us  [per_device(): own_got = lax.ppermute(other_send, 'sec', SWAP)]
    ppermute x1, starting transfers between devices: 0.88 us -> 2 us  [per_device(): own_got = lax.ppermute(own_demb, 'mp', SWAP)]
    ppermute x5, starting transfers between devices: 5.32 us -> 4.31 us  [across_blk(): return lax.ppermute(value, 'blk', [(i, i ^ step) for i in range(blocks)])]
    ppermute x1, starting transfers between devices: 0.26 us -> 1.21 us  [per_device(): own_got = lax.ppermute(other_send, 'sec', SWAP)]
    ppermute x5, waiting for transfers between devices: 16.8 us -> 16.1 us  [across_blk(): return lax.ppermute(value, 'blk', [(i, i ^ step) for i in range(blocks)])]
  transfers between devices with their start and end apart: 16 -> 18, of which waited for: 6 -> 6; matrix products, arithmetic and copies ran while one was open for 0% -> 0% of each run, Pallas kernels for 6% -> 6%
where the time goes in v5:
time: 59.7 us; the launch traced here: 59.5 us
  starting transfers between devices  26 us (44%)
  waiting for transfers between devices  23.3 us (39%)
  Pallas kernels  8.06 us (14%)
  between operations  2.06 us (3%)
    ppermute x5, waiting for transfers between devices, across_blk(): return lax.ppermute(value, 'blk', [(i, i ^ step) for i in range(blocks)])  16.1 us
    ppermute x1, starting transfers between devices, per_device(): passed = lax.ppermute(passed, 'blk', [(4, 6), (5, 7), (2, 0), (3, 1)])  8.65 us
    pallas_call x12, Pallas kernels, local_call(): pl.pallas_call(kernel, out_shape=outs, in_specs=[pl.BlockSpec(memory_spac...  8.06 us
    ppermute x1, waiting for transfers between devices, per_device(): other_got = lax.ppermute(own_send, 'sec', SWAP)  5.14 us
    ppermute x5, starting transfers between devices, across_blk(): return lax.ppermute(value, 'blk', [(i, i ^ step) for i in range(blocks)])  4.31 us
    ppermute x4, starting transfers between devices, per_device(): theirs = [lax.ppermute(v, 'mp', SWAP) for v in mine]  3.24 us
    ppermute x1, starting transfers between devices, per_device(): direct = lax.ppermute(second, 'blk', [(2, 4), (4, 2), (3, 5), (5, 3)])  3.18 us
    ppermute x1, starting transfers between devices, per_device(): own_got = lax.ppermute(own_demb, 'mp', SWAP)  2 us
  transfers between devices with their start and end apart: 18, of which 6 were waited for; matrix products, arithmetic and copies ran while one was open for 0% of the time, Pallas kernels for 6%

profile of v5, /device:TPU:19, one launch (start us, length us, event | category | flops | bytes accessed | tf_op | source)
XLA Modules:
  0.0 59.5 jit_solution(6614831568134016625)
XLA Ops:
  0.6 2.1 %embed_sent.1 = (bf16[2,96,1152]{2,1,0:T(8,128)(2,1)S(1)}, bf16[192,384]{1,0:T(8,128)(2,1)S(1)}, bf16[192,512]{1,0:T(8,128)(2,1)S(1)}, bf16[384,1152]{1,0:T(8,128)(2,1)S(1)}, bf16[512,1152]{1,0:T(8,128)(2,1)S(1)}) custom-call(bf16[192,384]{1,0:T(8,128)(2,1)} %refs_0_.1, bf16[192,512]{1,0:T(8,128)(2,1)} %refs_1_.1, bf16[384,1152]{1,0:T(8,128)(2,1)} %refs_2_.1, ...), custom_call_target="tpu_custom_call" | custom-call | flops 198180864 | bytes 2408448 | tf_op jit(solution)/shard_map/embed_sent/pallas_call | solution.py:21
  2.7 0.7 %collective-permute-start = (bf16[2,96,1152]{2,1,0:T(8,128)(2,1)S(1)}, bf16[2,96,1152]{2,1,0:T(8,128)(2,1)S(1)}, u32[]{:S(2)}, u32[]{:S(2)}) collective-permute-start(bf16[2,96,1152]{2,1,0:T(8,128)(2,1)S(1)} %get-tuple-element.33), channel_id=1, source_target_pairs={{0,1},{1,0},{2,3},{3,2},{4,5},{5,4},{6,7},{7,6},{8,9},{9,8},{10,11... | collective-permute-start | bytes 1327112 | tf_op jit(solution)/shard_map/ppermute | solution.py:312
  3.4 0.5 embed_kept.1.kept
  3.9 0.0 copy-start
  3.9 0.9 %collective-permute-done.got = bf16[2,96,1152]{2,1,0:T(8,128)(2,1)S(1)} collective-permute-done((bf16[2,96,1152]{2,1,0:T(8,128)(2,1)S(1)}, bf16[2,96,1152]{2,1,0:T(8,128)(2,1)S(1)}, u32[]{:S(2)}, u32[]{:S(2)}) %collective-permute-start) | collective-permute-done | bytes 442400 | tf_op jit(solution)/shard_map/ppermute | solution.py:312
  4.9 0.1 join_cores.1
  4.9 0.3 collective-permute-start.2
  5.3 1.2 %collective-permute-start.1 = (bf16[96,1152]{1,0:T(8,128)(2,1)S(1)}, bf16[96,1152]{1,0:T(8,128)(2,1)S(1)}, u32[]{:S(2)}, u32[]{:S(2)}) collective-permute-start(bf16[96,1152]{1,0:T(8,128)(2,1)S(1)} %get-tuple-element.34), channel_id=1, source_target_pairs={{0,16},{16,0},{1,17},{17,1},{2,18},{18,2},{3,19},{19,3},{4,20},{20... | collective-permute-start | bytes 663560 | tf_op jit(solution)/shard_map/ppermute | solution.py:324
  6.5 5.1 %collective-permute-done.2.summed = bf16[96,1152]{1,0:T(8,128)(2,1)S(1)} collective-permute-done((bf16[96,1152]{1,0:T(8,128)(2,1)S(1)}, bf16[96,1152]{1,0:T(8,128)(2,1)S(1)}, u32[]{:S(2)}, u32[]{:S(2)}) %collective-permute-start.2) | collective-permute-done | bytes 221216 | tf_op jit(solution)/shard_map/ppermute | solution.py:323
  11.6 0.2 other_unit.1
  11.8 0.2 collective-permute-start.5
  12.0 1.3 %collective-permute-start.10 = (bf16[880,128]{1,0:T(8,128)(2,1)S(1)}, bf16[880,128]{1,0:T(8,128)(2,1)S(1)}, u32[]{:S(2)}, u32[]{:S(2)}) collective-permute-start(bf16[880,128]{1,0:T(8,128)(2,1)S(1)} %get-tuple-element.38.refs_2_), channel_id=1, source_target_pairs={{0,4},{2,6},{4,0},{6,2},{8,12},{10,14},{12,8},{14,10},{1,5},{3,7},... | collective-permute-start | bytes 675848 | tf_op jit(solution)/shard_map/ppermute | solution.py:280
  13.3 3.2 %collective-permute-start.4 = (bf16[440,128]{1,0:T(8,128)(2,1)S(1)}, bf16[440,128]{1,0:T(8,128)(2,1)S(1)}, u32[]{:S(2)}, u32[]{:S(2)}) collective-permute-start(bf16[440,128]{1,0:T(8,128)(2,1)S(1)} %get-tuple-element.55), channel_id=1, source_target_pairs={{4,8},{8,4},{6,10},{10,6},{5,9},{9,5},{7,11},{11,7},{20,24},{24,20... | collective-permute-start | bytes 337928 | tf_op jit(solution)/shard_map/ppermute | solution.py:345
  16.5 0.3 collective-permute-start.3
  16.7 3.9 %collective-permute-done.5.refs_6_ = bf16[880,128]{1,0:T(8,128)(2,1)S(1)} collective-permute-done((bf16[880,128]{1,0:T(8,128)(2,1)S(1)}, bf16[880,128]{1,0:T(8,128)(2,1)S(1)}, u32[]{:S(2)}, u32[]{:S(2)}) %collective-permute-start.5) | collective-permute-done | bytes 225312 | tf_op jit(solution)/shard_map/ppermute | solution.py:280
  20.6 8.6 %collective-permute-start.6 = (bf16[440,128]{1,0:T(8,128)(2,1)S(1)}, bf16[440,128]{1,0:T(8,128)(2,1)S(1)}, u32[]{:S(2)}, u32[]{:S(2)}) collective-permute-start(bf16[440,128]{1,0:T(8,128)(2,1)S(1)} %slice.12), channel_id=1, source_target_pairs={{8,12},{10,14},{4,0},{6,2},{9,13},{11,15},{5,1},{7,3},{24,28},{26,... | collective-permute-start | bytes 337928 | tf_op jit(solution)/shard_map/ppermute | solution.py:347
  30.6 0.0 collective-permute-done.1.summed
  30.6 2.4 %collective-permute-start.9 = (bf16[880,128]{1,0:T(8,128)(2,1)S(1)}, bf16[880,128]{1,0:T(8,128)(2,1)S(1)}, u32[]{:S(2)}, u32[]{:S(2)}) collective-permute-start(bf16[880,128]{1,0:T(8,128)(2,1)S(1)} %get-tuple-element.38.refs_2_), channel_id=1, source_target_pairs={{0,1},{1,0},{2,3},{3,2},{4,5},{5,4},{6,7},{7,6},{8,9},{9,8},{10,11... | collective-permute-start | bytes 675848 | tf_op jit(solution)/shard_map/ppermute | solution.py:356
  32.9 0.2 own_unit.1
  33.2 0.0 collective-permute-done.4.refs_1_
  33.2 1.3 %collective-permute-start.8 = (bf16[872,128]{1,0:T(8,128)(2,1)S(1)}, bf16[872,128]{1,0:T(8,128)(2,1)S(1)}, u32[]{:S(2)}, u32[]{:S(2)}) collective-permute-start(bf16[872,128]{1,0:T(8,128)(2,1)S(1)} %get-tuple-element.36.refs_0_), channel_id=1, source_target_pairs={{0,2},{2,0},{4,6},{6,4},{8,10},{10,8},{12,14},{14,12},{1,3},{3,1},... | collective-permute-start | bytes 669704 | tf_op jit(solution)/shard_map/ppermute | solution.py:280
  34.5 0.0 collective-permute-done.3.refs_0_
  34.5 0.3 collective-permute-start.12
  34.8 0.0 collective-permute-done.10.refs_4_
  34.8 0.2 collective-permute-start.11
  35.0 0.0 collective-permute-done.6.refs_2_
  35.1 0.4 collective-permute-start.7
  35.4 4.9 %collective-permute-done.8.refs_1_.refs_0_ = bf16[872,128]{1,0:T(8,128)(2,1)S(1)} collective-permute-done((bf16[872,128]{1,0:T(8,128)(2,1)S(1)}, bf16[872,128]{1,0:T(8,128)(2,1)S(1)}, u32[]{:S(2)}, u32[]{:S(2)}) %collective-permute-start.8) | collective-permute-done | bytes 223264 | tf_op jit(solution)/shard_map/ppermute | solution.py:280
  40.3 0.0 collective-permute-done.9.refs_3_
  40.3 0.0 collective-permute-done.12.refs_7_
  40.3 0.0 collective-permute-done.11.refs_5_
  40.4 1.6 %pairs.3 = (f32[192,1152]{1,0:T(8,128)S(1)}, f32[192,1]{1,0:T(8,128)S(1)}) custom-call(f32[2,128]{1,0:T(2,128)S(1)} %get-tuple-element.35.params, bf16[872,128]{1,0:T(8,128)(2,1)S(1)} %get-tuple-element.36.refs_0_, bf16[872,128]{1,0:T(8,128)(2,1)S(1)} %collective-permute-done.8.refs_1_.refs_0_, bf16[880,128]{1,0:T(8,128)(2,1)S(1)} %get-tuple-element.38.refs_2_, ...), custom_call_target="tpu_custom_call" | custom-call | flops 509607936 | bytes 1799168 | tf_op jit(solution)/shard_map/pairs/pallas_call | solution.py:21
  41.9 0.0 collective-permute-done.7.refs_2_
  41.9 0.7 %pairs.5 = bf16[872,128]{1,0:T(8,128)(2,1)S(1)} custom-call(f32[2,128]{1,0:T(2,128)S(1)} %get-tuple-element.35.params, bf16[872,128]{1,0:T(8,128)(2,1)S(1)} %collective-permute-done.8.refs_1_.refs_0_, bf16[880,128]{1,0:T(8,128)(2,1)S(1)} %join_far.1.refs_1_, bf16[880,128]{1,0:T(8,128)(2,1)S(1)} %collective-permute-done.7.refs_2_, ...), custom_call_target="tpu_custom_call" | custom-call | flops 84934656 | bytes 1560320 | tf_op jit(solution)/shard_map/pairs/pallas_call | solution.py:21
  42.6 1.3 %collective-permute-start.13 = (bf16[872,128]{1,0:T(8,128)(2,1)S(1)}, bf16[872,128]{1,0:T(8,128)(2,1)S(1)}, u32[]{:S(2)}, u32[]{:S(2)}) collective-permute-start(bf16[872,128]{1,0:T(8,128)(2,1)S(1)} %pairs.5), channel_id=1, source_target_pairs={{0,2},{2,0},{4,6},{6,4},{8,10},{10,8},{12,14},{14,12},{1,3},{3,1},... | collective-permute-start | bytes 669704 | tf_op jit(solution)/shard_map/ppermute | solution.py:280
  43.9 0.0 collective-permute-start.16
  43.9 0.7 %pairs.4 = (f32[96,1152]{1,0:T(8,128)S(1)}, bf16[96,1152]{1,0:T(8,128)(2,1)S(1)}, f32[1,96]{1,0:T(1,128)S(1)}) custom-call(f32[2,128]{1,0:T(2,128)S(1)} %get-tuple-element.35.params, bf16[872,128]{1,0:T(8,128)(2,1)S(1)} %get-tuple-element.36.refs_0_, bf16[880,128]{1,0:T(8,128)(2,1)S(1)} %join_far.1.refs_1_, ...), custom_call_target="tpu_custom_call" | custom-call | flops 84934656 | bytes 1560320 | tf_op jit(solution)/shard_map/pairs/pallas_call | solution.py:21
  44.6 1.5 %collective-permute-start.15 = (bf16[96,1152]{1,0:T(8,128)(2,1)S(1)}, bf16[96,1152]{1,0:T(8,128)(2,1)S(1)}, u32[]{:S(2)}, u32[]{:S(2)}) collective-permute-start(bf16[96,1152]{1,0:T(8,128)(2,1)S(1)} %get-tuple-element.51), channel_id=1, source_target_pairs={{0,16},{16,0},{1,17},{17,1},{2,18},{18,2},{3,19},{19,3},{4,20},{20... | collective-permute-start | bytes 663560 | tf_op jit(solution)/shard_map/ppermute | solution.py:401
  46.1 7.3 %collective-permute-done.13.near = bf16[872,128]{1,0:T(8,128)(2,1)S(1)} collective-permute-done((bf16[872,128]{1,0:T(8,128)(2,1)S(1)}, bf16[872,128]{1,0:T(8,128)(2,1)S(1)}, u32[]{:S(2)}, u32[]{:S(2)}) %collective-permute-start.13) | collective-permute-done | bytes 223264 | tf_op jit(solution)/shard_map/ppermute | solution.py:280
  53.4 0.2 own_demb.1
  53.7 2.0 %collective-permute-start.14 = (bf16[104,1152]{1,0:T(8,128)(2,1)S(1)}, bf16[104,1152]{1,0:T(8,128)(2,1)S(1)}, u32[]{:S(2)}, u32[]{:S(2)}) collective-permute-start(bf16[104,1152]{1,0:T(8,128)(2,1)S(1)} %get-tuple-element.50.own), channel_id=1, source_target_pairs={{0,1},{1,0},{2,3},{3,2},{4,5},{5,4},{6,7},{7,6},{8,9},{9,8},{10,11... | collective-permute-start | bytes 718856 | tf_op jit(solution)/shard_map/ppermute | solution.py:409
  55.7 0.0 collective-permute-done.15.across
  55.7 0.0 collective-permute-done.16.diagonal
  55.7 0.2 other_demb.1.other
  55.9 0.9 %collective-permute-start.17 = (bf16[96,1152]{1,0:T(8,128)(2,1)S(1)}, bf16[96,1152]{1,0:T(8,128)(2,1)S(1)}, u32[]{:S(2)}, u32[]{:S(2)}) collective-permute-start(bf16[96,1152]{1,0:T(8,128)(2,1)S(1)} %other_demb.1.other), channel_id=1, source_target_pairs={{0,1},{1,0},{2,3},{3,2},{4,5},{5,4},{6,7},{7,6},{8,9},{9,8},{10,11... | collective-permute-start | bytes 663560 | tf_op jit(solution)/shard_map/ppermute | solution.py:417
  56.8 1.1 %collective-permute-done.17.other_got = bf16[96,1152]{1,0:T(8,128)(2,1)S(1)} collective-permute-done((bf16[96,1152]{1,0:T(8,128)(2,1)S(1)}, bf16[96,1152]{1,0:T(8,128)(2,1)S(1)}, u32[]{:S(2)}, u32[]{:S(2)}) %collective-permute-start.17) | collective-permute-done | bytes 221216 | tf_op jit(solution)/shard_map/ppermute | solution.py:417
  58.0 0.0 collective-permute-done.14.own_got
  58.0 1.6 %grads.1 = (f32[1,192]{1,0:T(1,128)}, bf16[192,384]{1,0:T(8,128)(2,1)}, bf16[192,512]{1,0:T(8,128)(2,1)}) custom-call(bf16[104,1152]{1,0:T(8,128)(2,1)S(1)} %get-tuple-element.50.own, bf16[104,1152]{1,0:T(8,128)(2,1)S(1)} %collective-permute-done.14.own_got, bf16[96,1152]{1,0:T(8,128)(2,1)S(1)} %other_demb.1.other, ...), custom_call_target="tpu_custom_call" | custom-call | flops 396361728 | bytes 2986368 | tf_op jit(solution)/shard_map/grads/pallas_call | solution.py:21
  (4 shorter events, 0.1 us)
Async XLA Ops:
  2.7 2.2 %collective-permute-start = (bf16[2,96,1152]{2,1,0:T(8,128)(2,1)S(1)}, bf16[2,96,1152]{2,1,0:T(8,128)(2,1)S(1)}, u32[]{:S(2)}, u32[]{:S(2)}) collective-permute-start(bf16[2,96,1152]{2,1,0:T(8,128)(2,1)S(1)} %get-tuple-element.33), channel_id=1, source_target_pairs={{0,1},{1,0},{2,3},{3,2},{4,5},{5,4},{6,7},{7,6},{8,9},{9,8},{10,11... | collective-permute-start | bytes 1327112 | tf_op jit(solution)/shard_map/ppermute | solution.py:312
  3.9 7.7 %copy-start = (s32[192]{0:T(256)S(1)}, s32[192]{0:T(256)}, u32[]{:S(2)}) copy-start(s32[192]{0:T(256)} %param.13) | copy-start | bytes 2308
  4.9 6.7 %collective-permute-start.2 = (bf16[96,1152]{1,0:T(8,128)(2,1)S(1)}, bf16[96,1152]{1,0:T(8,128)(2,1)S(1)}, u32[]{:S(2)}, u32[]{:S(2)}) collective-permute-start(bf16[96,1152]{1,0:T(8,128)(2,1)S(1)} %get-tuple-element.37), channel_id=1, source_target_pairs={{0,16},{16,0},{1,17},{17,1},{2,18},{18,2},{3,19},{19,3},{4,20},{20... | collective-permute-start | bytes 663560 | tf_op jit(solution)/shard_map/ppermute | solution.py:323
  5.3 25.3 %collective-permute-start.1 = (bf16[96,1152]{1,0:T(8,128)(2,1)S(1)}, bf16[96,1152]{1,0:T(8,128)(2,1)S(1)}, u32[]{:S(2)}, u32[]{:S(2)}) collective-permute-start(bf16[96,1152]{1,0:T(8,128)(2,1)S(1)} %get-tuple-element.34), channel_id=1, source_target_pairs={{0,16},{16,0},{1,17},{17,1},{2,18},{18,2},{3,19},{19,3},{4,20},{20... | collective-permute-start | bytes 663560 | tf_op jit(solution)/shard_map/ppermute | solution.py:324
  11.8 8.8 %collective-permute-start.5 = (bf16[880,128]{1,0:T(8,128)(2,1)S(1)}, bf16[880,128]{1,0:T(8,128)(2,1)S(1)}, u32[]{:S(2)}, u32[]{:S(2)}) collective-permute-start(bf16[880,128]{1,0:T(8,128)(2,1)S(1)} %get-tuple-element.38.refs_2_), channel_id=1, source_target_pairs={{0,8},{2,10},{4,12},{6,14},{8,0},{10,2},{12,4},{14,6},{1,9},{3,11}... | collective-permute-start | bytes 675848 | tf_op jit(solution)/shard_map/ppermute | solution.py:280
  12.0 22.8 %collective-permute-start.10 = (bf16[880,128]{1,0:T(8,128)(2,1)S(1)}, bf16[880,128]{1,0:T(8,128)(2,1)S(1)}, u32[]{:S(2)}, u32[]{:S(2)}) collective-permute-start(bf16[880,128]{1,0:T(8,128)(2,1)S(1)} %get-tuple-element.38.refs_2_), channel_id=1, source_target_pairs={{0,4},{2,6},{4,0},{6,2},{8,12},{10,14},{12,8},{14,10},{1,5},{3,7},... | collective-permute-start | bytes 675848 | tf_op jit(solution)/shard_map/ppermute | solution.py:280
  13.3 19.9 %collective-permute-start.4 = (bf16[440,128]{1,0:T(8,128)(2,1)S(1)}, bf16[440,128]{1,0:T(8,128)(2,1)S(1)}, u32[]{:S(2)}, u32[]{:S(2)}) collective-permute-start(bf16[440,128]{1,0:T(8,128)(2,1)S(1)} %get-tuple-element.55), channel_id=1, source_target_pairs={{4,8},{8,4},{6,10},{10,6},{5,9},{9,5},{7,11},{11,7},{20,24},{24,20... | collective-permute-start | bytes 337928 | tf_op jit(solution)/shard_map/ppermute | solution.py:345
  16.5 18.0 %collective-permute-start.3 = (bf16[440,128]{1,0:T(8,128)(2,1)S(1)}, bf16[440,128]{1,0:T(8,128)(2,1)S(1)}, u32[]{:S(2)}, u32[]{:S(2)}) collective-permute-start(bf16[440,128]{1,0:T(8,128)(2,1)S(1)} %get-tuple-element.56), channel_id=1, source_target_pairs={{0,12},{2,14},{4,8},{6,10},{8,4},{10,6},{12,0},{14,2},{1,13},{3,15... | collective-permute-start | bytes 337928 | tf_op jit(solution)/shard_map/ppermute | solution.py:280
  20.6 14.4 %collective-permute-start.6 = (bf16[440,128]{1,0:T(8,128)(2,1)S(1)}, bf16[440,128]{1,0:T(8,128)(2,1)S(1)}, u32[]{:S(2)}, u32[]{:S(2)}) collective-permute-start(bf16[440,128]{1,0:T(8,128)(2,1)S(1)} %slice.12), channel_id=1, source_target_pairs={{8,12},{10,14},{4,0},{6,2},{9,13},{11,15},{5,1},{7,3},{24,28},{26,... | collective-permute-start | bytes 337928 | tf_op jit(solution)/shard_map/ppermute | solution.py:347
  30.6 9.8 %collective-permute-start.9 = (bf16[880,128]{1,0:T(8,128)(2,1)S(1)}, bf16[880,128]{1,0:T(8,128)(2,1)S(1)}, u32[]{:S(2)}, u32[]{:S(2)}) collective-permute-start(bf16[880,128]{1,0:T(8,128)(2,1)S(1)} %get-tuple-element.38.refs_2_), channel_id=1, source_target_pairs={{0,1},{1,0},{2,3},{3,2},{4,5},{5,4},{6,7},{7,6},{8,9},{9,8},{10,11... | collective-permute-start | bytes 675848 | tf_op jit(solution)/shard_map/ppermute | solution.py:356
  33.2 7.2 %collective-permute-start.8 = (bf16[872,128]{1,0:T(8,128)(2,1)S(1)}, bf16[872,128]{1,0:T(8,128)(2,1)S(1)}, u32[]{:S(2)}, u32[]{:S(2)}) collective-permute-start(bf16[872,128]{1,0:T(8,128)(2,1)S(1)} %get-tuple-element.36.refs_0_), channel_id=1, source_target_pairs={{0,2},{2,0},{4,6},{6,4},{8,10},{10,8},{12,14},{14,12},{1,3},{3,1},... | collective-permute-start | bytes 669704 | tf_op jit(solution)/shard_map/ppermute | solution.py:280
  34.5 5.9 %collective-permute-start.12 = (bf16[880,128]{1,0:T(8,128)(2,1)S(1)}, bf16[880,128]{1,0:T(8,128)(2,1)S(1)}, u32[]{:S(2)}, u32[]{:S(2)}) collective-permute-start(bf16[880,128]{1,0:T(8,128)(2,1)S(1)} %collective-permute-done.5.refs_6_), channel_id=1, source_target_pairs={{0,1},{1,0},{2,3},{3,2},{4,5},{5,4},{6,7},{7,6},{8,9},{9,8},{10,11... | collective-permute-start | bytes 675848 | tf_op jit(solution)/shard_map/ppermute | solution.py:356
  34.8 5.6 %collective-permute-start.11 = (bf16[880,128]{1,0:T(8,128)(2,1)S(1)}, bf16[880,128]{1,0:T(8,128)(2,1)S(1)}, u32[]{:S(2)}, u32[]{:S(2)}) collective-permute-start(bf16[880,128]{1,0:T(8,128)(2,1)S(1)} %collective-permute-done.10.refs_4_), channel_id=1, source_target_pairs={{0,1},{1,0},{2,3},{3,2},{4,5},{5,4},{6,7},{7,6},{8,9},{9,8},{10,11... | collective-permute-start | bytes 675848 | tf_op jit(solution)/shard_map/ppermute | solution.py:356
  35.1 6.9 %collective-permute-start.7 = (bf16[880,128]{1,0:T(8,128)(2,1)S(1)}, bf16[880,128]{1,0:T(8,128)(2,1)S(1)}, u32[]{:S(2)}, u32[]{:S(2)}) collective-permute-start(bf16[880,128]{1,0:T(8,128)(2,1)S(1)} %join_far.1.refs_1_), channel_id=1, source_target_pairs={{0,1},{1,0},{2,3},{3,2},{4,5},{5,4},{6,7},{7,6},{8,9},{9,8},{10,11... | collective-permute-start | bytes 675848 | tf_op jit(solution)/shard_map/ppermute | solution.py:356
  42.6 10.8 %collective-permute-start.13 = (bf16[872,128]{1,0:T(8,128)(2,1)S(1)}, bf16[872,128]{1,0:T(8,128)(2,1)S(1)}, u32[]{:S(2)}, u32[]{:S(2)}) collective-permute-start(bf16[872,128]{1,0:T(8,128)(2,1)S(1)} %pairs.5), channel_id=1, source_target_pairs={{0,2},{2,0},{4,6},{6,4},{8,10},{10,8},{12,14},{14,12},{1,3},{3,1},... | collective-permute-start | bytes 669704 | tf_op jit(solution)/shard_map/ppermute | solution.py:280
  43.9 11.8 %collective-permute-start.16 = (bf16[872,128]{1,0:T(8,128)(2,1)S(1)}, bf16[872,128]{1,0:T(8,128)(2,1)S(1)}, u32[]{:S(2)}, u32[]{:S(2)}) collective-permute-start(bf16[872,128]{1,0:T(8,128)(2,1)S(1)} %pairs.5), channel_id=1, source_target_pairs={{0,18},{2,16},{4,22},{6,20},{8,26},{10,24},{12,30},{14,28},{16,2},... | collective-permute-start | bytes 669704 | tf_op jit(solution)/shard_map/ppermute | solution.py:399
  44.6 11.1 %collective-permute-start.15 = (bf16[96,1152]{1,0:T(8,128)(2,1)S(1)}, bf16[96,1152]{1,0:T(8,128)(2,1)S(1)}, u32[]{:S(2)}, u32[]{:S(2)}) collective-permute-start(bf16[96,1152]{1,0:T(8,128)(2,1)S(1)} %get-tuple-element.51), channel_id=1, source_target_pairs={{0,16},{16,0},{1,17},{17,1},{2,18},{18,2},{3,19},{19,3},{4,20},{20... | collective-permute-start | bytes 663560 | tf_op jit(solution)/shard_map/ppermute | solution.py:401
  53.7 4.3 %collective-permute-start.14 = (bf16[104,1152]{1,0:T(8,128)(2,1)S(1)}, bf16[104,1152]{1,0:T(8,128)(2,1)S(1)}, u32[]{:S(2)}, u32[]{:S(2)}) collective-permute-start(bf16[104,1152]{1,0:T(8,128)(2,1)S(1)} %get-tuple-element.50.own), channel_id=1, source_target_pairs={{0,1},{1,0},{2,3},{3,2},{4,5},{5,4},{6,7},{7,6},{8,9},{9,8},{10,11... | collective-permute-start | bytes 718856 | tf_op jit(solution)/shard_map/ppermute | solution.py:409
  55.9 2.0 %collective-permute-start.17 = (bf16[96,1152]{1,0:T(8,128)(2,1)S(1)}, bf16[96,1152]{1,0:T(8,128)(2,1)S(1)}, u32[]{:S(2)}, u32[]{:S(2)}) collective-permute-start(bf16[96,1152]{1,0:T(8,128)(2,1)S(1)} %other_demb.1.other), channel_id=1, source_target_pairs={{0,1},{1,0},{2,3},{3,2},{4,5},{5,4},{6,7},{7,6},{8,9},{9,8},{10,11... | collective-permute-start | bytes 663560 | tf_op jit(solution)/shard_map/ppermute | solution.py:417

commit v6 on v4

--- a/solution.py
+++ b/solution.py
@@ -16,6 +16,7 @@
 
 def local_call(
     kernel, name, outs, arrays, scratch=(), flops=0, transcendentals=0, held=(),
+    aliases=(),
 ):
     nbytes = sum(a.size * a.dtype.itemsize for a in (*arrays, *held))
     return pl.pallas_call(
@@ -30,6 +31,7 @@
             flops=flops, bytes_accessed=nbytes, transcendentals=transcendentals
         ),
         name=name,
+        input_output_aliases=dict(aliases),
     )(*arrays, *held)
 
 
@@ -38,44 +40,69 @@
     return [(start, size) for start in range(0, rows, size)]
 
 
-def embed_rows(which, image_pooled, text_pooled, image_proj, text_proj, out, before):
-    half = out.shape[1]
-    core = lax.axis_index("mp")
-    start = pl.multiple_of((core if which == 0 else 1 - core) * half, half)
-    rows = pl.ds(start, half)
-    for index, (pooled, proj) in enumerate(
-        ((image_pooled, image_proj), (text_pooled, text_proj))
-    ):
-        for copy in before[index]:
-            copy.wait()
-        out[index] = jnp.dot(pooled[rows, :], proj[...], preferred_element_type=F32).astype(
-            out.dtype
-        )
-
-
-def embed_sent_kernel(*refs):
-    sources, sent, held, sems = refs[:4], refs[4], refs[5:9], refs[9]
-    before = [[], []]
-    count = 0
-    for index in (0, 2, 1, 3):
-        source, target = sources[index], held[index]
+def own_first(image, text, own, body):
+    is_image = (lax.axis_index("sec") == 0) == own
+    pl.when(is_image)(lambda: body(*image))
+    pl.when(jnp.logical_not(is_image))(lambda: body(*text))
+
+
+def bring(sources, targets, sems):
+    copies = []
+    for source, target in zip(sources, targets):
         for start, size in cuts(source.shape[0]):
             rows = pl.ds(start, size)
-            copy = pltpu.make_async_copy(source.at[rows], target.at[rows], sems.at[count])
-            copy.start()
-            before[index % 2].append(copy)
-            count += 1
-    embed_rows(1, *held, sent, before)
-
-
-def embed_kept_kernel(*refs):
-    embed_rows(0, *refs[:4], refs[4], [[], []])
-
-
-def join_cores_kernel(kept, got, own_send, other_send):
-    section = lax.axis_index("sec")
-    own_send[...] = (kept[section] + got[section].astype(F32)).astype(BF16)
-    other_send[...] = (kept[1 - section] + got[1 - section].astype(F32)).astype(BF16)
+            sem = sems.at[len(copies)]
+            copies.append(pltpu.make_async_copy(source.at[rows], target.at[rows], sem))
+            copies[-1].start()
+    return copies
+
+
+def embed(pooled, proj, out, keep):
+    half = out.shape[0]
+    core = lax.axis_index("mp")
+    rows = pl.ds(pl.multiple_of((core if keep else 1 - core) * half, half), half)
+    out[...] = jnp.dot(pooled[rows, :], proj[...], preferred_element_type=F32).astype(out.dtype)
+
+
+def own_sent_kernel(
+    image_pooled, text_pooled, image_proj, text_proj,
+    sent, image_rows, text_rows, image_held, text_held, sems,
+):
+    def body(pooled, proj, rows, held):
+        for copy in bring((pooled, proj), (rows, held), sems):
+            copy.wait()
+        embed(rows, held, sent, False)
+
+    image = (image_pooled, image_proj, image_rows, image_held)
+    own_first(image, (text_pooled, text_proj, text_rows, text_held), True, body)
+
+
+def own_kept_kernel(image_rows, text_rows, image_held, text_held, kept):
+    own_first(
+        (image_rows, image_held),
+        (text_rows, text_held),
+        True,
+        lambda rows, held: embed(rows, held, kept, True),
+    )
+
+
+def other_embed_kernel(
+    image_rows_in, text_rows_in, image_held_in, text_held_in, _,
+    image_pooled, text_pooled, image_proj, text_proj,
+    sent, kept, image_held, text_held, image_rows, text_rows, sems,
+):
+    def body(pooled, proj, rows, held):
+        for copy in bring((pooled, proj), (rows, held), sems):
+            copy.wait()
+        embed(rows, held, sent, False)
+        embed(rows, held, kept, True)
+
+    image = (image_pooled, image_proj, image_rows, image_held)
+    own_first(image, (text_pooled, text_proj, text_rows, text_held), False, body)
+
+
+def join_cores_kernel(kept, got, send):
+    send[...] = (kept[...] + got[...].astype(F32)).astype(BF16)
 
 
 def write_block(block, value, extra):
@@ -122,9 +149,7 @@
         extra[...] = jnp.zeros_like(extra)
         extra[0:1, 0:half] = (half_ids >> 7).astype(F32)
         extra[1:2, 0:half] = (half_ids & 127).astype(F32)
-        section = lax.axis_index("sec")
-        section = section if own else 1 - section
-        emb = kept[section] + got[section].astype(F32) + summed[...].astype(F32)
+        emb = kept[...] + got[...].astype(F32) + summed[...].astype(F32)
         row_norm = jnp.sqrt(jnp.sum(emb * emb, axis=1, keepdims=True) + 1e-06)
         value = emb / row_norm
         unit[...] = value
@@ -160,12 +185,13 @@
             scale * lax.dot_general(own[...], visited[...], NT, preferred_element_type=F32)
             + params[1:2, 0:1]
         )
-        sign = jnp.where(ids == visit_ids[0:1, :], 1.0, -1.0).astype(F32)
-        value = -sign * scores
+        match = ids == visit_ids[0:1, :]
+        value = jnp.where(match, -scores, scores)
         small = jnp.exp(-jnp.abs(value))
-        losses = jnp.maximum(value, 0.0) + jnp.log1p(small)
-        sigmoid = jnp.where(value >= 0.0, 1.0, small) / (1.0 + small)
-        weight = (-scale * sign * sigmoid).astype(BF16)
+        total = 1.0 + small
+        losses = jnp.maximum(value, 0.0) + jnp.log(total)
+        sigmoid = jnp.where(value >= 0.0, 1.0, small) / total
+        weight = (jnp.where(match, -scale, scale) * sigmoid).astype(BF16)
         grad = jnp.dot(weight, visited[...], preferred_element_type=F32)
         loss = jnp.sum(losses, axis=1, keepdims=True)
         if not first:
@@ -268,43 +294,57 @@
         embed_flops = 2 * half * width * (image_proj.shape[0] + text_proj.shape[0])
 
         ids_row = ids[None, :]
-        copies = sum(len(cuts(t.shape[0])) for t in towers)
-        sent, *towers = local_call(
-            embed_sent_kernel,
-            "embed_sent",
-            [jax.ShapeDtypeStruct((2, half, width), BF16)]
-            + [jax.ShapeDtypeStruct(t.shape, t.dtype) for t in towers],
+        copies = max(
+            len(cuts(rows)) + len(cuts(proj.shape[0])) for proj in (image_proj, text_proj)
+        )
+        held = [pltpu.with_memory_space_constraint(t, pltpu.HBM) for t in towers]
+        own_sent, *towers = local_call(
+            own_sent_kernel,
+            "own_sent",
+            [whole_b16] + [jax.ShapeDtypeStruct(t.shape, t.dtype) for t in towers],
             [],
             scratch=[pltpu.SemaphoreType.DMA((copies,))],
+            flops=embed_flops // 2,
+            held=held,
+        )
+        own_got = lax.ppermute(own_sent, "mp", SWAP)
+        (own_kept,) = local_call(
+            own_kept_kernel, "own_kept", [whole_f32], towers, flops=embed_flops // 2
+        )
+        (own_send,) = local_call(join_cores_kernel, "own_send", [whole_b16], [own_kept, own_got])
+        other_summed = lax.ppermute(own_send, "sec", SWAP)
+        other_sent, other_kept, image_proj, text_proj = local_call(
+            other_embed_kernel,
+            "other_embed",
+            [whole_b16, whole_f32]
+            + [jax.ShapeDtypeStruct(t.shape, t.dtype) for t in towers[2:]],
+            [*towers, own_send],
+            scratch=[pltpu.VMEM(t.shape, t.dtype) for t in towers[:2]]
+            + [pltpu.SemaphoreType.DMA((copies,))],
             flops=embed_flops,
-            held=[pltpu.with_memory_space_constraint(t, pltpu.HBM) for t in towers],
-        )
-        image_proj, text_proj = towers[2:]
-        got = lax.ppermute(sent, "mp", SWAP)
-        (kept,) = local_call(
-            embed_kept_kernel,
-            "embed_kept",
-            [jax.ShapeDtypeStruct((2, half, width), F32)],
-            towers,
-            flops=embed_flops,
-        )
-        own_send, other_send = local_call(
-            join_cores_kernel, "join_cores", [whole_b16, whole_b16], [kept, got]
-        )
-        other_got = lax.ppermute(own_send, "sec", SWAP)
-        own_got = lax.ppermute(other_send, "sec", SWAP)
+            held=held,
+            aliases={2: 2, 3: 3},
+        )
+        other_got = lax.ppermute(other_sent, "mp", SWAP)
+        (other_send,) = local_call(
+            join_cores_kernel, "other_send", [whole_b16], [other_kept, other_got]
+        )
+        own_summed = lax.ppermute(other_send, "sec", SWAP)
+        (other_summed,) = local_call(
+            relay_kernel, "relay", [whole_b16], [other_summed], flops=10**9
+        )
         other_unit, visit, other_norm = local_call(
             unit_kernel(False),
             "other_unit",
             [whole_f32, block_b16, norm_shape],
-            [kept, got, other_got, ids_row],
+            [other_kept, other_got, other_summed, ids_row],
             scratch=[pltpu.VMEM((EXTRA, LANES), F32)],
         )
         own_unit, own_block, own_norm, params = local_call(
             unit_kernel(True),
             "own_unit",
             [whole_f32, block_b16, norm_shape, jax.ShapeDtypeStruct((2, LANES), F32)],
-            [kept, got, own_got, ids_row, multiplier, bias],
+            [own_kept, own_got, own_summed, ids_row, multiplier, bias],
             scratch=[pltpu.VMEM((EXTRA, LANES), F32)],
         )
 
@@ -366,7 +406,7 @@
             [grad_keep, near, own_unit, own_norm, loss_own],
             scratch=[pltpu.VMEM((half, width), BF16), pltpu.VMEM((EXTRA, LANES), F32)],
         )
-        own_got = lax.ppermute(own_demb, "mp", SWAP)
+        demb_got = lax.ppermute(own_demb, "mp", SWAP)
         (other_demb,) = local_call(
             other_demb_kernel,
             "other_demb",
@@ -374,7 +414,7 @@
             [across, diagonal, other_unit, other_norm],
             scratch=[pltpu.VMEM((half, width), BF16)],
         )
-        other_got = lax.ppermute(other_demb, "mp", SWAP)
+        other_demb_got = lax.ppermute(other_demb, "mp", SWAP)
         return local_call(
             grads_kernel,
             "grads",
@@ -383,7 +423,7 @@
                 jax.ShapeDtypeStruct((rows, image_proj.shape[0]), BF16),
                 jax.ShapeDtypeStruct((rows, text_proj.shape[0]), BF16),
             ],
-            [own_demb, own_got, other_demb, other_got, loss_mine, image_proj, text_proj],
+            [own_demb, demb_got, other_demb, other_demb_got, loss_mine, image_proj, text_proj],
             scratch=[pltpu.VMEM((2, rows, width), BF16)],
             flops=2 * embed_flops,
         )

time: 54.5 us -> 53.7 us (0.985)
  waiting for transfers between devices: 26.4 us -> 24.1 us
  Pallas kernels: 8.03 us -> 9.17 us
    ppermute x5 -> x6, waiting for transfers between devices: 9.53 us -> 7.21 us  [the longest x1 4.05 us: per_device(): other_summed = lax.ppermute(own_send, 'sec', SWAP)]
    pallas_call x12 -> x15, Pallas kernels: 8.03 us -> 9.17 us  [local_call(): pl.pallas_call(kernel, out_shape=outs, in_specs=[pl.BlockSpec(memory_spac...]
    ppermute x5 -> x6, starting transfers between devices: 3.13 us -> 3.61 us  [the longest x1 0.92 us: per_device(): other_demb_got = lax.ppermute(other_demb, 'mp', SWAP)]
  transfers between devices with their start and end apart: 16 -> 17, of which waited for: 6 -> 6; matrix products, arithmetic and copies ran while one was open for 0% -> 0% of each run, Pallas kernels for 6% -> 9%
where the time goes in v6:
time: 53.7 us; the launch traced here: 53.6 us
  waiting for transfers between devices  24.1 us (45%)
  starting transfers between devices  18.3 us (34%)
  Pallas kernels  9.17 us (17%)
  between operations  2.07 us (4%)
    ppermute x5, waiting for transfers between devices, across_blk(): return lax.ppermute(value, 'blk', [(i, i ^ step) for i in range(blocks)])  16.8 us
    pallas_call x15, Pallas kernels, local_call(): pl.pallas_call(kernel, out_shape=outs, in_specs=[pl.BlockSpec(memory_spac...  9.17 us
    ppermute x4, starting transfers between devices, per_device(): theirs = [lax.ppermute(v, 'mp', SWAP) for v in mine]  7.84 us
    ppermute x5, starting transfers between devices, across_blk(): return lax.ppermute(value, 'blk', [(i, i ^ step) for i in range(blocks)])  5.32 us
    ppermute x1, waiting for transfers between devices, per_device(): other_summed = lax.ppermute(own_send, 'sec', SWAP)  4.05 us
    ppermute x1, starting transfers between devices, per_device(): across = lax.ppermute(grad_own, 'sec', SWAP)  1.43 us
    ppermute x1, waiting for transfers between devices, per_device(): own_summed = lax.ppermute(other_send, 'sec', SWAP)  1.29 us
    ppermute x1, waiting for transfers between devices, per_device(): other_demb_got = lax.ppermute(other_demb, 'mp', SWAP)  1.1 us
  transfers between devices with their start and end apart: 17, of which 6 were waited for; matrix products, arithmetic and copies ran while one was open for 0% of the time, Pallas kernels for 9%

profile of v6, /device:TPU:19, one launch (start us, length us, event | category | flops | bytes accessed | tf_op | source)
XLA Modules:
  0.0 53.6 jit_solution(10465177140417133982)
XLA Ops:
  0.6 1.7 %own_sent.1 = (bf16[96,1152]{1,0:T(8,128)(2,1)S(1)}, bf16[192,384]{1,0:T(8,128)(2,1)S(1)}, bf16[192,512]{1,0:T(8,128)(2,1)S(1)}, bf16[384,1152]{1,0:T(8,128)(2,1)S(1)}, bf16[512,1152]{1,0:T(8,128)(2,1)S(1)}) custom-call(bf16[192,384]{1,0:T(8,128)(2,1)} %image_pooled.3, bf16[192,512]{1,0:T(8,128)(2,1)} %text_pooled.3, bf16[384,1152]{1,0:T(8,128)(2,1)} %image_proj.3, ...), custom_call_target="tpu_custom_call" | custom-call | flops 99090432 | bytes 2408448 | tf_op jit(solution)/shard_map/own_sent/pallas_call | solution.py:22
  2.4 0.7 %collective-permute-start = (bf16[96,1152]{1,0:T(8,128)(2,1)S(1)}, bf16[96,1152]{1,0:T(8,128)(2,1)S(1)}, u32[]{:S(2)}, u32[]{:S(2)}) collective-permute-start(bf16[96,1152]{1,0:T(8,128)(2,1)S(1)} %get-tuple-element.33), channel_id=1, source_target_pairs={{0,1},{1,0},{2,3},{3,2},{4,5},{5,4},{6,7},{7,6},{8,9},{9,8},{10,11... | collective-permute-start | bytes 663560 | tf_op jit(solution)/shard_map/ppermute | solution.py:310
  3.1 0.3 own_kept.1.kept
  3.5 0.8 %collective-permute-done.got = bf16[96,1152]{1,0:T(8,128)(2,1)S(1)} collective-permute-done((bf16[96,1152]{1,0:T(8,128)(2,1)S(1)}, bf16[96,1152]{1,0:T(8,128)(2,1)S(1)}, u32[]{:S(2)}, u32[]{:S(2)}) %collective-permute-start) | collective-permute-done | bytes 221216 | tf_op jit(solution)/shard_map/ppermute | solution.py:310
  4.3 0.2 collective-permute-start.3
  4.4 1.7 %other_embed.1 = (bf16[96,1152]{1,0:T(8,128)(2,1)S(1)}, f32[96,1152]{1,0:T(8,128)S(1)}, bf16[384,1152]{1,0:T(8,128)(2,1)S(1)}, bf16[512,1152]{1,0:T(8,128)(2,1)S(1)}) custom-call(bf16[192,384]{1,0:T(8,128)(2,1)S(1)} %get-tuple-element.29.image_rows.image_rows_in, ...), custom_call_target="tpu_custom_call", output_to_operand_aliasing={{2}: (2, {}), {3}: (3, {})} | custom-call | flops 198180864 | bytes 5038080 | tf_op jit(solution)/shard_map/other_embed/pallas_call | solution.py:22
  6.2 0.0 copy-start
  6.2 0.7 %collective-permute-start.1 = (bf16[96,1152]{1,0:T(8,128)(2,1)S(1)}, bf16[96,1152]{1,0:T(8,128)(2,1)S(1)}, u32[]{:S(2)}, u32[]{:S(2)}) collective-permute-start(bf16[96,1152]{1,0:T(8,128)(2,1)S(1)} %get-tuple-element.35), channel_id=1, source_target_pairs={{0,1},{1,0},{2,3},{3,2},{4,5},{5,4},{6,7},{7,6},{8,9},{9,8},{10,11... | collective-permute-start | bytes 663560 | tf_op jit(solution)/shard_map/ppermute | solution.py:328
  6.9 4.1 %collective-permute-done.3.block = bf16[96,1152]{1,0:T(8,128)(2,1)S(1)} collective-permute-done((bf16[96,1152]{1,0:T(8,128)(2,1)S(1)}, bf16[96,1152]{1,0:T(8,128)(2,1)S(1)}, u32[]{:S(2)}, u32[]{:S(2)}) %collective-permute-start.3) | collective-permute-done | bytes 221216 | tf_op jit(solution)/shard_map/ppermute | solution.py:315
  11.0 0.0 collective-permute-done.1.got
  11.0 0.0 copy-done
  11.0 0.2 other_unit.1
  11.2 0.1 collective-permute-start.10
  11.3 1.3 %collective-permute-start.8 = (bf16[872,128]{1,0:T(8,128)(2,1)S(1)}, bf16[872,128]{1,0:T(8,128)(2,1)S(1)}, u32[]{:S(2)}, u32[]{:S(2)}) collective-permute-start(bf16[872,128]{1,0:T(8,128)(2,1)S(1)} %get-tuple-element.38.refs_2_), channel_id=1, source_target_pairs={{0,4},{2,6},{4,0},{6,2},{8,12},{10,14},{12,8},{14,10},{1,5},{3,7},... | collective-permute-start | bytes 669704 | tf_op jit(solution)/shard_map/ppermute | solution.py:278
  12.7 1.3 %collective-permute-start.4 = (bf16[872,128]{1,0:T(8,128)(2,1)S(1)}, bf16[872,128]{1,0:T(8,128)(2,1)S(1)}, u32[]{:S(2)}, u32[]{:S(2)}) collective-permute-start(bf16[872,128]{1,0:T(8,128)(2,1)S(1)} %get-tuple-element.38.refs_2_), channel_id=1, source_target_pairs={{0,12},{2,14},{4,8},{6,10},{8,4},{10,6},{12,0},{14,2},{1,13},{3,15... | collective-permute-start | bytes 669704 | tf_op jit(solution)/shard_map/ppermute | solution.py:278
  13.9 0.1 other_send.1
  14.0 0.2 collective-permute-start.2
  15.5 2.4 %collective-permute-start.7 = (bf16[872,128]{1,0:T(8,128)(2,1)S(1)}, bf16[872,128]{1,0:T(8,128)(2,1)S(1)}, u32[]{:S(2)}, u32[]{:S(2)}) collective-permute-start(bf16[872,128]{1,0:T(8,128)(2,1)S(1)} %get-tuple-element.38.refs_2_), channel_id=1, source_target_pairs={{0,1},{1,0},{2,3},{3,2},{4,5},{5,4},{6,7},{7,6},{8,9},{9,8},{10,11... | collective-permute-start | bytes 669704 | tf_op jit(solution)/shard_map/ppermute | solution.py:356
  17.8 1.3 %collective-permute-done.2.summed = bf16[96,1152]{1,0:T(8,128)(2,1)S(1)} collective-permute-done((bf16[96,1152]{1,0:T(8,128)(2,1)S(1)}, bf16[96,1152]{1,0:T(8,128)(2,1)S(1)}, u32[]{:S(2)}, u32[]{:S(2)}) %collective-permute-start.2) | collective-permute-done | bytes 221216 | tf_op jit(solution)/shard_map/ppermute | solution.py:332
  19.1 0.2 own_unit.1
  19.4 1.3 %collective-permute-start.6 = (bf16[872,128]{1,0:T(8,128)(2,1)S(1)}, bf16[872,128]{1,0:T(8,128)(2,1)S(1)}, u32[]{:S(2)}, u32[]{:S(2)}) collective-permute-start(bf16[872,128]{1,0:T(8,128)(2,1)S(1)} %get-tuple-element.37.refs_0_), channel_id=1, source_target_pairs={{0,2},{2,0},{4,6},{6,4},{8,10},{10,8},{12,14},{14,12},{1,3},{3,1},... | collective-permute-start | bytes 669704 | tf_op jit(solution)/shard_map/ppermute | solution.py:278
  20.7 0.0 collective-permute-done.10.refs_6_
  20.7 3.6 %collective-permute-start.11 = (bf16[872,128]{1,0:T(8,128)(2,1)S(1)}, bf16[872,128]{1,0:T(8,128)(2,1)S(1)}, u32[]{:S(2)}, u32[]{:S(2)}) collective-permute-start(bf16[872,128]{1,0:T(8,128)(2,1)S(1)} %collective-permute-done.10.refs_6_), channel_id=1, source_target_pairs={{0,1},{1,0},{2,3},{3,2},{4,5},{5,4},{6,7},{7,6},{8,9},{9,8},{10,11... | collective-permute-start | bytes 669704 | tf_op jit(solution)/shard_map/ppermute | solution.py:356
  24.3 0.0 collective-permute-done.8.refs_4_
  24.3 1.3 %collective-permute-start.9 = (bf16[872,128]{1,0:T(8,128)(2,1)S(1)}, bf16[872,128]{1,0:T(8,128)(2,1)S(1)}, u32[]{:S(2)}, u32[]{:S(2)}) collective-permute-start(bf16[872,128]{1,0:T(8,128)(2,1)S(1)} %collective-permute-done.8.refs_4_), channel_id=1, source_target_pairs={{0,1},{1,0},{2,3},{3,2},{4,5},{5,4},{6,7},{7,6},{8,9},{9,8},{10,11... | collective-permute-start | bytes 669704 | tf_op jit(solution)/shard_map/ppermute | solution.py:356
  25.6 8.4 %collective-permute-done.4.block = bf16[872,128]{1,0:T(8,128)(2,1)S(1)} collective-permute-done((bf16[872,128]{1,0:T(8,128)(2,1)S(1)}, bf16[872,128]{1,0:T(8,128)(2,1)S(1)}, u32[]{:S(2)}, u32[]{:S(2)}) %collective-permute-start.4) | collective-permute-done | bytes 223264 | tf_op jit(solution)/shard_map/ppermute | solution.py:278
  33.9 0.6 %collective-permute-start.5 = (bf16[872,128]{1,0:T(8,128)(2,1)S(1)}, bf16[872,128]{1,0:T(8,128)(2,1)S(1)}, u32[]{:S(2)}, u32[]{:S(2)}) collective-permute-start(bf16[872,128]{1,0:T(8,128)(2,1)S(1)} %relay.3.refs_1_), channel_id=1, source_target_pairs={{0,1},{1,0},{2,3},{3,2},{4,5},{5,4},{6,7},{7,6},{8,9},{9,8},{10,11... | collective-permute-start | bytes 669704 | tf_op jit(solution)/shard_map/ppermute | solution.py:356
  34.5 0.0 collective-permute-done.7.refs_3_
  34.5 0.0 collective-permute-done.6.refs_1_.refs_0_
  34.5 0.0 collective-permute-done.11.refs_7_
  34.5 0.0 collective-permute-done.9.refs_5_
  34.5 1.4 %pairs.3 = (f32[192,1152]{1,0:T(8,128)S(1)}, f32[192,1]{1,0:T(8,128)S(1)}) custom-call(f32[2,128]{1,0:T(2,128)S(1)} %get-tuple-element.36.params, bf16[872,128]{1,0:T(8,128)(2,1)S(1)} %get-tuple-element.37.refs_0_, bf16[872,128]{1,0:T(8,128)(2,1)S(1)} %collective-permute-done.6.refs_1_.refs_0_, bf16[872,128]{1,0:T(8,128)(2,1)S(1)} %get-tuple-element.38.refs_2_, ...), custom_call_target="tpu_custom_call" | custom-call | flops 509607936 | bytes 1786880 | tf_op jit(solution)/shard_map/pairs/pallas_call | solution.py:22
  36.0 0.0 collective-permute-done.5.refs_2_
  36.0 0.7 %pairs.5 = bf16[872,128]{1,0:T(8,128)(2,1)S(1)} custom-call(f32[2,128]{1,0:T(2,128)S(1)} %get-tuple-element.36.params, bf16[872,128]{1,0:T(8,128)(2,1)S(1)} %collective-permute-done.6.refs_1_.refs_0_, bf16[872,128]{1,0:T(8,128)(2,1)S(1)} %relay.3.refs_1_, bf16[872,128]{1,0:T(8,128)(2,1)S(1)} %collective-permute-done.5.refs_2_, ...), custom_call_target="tpu_custom_call" | custom-call | flops 84934656 | bytes 1556224 | tf_op jit(solution)/shard_map/pairs/pallas_call | solution.py:22
  36.7 1.3 %collective-permute-start.12 = (bf16[872,128]{1,0:T(8,128)(2,1)S(1)}, bf16[872,128]{1,0:T(8,128)(2,1)S(1)}, u32[]{:S(2)}, u32[]{:S(2)}) collective-permute-start(bf16[872,128]{1,0:T(8,128)(2,1)S(1)} %pairs.5), channel_id=1, source_target_pairs={{0,2},{2,0},{4,6},{6,4},{8,10},{10,8},{12,14},{14,12},{1,3},{3,1},... | collective-permute-start | bytes 669704 | tf_op jit(solution)/shard_map/ppermute | solution.py:278
  38.0 0.0 collective-permute-start.15
  38.0 0.7 %pairs.4 = (f32[96,1152]{1,0:T(8,128)S(1)}, bf16[96,1152]{1,0:T(8,128)(2,1)S(1)}, f32[1,96]{1,0:T(1,128)S(1)}) custom-call(f32[2,128]{1,0:T(2,128)S(1)} %get-tuple-element.36.params, bf16[872,128]{1,0:T(8,128)(2,1)S(1)} %get-tuple-element.37.refs_0_, bf16[872,128]{1,0:T(8,128)(2,1)S(1)} %relay.3.refs_1_, ...), custom_call_target="tpu_custom_call" | custom-call | flops 84934656 | bytes 1556224 | tf_op jit(solution)/shard_map/pairs/pallas_call | solution.py:22
  38.7 1.4 %collective-permute-start.14 = (bf16[96,1152]{1,0:T(8,128)(2,1)S(1)}, bf16[96,1152]{1,0:T(8,128)(2,1)S(1)}, u32[]{:S(2)}, u32[]{:S(2)}) collective-permute-start(bf16[96,1152]{1,0:T(8,128)(2,1)S(1)} %get-tuple-element.49), channel_id=1, source_target_pairs={{0,16},{16,0},{1,17},{17,1},{2,18},{18,2},{3,19},{19,3},{4,20},{20... | collective-permute-start | bytes 663560 | tf_op jit(solution)/shard_map/ppermute | solution.py:401
  40.1 8.5 %collective-permute-done.12.near = bf16[872,128]{1,0:T(8,128)(2,1)S(1)} collective-permute-done((bf16[872,128]{1,0:T(8,128)(2,1)S(1)}, bf16[872,128]{1,0:T(8,128)(2,1)S(1)}, u32[]{:S(2)}, u32[]{:S(2)}) %collective-permute-start.12) | collective-permute-done | bytes 223264 | tf_op jit(solution)/shard_map/ppermute | solution.py:278
  48.6 0.2 own_demb.1
  48.8 0.9 %collective-permute-start.13 = (bf16[104,1152]{1,0:T(8,128)(2,1)S(1)}, bf16[104,1152]{1,0:T(8,128)(2,1)S(1)}, u32[]{:S(2)}, u32[]{:S(2)}) collective-permute-start(bf16[104,1152]{1,0:T(8,128)(2,1)S(1)} %get-tuple-element.48.own), channel_id=1, source_target_pairs={{0,1},{1,0},{2,3},{3,2},{4,5},{5,4},{6,7},{7,6},{8,9},{9,8},{10,11... | collective-permute-start | bytes 718856 | tf_op jit(solution)/shard_map/ppermute | solution.py:409
  49.7 0.0 collective-permute-done.14.across
  49.7 0.0 collective-permute-done.15.diagonal
  49.7 0.2 other_demb.1.other
  50.0 0.9 %collective-permute-start.16 = (bf16[96,1152]{1,0:T(8,128)(2,1)S(1)}, bf16[96,1152]{1,0:T(8,128)(2,1)S(1)}, u32[]{:S(2)}, u32[]{:S(2)}) collective-permute-start(bf16[96,1152]{1,0:T(8,128)(2,1)S(1)} %other_demb.1.other), channel_id=1, source_target_pairs={{0,1},{1,0},{2,3},{3,2},{4,5},{5,4},{6,7},{7,6},{8,9},{9,8},{10,11... | collective-permute-start | bytes 663560 | tf_op jit(solution)/shard_map/ppermute | solution.py:417
  50.9 1.1 %collective-permute-done.16.other_got = bf16[96,1152]{1,0:T(8,128)(2,1)S(1)} collective-permute-done((bf16[96,1152]{1,0:T(8,128)(2,1)S(1)}, bf16[96,1152]{1,0:T(8,128)(2,1)S(1)}, u32[]{:S(2)}, u32[]{:S(2)}) %collective-permute-start.16) | collective-permute-done | bytes 221216 | tf_op jit(solution)/shard_map/ppermute | solution.py:417
  52.0 0.0 collective-permute-done.13.own_got
  52.0 1.6 %grads.1 = (f32[1,192]{1,0:T(1,128)}, bf16[192,384]{1,0:T(8,128)(2,1)}, bf16[192,512]{1,0:T(8,128)(2,1)}) custom-call(bf16[104,1152]{1,0:T(8,128)(2,1)S(1)} %get-tuple-element.48.own, bf16[104,1152]{1,0:T(8,128)(2,1)S(1)} %collective-permute-done.13.own_got, bf16[96,1152]{1,0:T(8,128)(2,1)S(1)} %other_demb.1.other, ...), custom_call_target="tpu_custom_call" | custom-call | flops 396361728 | bytes 2986368 | tf_op jit(solution)/shard_map/grads/pallas_call | solution.py:22
  (3 shorter events, 0.1 us)
Async XLA Ops:
  2.4 1.9 %collective-permute-start = (bf16[96,1152]{1,0:T(8,128)(2,1)S(1)}, bf16[96,1152]{1,0:T(8,128)(2,1)S(1)}, u32[]{:S(2)}, u32[]{:S(2)}) collective-permute-start(bf16[96,1152]{1,0:T(8,128)(2,1)S(1)} %get-tuple-element.33), channel_id=1, source_target_pairs={{0,1},{1,0},{2,3},{3,2},{4,5},{5,4},{6,7},{7,6},{8,9},{9,8},{10,11... | collective-permute-start | bytes 663560 | tf_op jit(solution)/shard_map/ppermute | solution.py:310
  4.3 6.7 %collective-permute-start.3 = (bf16[96,1152]{1,0:T(8,128)(2,1)S(1)}, bf16[96,1152]{1,0:T(8,128)(2,1)S(1)}, u32[]{:S(2)}, u32[]{:S(2)}) collective-permute-start(bf16[96,1152]{1,0:T(8,128)(2,1)S(1)} %own_send.1._), channel_id=1, source_target_pairs={{0,16},{16,0},{1,17},{17,1},{2,18},{18,2},{3,19},{19,3},{4,20},{20... | collective-permute-start | bytes 663560 | tf_op jit(solution)/shard_map/ppermute | solution.py:315
  6.2 4.8 %copy-start = (s32[192]{0:T(256)S(1)}, s32[192]{0:T(256)}, u32[]{:S(2)}) copy-start(s32[192]{0:T(256)} %param.13) | copy-start | bytes 2308
  6.2 4.8 %collective-permute-start.1 = (bf16[96,1152]{1,0:T(8,128)(2,1)S(1)}, bf16[96,1152]{1,0:T(8,128)(2,1)S(1)}, u32[]{:S(2)}, u32[]{:S(2)}) collective-permute-start(bf16[96,1152]{1,0:T(8,128)(2,1)S(1)} %get-tuple-element.35), channel_id=1, source_target_pairs={{0,1},{1,0},{2,3},{3,2},{4,5},{5,4},{6,7},{7,6},{8,9},{9,8},{10,11... | collective-permute-start | bytes 663560 | tf_op jit(solution)/shard_map/ppermute | solution.py:328
  11.2 9.4 %collective-permute-start.10 = (bf16[872,128]{1,0:T(8,128)(2,1)S(1)}, bf16[872,128]{1,0:T(8,128)(2,1)S(1)}, u32[]{:S(2)}, u32[]{:S(2)}) collective-permute-start(bf16[872,128]{1,0:T(8,128)(2,1)S(1)} %get-tuple-element.38.refs_2_), channel_id=1, source_target_pairs={{0,8},{2,10},{4,12},{6,14},{8,0},{10,2},{12,4},{14,6},{1,9},{3,11}... | collective-permute-start | bytes 669704 | tf_op jit(solution)/shard_map/ppermute | solution.py:278
  11.3 12.9 %collective-permute-start.8 = (bf16[872,128]{1,0:T(8,128)(2,1)S(1)}, bf16[872,128]{1,0:T(8,128)(2,1)S(1)}, u32[]{:S(2)}, u32[]{:S(2)}) collective-permute-start(bf16[872,128]{1,0:T(8,128)(2,1)S(1)} %get-tuple-element.38.refs_2_), channel_id=1, source_target_pairs={{0,4},{2,6},{4,0},{6,2},{8,12},{10,14},{12,8},{14,10},{1,5},{3,7},... | collective-permute-start | bytes 669704 | tf_op jit(solution)/shard_map/ppermute | solution.py:278
  12.7 21.3 %collective-permute-start.4 = (bf16[872,128]{1,0:T(8,128)(2,1)S(1)}, bf16[872,128]{1,0:T(8,128)(2,1)S(1)}, u32[]{:S(2)}, u32[]{:S(2)}) collective-permute-start(bf16[872,128]{1,0:T(8,128)(2,1)S(1)} %get-tuple-element.38.refs_2_), channel_id=1, source_target_pairs={{0,12},{2,14},{4,8},{6,10},{8,4},{10,6},{12,0},{14,2},{1,13},{3,15... | collective-permute-start | bytes 669704 | tf_op jit(solution)/shard_map/ppermute | solution.py:278
  14.0 5.1 %collective-permute-start.2 = (bf16[96,1152]{1,0:T(8,128)(2,1)S(1)}, bf16[96,1152]{1,0:T(8,128)(2,1)S(1)}, u32[]{:S(2)}, u32[]{:S(2)}) collective-permute-start(bf16[96,1152]{1,0:T(8,128)(2,1)S(1)} %other_send.1), channel_id=1, source_target_pairs={{0,16},{16,0},{1,17},{17,1},{2,18},{18,2},{3,19},{19,3},{4,20},{20... | collective-permute-start | bytes 663560 | tf_op jit(solution)/shard_map/ppermute | solution.py:332
  15.5 19.1 %collective-permute-start.7 = (bf16[872,128]{1,0:T(8,128)(2,1)S(1)}, bf16[872,128]{1,0:T(8,128)(2,1)S(1)}, u32[]{:S(2)}, u32[]{:S(2)}) collective-permute-start(bf16[872,128]{1,0:T(8,128)(2,1)S(1)} %get-tuple-element.38.refs_2_), channel_id=1, source_target_pairs={{0,1},{1,0},{2,3},{3,2},{4,5},{5,4},{6,7},{7,6},{8,9},{9,8},{10,11... | collective-permute-start | bytes 669704 | tf_op jit(solution)/shard_map/ppermute | solution.py:356
  19.4 15.2 %collective-permute-start.6 = (bf16[872,128]{1,0:T(8,128)(2,1)S(1)}, bf16[872,128]{1,0:T(8,128)(2,1)S(1)}, u32[]{:S(2)}, u32[]{:S(2)}) collective-permute-start(bf16[872,128]{1,0:T(8,128)(2,1)S(1)} %get-tuple-element.37.refs_0_), channel_id=1, source_target_pairs={{0,2},{2,0},{4,6},{6,4},{8,10},{10,8},{12,14},{14,12},{1,3},{3,1},... | collective-permute-start | bytes 669704 | tf_op jit(solution)/shard_map/ppermute | solution.py:278
  20.7 13.9 %collective-permute-start.11 = (bf16[872,128]{1,0:T(8,128)(2,1)S(1)}, bf16[872,128]{1,0:T(8,128)(2,1)S(1)}, u32[]{:S(2)}, u32[]{:S(2)}) collective-permute-start(bf16[872,128]{1,0:T(8,128)(2,1)S(1)} %collective-permute-done.10.refs_6_), channel_id=1, source_target_pairs={{0,1},{1,0},{2,3},{3,2},{4,5},{5,4},{6,7},{7,6},{8,9},{9,8},{10,11... | collective-permute-start | bytes 669704 | tf_op jit(solution)/shard_map/ppermute | solution.py:356
  24.3 10.2 %collective-permute-start.9 = (bf16[872,128]{1,0:T(8,128)(2,1)S(1)}, bf16[872,128]{1,0:T(8,128)(2,1)S(1)}, u32[]{:S(2)}, u32[]{:S(2)}) collective-permute-start(bf16[872,128]{1,0:T(8,128)(2,1)S(1)} %collective-permute-done.8.refs_4_), channel_id=1, source_target_pairs={{0,1},{1,0},{2,3},{3,2},{4,5},{5,4},{6,7},{7,6},{8,9},{9,8},{10,11... | collective-permute-start | bytes 669704 | tf_op jit(solution)/shard_map/ppermute | solution.py:356
  33.9 2.0 %collective-permute-start.5 = (bf16[872,128]{1,0:T(8,128)(2,1)S(1)}, bf16[872,128]{1,0:T(8,128)(2,1)S(1)}, u32[]{:S(2)}, u32[]{:S(2)}) collective-permute-start(bf16[872,128]{1,0:T(8,128)(2,1)S(1)} %relay.3.refs_1_), channel_id=1, source_target_pairs={{0,1},{1,0},{2,3},{3,2},{4,5},{5,4},{6,7},{7,6},{8,9},{9,8},{10,11... | collective-permute-start | bytes 669704 | tf_op jit(solution)/shard_map/ppermute | solution.py:356
  36.7 11.9 %collective-permute-start.12 = (bf16[872,128]{1,0:T(8,128)(2,1)S(1)}, bf16[872,128]{1,0:T(8,128)(2,1)S(1)}, u32[]{:S(2)}, u32[]{:S(2)}) collective-permute-start(bf16[872,128]{1,0:T(8,128)(2,1)S(1)} %pairs.5), channel_id=1, source_target_pairs={{0,2},{2,0},{4,6},{6,4},{8,10},{10,8},{12,14},{14,12},{1,3},{3,1},... | collective-permute-start | bytes 669704 | tf_op jit(solution)/shard_map/ppermute | solution.py:278
  38.0 11.8 %collective-permute-start.15 = (bf16[872,128]{1,0:T(8,128)(2,1)S(1)}, bf16[872,128]{1,0:T(8,128)(2,1)S(1)}, u32[]{:S(2)}, u32[]{:S(2)}) collective-permute-start(bf16[872,128]{1,0:T(8,128)(2,1)S(1)} %pairs.5), channel_id=1, source_target_pairs={{0,18},{2,16},{4,22},{6,20},{8,26},{10,24},{12,30},{14,28},{16,2},... | collective-permute-start | bytes 669704 | tf_op jit(solution)/shard_map/ppermute | solution.py:399
  38.7 11.0 %collective-permute-start.14 = (bf16[96,1152]{1,0:T(8,128)(2,1)S(1)}, bf16[96,1152]{1,0:T(8,128)(2,1)S(1)}, u32[]{:S(2)}, u32[]{:S(2)}) collective-permute-start(bf16[96,1152]{1,0:T(8,128)(2,1)S(1)} %get-tuple-element.49), channel_id=1, source_target_pairs={{0,16},{16,0},{1,17},{17,1},{2,18},{18,2},{3,19},{19,3},{4,20},{20... | collective-permute-start | bytes 663560 | tf_op jit(solution)/shard_map/ppermute | solution.py:401
  48.8 3.2 %collective-permute-start.13 = (bf16[104,1152]{1,0:T(8,128)(2,1)S(1)}, bf16[104,1152]{1,0:T(8,128)(2,1)S(1)}, u32[]{:S(2)}, u32[]{:S(2)}) collective-permute-start(bf16[104,1152]{1,0:T(8,128)(2,1)S(1)} %get-tuple-element.48.own), channel_id=1, source_target_pairs={{0,1},{1,0},{2,3},{3,2},{4,5},{5,4},{6,7},{7,6},{8,9},{9,8},{10,11... | collective-permute-start | bytes 718856 | tf_op jit(solution)/shard_map/ppermute | solution.py:409
  50.0 2.0 %collective-permute-start.16 = (bf16[96,1152]{1,0:T(8,128)(2,1)S(1)}, bf16[96,1152]{1,0:T(8,128)(2,1)S(1)}, u32[]{:S(2)}, u32[]{:S(2)}) collective-permute-start(bf16[96,1152]{1,0:T(8,128)(2,1)S(1)} %other_demb.1.other), channel_id=1, source_target_pairs={{0,1},{1,0},{2,3},{3,2},{4,5},{5,4},{6,7},{7,6},{8,9},{9,8},{10,11... | collective-permute-start | bytes 663560 | tf_op jit(solution)/shard_map/ppermute | solution.py:417

commit v7 on v6

--- a/solution.py
+++ b/solution.py
@@ -238,36 +238,38 @@
     out[...] = finish(across[...].astype(F32) + joined[...].astype(F32), unit, norm)
 
 
-def grads_kernel(
-    own, own_got, other, other_got, loss_mine, image_proj, text_proj,
-    pair_loss, image_grad, text_grad, joined,
-):
-    half = joined.shape[1] // 2
+def tower_grad(mine, theirs, proj, joined):
+    half = joined.shape[0] // 2
     core = lax.axis_index("mp")
-
-    def tower(index, mine, theirs, proj, grad):
-        mine, theirs = mine[pl.ds(0, half), :], theirs[pl.ds(0, half), :]
-        joined[index, pl.ds(0, half), :] = jnp.where(core == 0, mine, theirs)
-        joined[index, pl.ds(half, half), :] = jnp.where(core == 0, theirs, mine)
-        grad[...] = lax.dot_general(
-            joined[index], proj[...], NT, preferred_element_type=F32
-        ).astype(BF16)
-
-    @pl.when(lax.axis_index("sec") == 0)
-    def _():
-        tower(0, own, own_got, image_proj, image_grad)
-        tower(1, other, other_got, text_proj, text_grad)
-
-    @pl.when(lax.axis_index("sec") != 0)
-    def _():
-        tower(1, own, own_got, text_proj, text_grad)
-        tower(0, other, other_got, image_proj, image_grad)
-
-    parts = own_got[pl.ds(half, EXTRA), pl.ds(0, LANES)].astype(F32)
+    mine, theirs = mine[pl.ds(0, half), :], theirs[pl.ds(0, half), :]
+    joined[pl.ds(0, half), :] = jnp.where(core == 0, mine, theirs)
+    joined[pl.ds(half, half), :] = jnp.where(core == 0, theirs, mine)
+    return lax.dot_general(
+        joined[...], proj[...], NT, preferred_element_type=F32
+    ).astype(BF16)
+
+
+def own_grad_kernel(mine, theirs, loss_mine, image_proj, text_proj, pair_loss, grad, joined):
+    def body(proj):
+        grad[:, pl.ds(0, proj.shape[0])] = tower_grad(mine, theirs, proj, joined)
+
+    own_first((image_proj,), (text_proj,), True, body)
+    half = joined.shape[0] // 2
+    core = lax.axis_index("mp")
+    parts = theirs[pl.ds(half, EXTRA), pl.ds(0, LANES)].astype(F32)
     loss = loss_mine[...]
     loss_theirs = (parts[0:1] + parts[1:2] + parts[2:3])[:, :half]
     pair_loss[0:1, 0:half] = jnp.where(core == 0, loss, loss_theirs)
     pair_loss[0:1, half : 2 * half] = jnp.where(core == 0, loss_theirs, loss)
+
+
+def grads_kernel(own_grad, mine, theirs, image_proj, text_proj, image_grad, text_grad, joined):
+    def body(proj, grad, proj_own, grad_own):
+        grad_own[...] = own_grad[:, pl.ds(0, proj_own.shape[0])]
+        grad[...] = tower_grad(mine, theirs, proj, joined)
+
+    image, text = (image_proj, image_grad), (text_proj, text_grad)
+    own_first((*image, *text), (*text, *image), False, body)
 
 
 def make_per_device(mesh):
@@ -415,18 +417,27 @@
             scratch=[pltpu.VMEM((half, width), BF16)],
         )
         other_demb_got = lax.ppermute(other_demb, "mp", SWAP)
-        return local_call(
+        features = (image_proj.shape[0], text_proj.shape[0])
+        pair_loss, own_grad = local_call(
+            own_grad_kernel,
+            "own_grad",
+            [
+                jax.ShapeDtypeStruct((1, rows), F32),
+                jax.ShapeDtypeStruct((rows, max(features)), BF16),
+            ],
+            [own_demb, demb_got, loss_mine, image_proj, text_proj],
+            scratch=[pltpu.VMEM((rows, width), BF16)],
+            flops=embed_flops,
+        )
+        image_grad, text_grad = local_call(
             grads_kernel,
             "grads",
-            [
-                jax.ShapeDtypeStruct((1, rows), F32),
-                jax.ShapeDtypeStruct((rows, image_proj.shape[0]), BF16),
-                jax.ShapeDtypeStruct((rows, text_proj.shape[0]), BF16),
-            ],
-            [own_demb, demb_got, other_demb, other_demb_got, loss_mine, image_proj, text_proj],
-            scratch=[pltpu.VMEM((2, rows, width), BF16)],
-            flops=2 * embed_flops,
-        )
+            [jax.ShapeDtypeStruct((rows, count), BF16) for count in features],
+            [own_grad, other_demb, other_demb_got, image_proj, text_proj],
+            scratch=[pltpu.VMEM((rows, width), BF16)],
+            flops=embed_flops,
+        )
+        return (pair_loss, image_grad, text_grad)
 
     return per_device
 

time: 53.7 us -> 53.5 us (level)
  waiting for transfers between devices: 24.1 us -> 23 us
  Pallas kernels: 9.17 us -> 10 us
    ppermute x1, waiting for transfers between devices: 1.1 us -> 0.01 us  [per_device(): other_demb_got = lax.ppermute(other_demb, 'mp', SWAP)]
    pallas_call x15 -> x16, Pallas kernels: 9.17 us -> 10 us  [local_call(): pl.pallas_call(kernel, out_shape=outs, in_specs=[pl.BlockSpec(memory_spac...]
  transfers between devices with their start and end apart: 17 -> 17, of which waited for: 6 -> 5; matrix products, arithmetic and copies ran while one was open for 0% -> 0% of each run, Pallas kernels for 9% -> 12%
where the time goes in v7:
time: 53.5 us; the launch traced here: 53.3 us
  waiting for transfers between devices  23 us (43%)
  starting transfers between devices  18.3 us (34%)
  Pallas kernels  10 us (19%)
  between operations  2.07 us (4%)
    ppermute x5, waiting for transfers between devices, across_blk(): return lax.ppermute(value, 'blk', [(i, i ^ step) for i in range(blocks)])  16.8 us
    pallas_call x16, Pallas kernels, local_call(): pl.pallas_call(kernel, out_shape=outs, in_specs=[pl.BlockSpec(memory_spac...  10 us
    ppermute x4, starting transfers between devices, per_device(): theirs = [lax.ppermute(v, 'mp', SWAP) for v in mine]  7.84 us
    ppermute x5, starting transfers between devices, across_blk(): return lax.ppermute(value, 'blk', [(i, i ^ step) for i in range(blocks)])  5.32 us
    ppermute x1, waiting for transfers between devices, per_device(): other_summed = lax.ppermute(own_send, 'sec', SWAP)  4.05 us
    ppermute x1, starting transfers between devices, per_device(): across = lax.ppermute(grad_own, 'sec', SWAP)  1.43 us
    ppermute x1, waiting for transfers between devices, per_device(): own_summed = lax.ppermute(other_send, 'sec', SWAP)  1.29 us
  transfers between devices with their start and end apart: 17, of which 5 were waited for; matrix products, arithmetic and copies ran while one was open for 0% of the time, Pallas kernels for 12%

profile of v7, /device:TPU:19, one launch (start us, length us, event | category | flops | bytes accessed | tf_op | source)
XLA Modules:
  0.0 53.3 jit_solution(746581793438671495)
XLA Ops:
  0.6 1.7 %own_sent.1 = (bf16[96,1152]{1,0:T(8,128)(2,1)S(1)}, bf16[192,384]{1,0:T(8,128)(2,1)S(1)}, bf16[192,512]{1,0:T(8,128)(2,1)S(1)}, bf16[384,1152]{1,0:T(8,128)(2,1)S(1)}, bf16[512,1152]{1,0:T(8,128)(2,1)S(1)}) custom-call(bf16[192,384]{1,0:T(8,128)(2,1)} %image_pooled.3, bf16[192,512]{1,0:T(8,128)(2,1)} %text_pooled.3, bf16[384,1152]{1,0:T(8,128)(2,1)} %image_proj.3, ...), custom_call_target="tpu_custom_call" | custom-call | flops 99090432 | bytes 2408448 | tf_op jit(solution)/shard_map/own_sent/pallas_call | solution.py:22
  2.4 0.7 %collective-permute-start = (bf16[96,1152]{1,0:T(8,128)(2,1)S(1)}, bf16[96,1152]{1,0:T(8,128)(2,1)S(1)}, u32[]{:S(2)}, u32[]{:S(2)}) collective-permute-start(bf16[96,1152]{1,0:T(8,128)(2,1)S(1)} %get-tuple-element.37), channel_id=1, source_target_pairs={{0,1},{1,0},{2,3},{3,2},{4,5},{5,4},{6,7},{7,6},{8,9},{9,8},{10,11... | collective-permute-start | bytes 663560 | tf_op jit(solution)/shard_map/ppermute | solution.py:312
  3.1 0.3 own_kept.1.kept
  3.5 0.8 %collective-permute-done.got = bf16[96,1152]{1,0:T(8,128)(2,1)S(1)} collective-permute-done((bf16[96,1152]{1,0:T(8,128)(2,1)S(1)}, bf16[96,1152]{1,0:T(8,128)(2,1)S(1)}, u32[]{:S(2)}, u32[]{:S(2)}) %collective-permute-start) | collective-permute-done | bytes 221216 | tf_op jit(solution)/shard_map/ppermute | solution.py:312
  4.3 0.2 collective-permute-start.3
  4.4 1.7 %other_embed.1 = (bf16[96,1152]{1,0:T(8,128)(2,1)S(1)}, f32[96,1152]{1,0:T(8,128)S(1)}, bf16[384,1152]{1,0:T(8,128)(2,1)S(1)}, bf16[512,1152]{1,0:T(8,128)(2,1)S(1)}) custom-call(bf16[192,384]{1,0:T(8,128)(2,1)S(1)} %get-tuple-element.33.image_rows.image_rows_in, ...), custom_call_target="tpu_custom_call", output_to_operand_aliasing={{2}: (2, {}), {3}: (3, {})} | custom-call | flops 198180864 | bytes 5038080 | tf_op jit(solution)/shard_map/other_embed/pallas_call | solution.py:22
  6.2 0.0 copy-start
  6.2 0.7 %collective-permute-start.1 = (bf16[96,1152]{1,0:T(8,128)(2,1)S(1)}, bf16[96,1152]{1,0:T(8,128)(2,1)S(1)}, u32[]{:S(2)}, u32[]{:S(2)}) collective-permute-start(bf16[96,1152]{1,0:T(8,128)(2,1)S(1)} %get-tuple-element.39), channel_id=1, source_target_pairs={{0,1},{1,0},{2,3},{3,2},{4,5},{5,4},{6,7},{7,6},{8,9},{9,8},{10,11... | collective-permute-start | bytes 663560 | tf_op jit(solution)/shard_map/ppermute | solution.py:330
  6.9 4.1 %collective-permute-done.3.block = bf16[96,1152]{1,0:T(8,128)(2,1)S(1)} collective-permute-done((bf16[96,1152]{1,0:T(8,128)(2,1)S(1)}, bf16[96,1152]{1,0:T(8,128)(2,1)S(1)}, u32[]{:S(2)}, u32[]{:S(2)}) %collective-permute-start.3) | collective-permute-done | bytes 221216 | tf_op jit(solution)/shard_map/ppermute | solution.py:317
  11.0 0.0 collective-permute-done.1.got
  11.0 0.2 other_unit.1
  11.2 0.1 collective-permute-start.10
  11.3 1.3 %collective-permute-start.8 = (bf16[872,128]{1,0:T(8,128)(2,1)S(1)}, bf16[872,128]{1,0:T(8,128)(2,1)S(1)}, u32[]{:S(2)}, u32[]{:S(2)}) collective-permute-start(bf16[872,128]{1,0:T(8,128)(2,1)S(1)} %get-tuple-element.42.refs_2_), channel_id=1, source_target_pairs={{0,4},{2,6},{4,0},{6,2},{8,12},{10,14},{12,8},{14,10},{1,5},{3,7},... | collective-permute-start | bytes 669704 | tf_op jit(solution)/shard_map/ppermute | solution.py:280
  12.7 1.3 %collective-permute-start.4 = (bf16[872,128]{1,0:T(8,128)(2,1)S(1)}, bf16[872,128]{1,0:T(8,128)(2,1)S(1)}, u32[]{:S(2)}, u32[]{:S(2)}) collective-permute-start(bf16[872,128]{1,0:T(8,128)(2,1)S(1)} %get-tuple-element.42.refs_2_), channel_id=1, source_target_pairs={{0,12},{2,14},{4,8},{6,10},{8,4},{10,6},{12,0},{14,2},{1,13},{3,15... | collective-permute-start | bytes 669704 | tf_op jit(solution)/shard_map/ppermute | solution.py:280
  13.9 0.1 other_send.1
  14.0 0.2 collective-permute-start.2
  15.5 2.4 %collective-permute-start.7 = (bf16[872,128]{1,0:T(8,128)(2,1)S(1)}, bf16[872,128]{1,0:T(8,128)(2,1)S(1)}, u32[]{:S(2)}, u32[]{:S(2)}) collective-permute-start(bf16[872,128]{1,0:T(8,128)(2,1)S(1)} %get-tuple-element.42.refs_2_), channel_id=1, source_target_pairs={{0,1},{1,0},{2,3},{3,2},{4,5},{5,4},{6,7},{7,6},{8,9},{9,8},{10,11... | collective-permute-start | bytes 669704 | tf_op jit(solution)/shard_map/ppermute | solution.py:358
  17.8 1.3 %collective-permute-done.2.summed = bf16[96,1152]{1,0:T(8,128)(2,1)S(1)} collective-permute-done((bf16[96,1152]{1,0:T(8,128)(2,1)S(1)}, bf16[96,1152]{1,0:T(8,128)(2,1)S(1)}, u32[]{:S(2)}, u32[]{:S(2)}) %collective-permute-start.2) | collective-permute-done | bytes 221216 | tf_op jit(solution)/shard_map/ppermute | solution.py:334
  19.1 0.2 own_unit.1
  19.4 1.3 %collective-permute-start.6 = (bf16[872,128]{1,0:T(8,128)(2,1)S(1)}, bf16[872,128]{1,0:T(8,128)(2,1)S(1)}, u32[]{:S(2)}, u32[]{:S(2)}) collective-permute-start(bf16[872,128]{1,0:T(8,128)(2,1)S(1)} %get-tuple-element.41.refs_0_), channel_id=1, source_target_pairs={{0,2},{2,0},{4,6},{6,4},{8,10},{10,8},{12,14},{14,12},{1,3},{3,1},... | collective-permute-start | bytes 669704 | tf_op jit(solution)/shard_map/ppermute | solution.py:280
  20.7 0.0 collective-permute-done.10.refs_6_
  20.7 3.6 %collective-permute-start.11 = (bf16[872,128]{1,0:T(8,128)(2,1)S(1)}, bf16[872,128]{1,0:T(8,128)(2,1)S(1)}, u32[]{:S(2)}, u32[]{:S(2)}) collective-permute-start(bf16[872,128]{1,0:T(8,128)(2,1)S(1)} %collective-permute-done.10.refs_6_), channel_id=1, source_target_pairs={{0,1},{1,0},{2,3},{3,2},{4,5},{5,4},{6,7},{7,6},{8,9},{9,8},{10,11... | collective-permute-start | bytes 669704 | tf_op jit(solution)/shard_map/ppermute | solution.py:358
  24.3 0.0 collective-permute-done.8.refs_4_
  24.3 1.3 %collective-permute-start.9 = (bf16[872,128]{1,0:T(8,128)(2,1)S(1)}, bf16[872,128]{1,0:T(8,128)(2,1)S(1)}, u32[]{:S(2)}, u32[]{:S(2)}) collective-permute-start(bf16[872,128]{1,0:T(8,128)(2,1)S(1)} %collective-permute-done.8.refs_4_), channel_id=1, source_target_pairs={{0,1},{1,0},{2,3},{3,2},{4,5},{5,4},{6,7},{7,6},{8,9},{9,8},{10,11... | collective-permute-start | bytes 669704 | tf_op jit(solution)/shard_map/ppermute | solution.py:358
  25.6 8.4 %collective-permute-done.4.block = bf16[872,128]{1,0:T(8,128)(2,1)S(1)} collective-permute-done((bf16[872,128]{1,0:T(8,128)(2,1)S(1)}, bf16[872,128]{1,0:T(8,128)(2,1)S(1)}, u32[]{:S(2)}, u32[]{:S(2)}) %collective-permute-start.4) | collective-permute-done | bytes 223264 | tf_op jit(solution)/shard_map/ppermute | solution.py:280
  33.9 0.6 %collective-permute-start.5 = (bf16[872,128]{1,0:T(8,128)(2,1)S(1)}, bf16[872,128]{1,0:T(8,128)(2,1)S(1)}, u32[]{:S(2)}, u32[]{:S(2)}) collective-permute-start(bf16[872,128]{1,0:T(8,128)(2,1)S(1)} %relay.3.refs_1_), channel_id=1, source_target_pairs={{0,1},{1,0},{2,3},{3,2},{4,5},{5,4},{6,7},{7,6},{8,9},{9,8},{10,11... | collective-permute-start | bytes 669704 | tf_op jit(solution)/shard_map/ppermute | solution.py:358
  34.5 0.0 collective-permute-done.7.refs_3_
  34.5 0.0 collective-permute-done.6.refs_1_.refs_0_
  34.5 0.0 collective-permute-done.11.refs_7_
  34.5 0.0 collective-permute-done.9.refs_5_
  34.5 1.4 %pairs.3 = (f32[192,1152]{1,0:T(8,128)S(1)}, f32[192,1]{1,0:T(8,128)S(1)}) custom-call(f32[2,128]{1,0:T(2,128)S(1)} %get-tuple-element.40.params, bf16[872,128]{1,0:T(8,128)(2,1)S(1)} %get-tuple-element.41.refs_0_, bf16[872,128]{1,0:T(8,128)(2,1)S(1)} %collective-permute-done.6.refs_1_.refs_0_, bf16[872,128]{1,0:T(8,128)(2,1)S(1)} %get-tuple-element.42.refs_2_, ...), custom_call_target="tpu_custom_call" | custom-call | flops 509607936 | bytes 1786880 | tf_op jit(solution)/shard_map/pairs/pallas_call | solution.py:22
  36.0 0.0 collective-permute-done.5.refs_2_
  36.0 0.7 %pairs.5 = bf16[872,128]{1,0:T(8,128)(2,1)S(1)} custom-call(f32[2,128]{1,0:T(2,128)S(1)} %get-tuple-element.40.params, bf16[872,128]{1,0:T(8,128)(2,1)S(1)} %collective-permute-done.6.refs_1_.refs_0_, bf16[872,128]{1,0:T(8,128)(2,1)S(1)} %relay.3.refs_1_, bf16[872,128]{1,0:T(8,128)(2,1)S(1)} %collective-permute-done.5.refs_2_, ...), custom_call_target="tpu_custom_call" | custom-call | flops 84934656 | bytes 1556224 | tf_op jit(solution)/shard_map/pairs/pallas_call | solution.py:22
  36.7 1.3 %collective-permute-start.12 = (bf16[872,128]{1,0:T(8,128)(2,1)S(1)}, bf16[872,128]{1,0:T(8,128)(2,1)S(1)}, u32[]{:S(2)}, u32[]{:S(2)}) collective-permute-start(bf16[872,128]{1,0:T(8,128)(2,1)S(1)} %pairs.5), channel_id=1, source_target_pairs={{0,2},{2,0},{4,6},{6,4},{8,10},{10,8},{12,14},{14,12},{1,3},{3,1},... | collective-permute-start | bytes 669704 | tf_op jit(solution)/shard_map/ppermute | solution.py:280
  38.0 0.1 collective-permute-start.15
  38.0 0.7 %pairs.4 = (f32[96,1152]{1,0:T(8,128)S(1)}, bf16[96,1152]{1,0:T(8,128)(2,1)S(1)}, f32[1,96]{1,0:T(1,128)S(1)}) custom-call(f32[2,128]{1,0:T(2,128)S(1)} %get-tuple-element.40.params, bf16[872,128]{1,0:T(8,128)(2,1)S(1)} %get-tuple-element.41.refs_0_, bf16[872,128]{1,0:T(8,128)(2,1)S(1)} %relay.3.refs_1_, ...), custom_call_target="tpu_custom_call" | custom-call | flops 84934656 | bytes 1556224 | tf_op jit(solution)/shard_map/pairs/pallas_call | solution.py:22
  38.7 1.4 %collective-permute-start.14 = (bf16[96,1152]{1,0:T(8,128)(2,1)S(1)}, bf16[96,1152]{1,0:T(8,128)(2,1)S(1)}, u32[]{:S(2)}, u32[]{:S(2)}) collective-permute-start(bf16[96,1152]{1,0:T(8,128)(2,1)S(1)} %get-tuple-element.58), channel_id=1, source_target_pairs={{0,16},{16,0},{1,17},{17,1},{2,18},{18,2},{3,19},{19,3},{4,20},{20... | collective-permute-start | bytes 663560 | tf_op jit(solution)/shard_map/ppermute | solution.py:403
  40.1 8.5 %collective-permute-done.12.near = bf16[872,128]{1,0:T(8,128)(2,1)S(1)} collective-permute-done((bf16[872,128]{1,0:T(8,128)(2,1)S(1)}, bf16[872,128]{1,0:T(8,128)(2,1)S(1)}, u32[]{:S(2)}, u32[]{:S(2)}) %collective-permute-start.12) | collective-permute-done | bytes 223264 | tf_op jit(solution)/shard_map/ppermute | solution.py:280
  48.6 0.2 own_demb.1
  48.8 0.9 %collective-permute-start.13 = (bf16[104,1152]{1,0:T(8,128)(2,1)S(1)}, bf16[104,1152]{1,0:T(8,128)(2,1)S(1)}, u32[]{:S(2)}, u32[]{:S(2)}) collective-permute-start(bf16[104,1152]{1,0:T(8,128)(2,1)S(1)} %get-tuple-element.52.mine), channel_id=1, source_target_pairs={{0,1},{1,0},{2,3},{3,2},{4,5},{5,4},{6,7},{7,6},{8,9},{9,8},{10,11... | collective-permute-start | bytes 718856 | tf_op jit(solution)/shard_map/ppermute | solution.py:411
  49.7 0.0 collective-permute-done.14.across
  49.7 0.0 collective-permute-done.15.diagonal
  49.7 0.2 other_demb.1.mine
  50.0 0.9 %collective-permute-start.16 = (bf16[96,1152]{1,0:T(8,128)(2,1)S(1)}, bf16[96,1152]{1,0:T(8,128)(2,1)S(1)}, u32[]{:S(2)}, u32[]{:S(2)}) collective-permute-start(bf16[96,1152]{1,0:T(8,128)(2,1)S(1)} %other_demb.1.mine), channel_id=1, source_target_pairs={{0,1},{1,0},{2,3},{3,2},{4,5},{5,4},{6,7},{7,6},{8,9},{9,8},{10,11... | collective-permute-start | bytes 663560 | tf_op jit(solution)/shard_map/ppermute | solution.py:419
  50.9 0.0 collective-permute-done.13.theirs
  50.9 1.2 %own_grad.1 = (f32[1,192]{1,0:T(1,128)}, bf16[192,512]{1,0:T(8,128)(2,1)S(1)}) custom-call(bf16[104,1152]{1,0:T(8,128)(2,1)S(1)} %get-tuple-element.52.mine, bf16[104,1152]{1,0:T(8,128)(2,1)S(1)} %collective-permute-done.13.theirs, f32[1,96]{1,0:T(1,128)S(1)} %get-tuple-element.53.loss_mine, bf16[384,1152]{1,0:T(8,128)(2,1)S(1)} %get-tuple-element.54.image_proj, ...), custom_call_target="tpu_custom_call" | custom-call | flops 198180864 | bytes 2544000 | tf_op jit(solution)/shard_map/own_grad/pallas_call | solution.py:22
  52.1 0.0 collective-permute-done.16.theirs
  52.1 1.2 %grads.1 = (bf16[192,384]{1,0:T(8,128)(2,1)}, bf16[192,512]{1,0:T(8,128)(2,1)}) custom-call(bf16[192,512]{1,0:T(8,128)(2,1)S(1)} %get-tuple-element.57.own_grad, bf16[96,1152]{1,0:T(8,128)(2,1)S(1)} %other_demb.1.mine, bf16[96,1152]{1,0:T(8,128)(2,1)S(1)} %collective-permute-done.16.theirs, bf16[384,1152]{1,0:T(8,128)(2,1)S(1)} %get-tuple-element.54.image_proj, ...), custom_call_target="tpu_custom_call" | custom-call | flops 198180864 | bytes 2703360 | tf_op jit(solution)/shard_map/grads/pallas_call | solution.py:22
  (4 shorter events, 0.1 us)
Async XLA Ops:
  2.4 1.9 %collective-permute-start = (bf16[96,1152]{1,0:T(8,128)(2,1)S(1)}, bf16[96,1152]{1,0:T(8,128)(2,1)S(1)}, u32[]{:S(2)}, u32[]{:S(2)}) collective-permute-start(bf16[96,1152]{1,0:T(8,128)(2,1)S(1)} %get-tuple-element.37), channel_id=1, source_target_pairs={{0,1},{1,0},{2,3},{3,2},{4,5},{5,4},{6,7},{7,6},{8,9},{9,8},{10,11... | collective-permute-start | bytes 663560 | tf_op jit(solution)/shard_map/ppermute | solution.py:312
  4.3 6.7 %collective-permute-start.3 = (bf16[96,1152]{1,0:T(8,128)(2,1)S(1)}, bf16[96,1152]{1,0:T(8,128)(2,1)S(1)}, u32[]{:S(2)}, u32[]{:S(2)}) collective-permute-start(bf16[96,1152]{1,0:T(8,128)(2,1)S(1)} %own_send.1._), channel_id=1, source_target_pairs={{0,16},{16,0},{1,17},{17,1},{2,18},{18,2},{3,19},{19,3},{4,20},{20... | collective-permute-start | bytes 663560 | tf_op jit(solution)/shard_map/ppermute | solution.py:317
  6.2 4.8 %copy-start = (s32[192]{0:T(256)S(1)}, s32[192]{0:T(256)}, u32[]{:S(2)}) copy-start(s32[192]{0:T(256)} %param.13) | copy-start | bytes 2308
  6.2 4.8 %collective-permute-start.1 = (bf16[96,1152]{1,0:T(8,128)(2,1)S(1)}, bf16[96,1152]{1,0:T(8,128)(2,1)S(1)}, u32[]{:S(2)}, u32[]{:S(2)}) collective-permute-start(bf16[96,1152]{1,0:T(8,128)(2,1)S(1)} %get-tuple-element.39), channel_id=1, source_target_pairs={{0,1},{1,0},{2,3},{3,2},{4,5},{5,4},{6,7},{7,6},{8,9},{9,8},{10,11... | collective-permute-start | bytes 663560 | tf_op jit(solution)/shard_map/ppermute | solution.py:330
  11.2 9.4 %collective-permute-start.10 = (bf16[872,128]{1,0:T(8,128)(2,1)S(1)}, bf16[872,128]{1,0:T(8,128)(2,1)S(1)}, u32[]{:S(2)}, u32[]{:S(2)}) collective-permute-start(bf16[872,128]{1,0:T(8,128)(2,1)S(1)} %get-tuple-element.42.refs_2_), channel_id=1, source_target_pairs={{0,8},{2,10},{4,12},{6,14},{8,0},{10,2},{12,4},{14,6},{1,9},{3,11}... | collective-permute-start | bytes 669704 | tf_op jit(solution)/shard_map/ppermute | solution.py:280
  11.3 12.9 %collective-permute-start.8 = (bf16[872,128]{1,0:T(8,128)(2,1)S(1)}, bf16[872,128]{1,0:T(8,128)(2,1)S(1)}, u32[]{:S(2)}, u32[]{:S(2)}) collective-permute-start(bf16[872,128]{1,0:T(8,128)(2,1)S(1)} %get-tuple-element.42.refs_2_), channel_id=1, source_target_pairs={{0,4},{2,6},{4,0},{6,2},{8,12},{10,14},{12,8},{14,10},{1,5},{3,7},... | collective-permute-start | bytes 669704 | tf_op jit(solution)/shard_map/ppermute | solution.py:280
  12.7 21.3 %collective-permute-start.4 = (bf16[872,128]{1,0:T(8,128)(2,1)S(1)}, bf16[872,128]{1,0:T(8,128)(2,1)S(1)}, u32[]{:S(2)}, u32[]{:S(2)}) collective-permute-start(bf16[872,128]{1,0:T(8,128)(2,1)S(1)} %get-tuple-element.42.refs_2_), channel_id=1, source_target_pairs={{0,12},{2,14},{4,8},{6,10},{8,4},{10,6},{12,0},{14,2},{1,13},{3,15... | collective-permute-start | bytes 669704 | tf_op jit(solution)/shard_map/ppermute | solution.py:280
  14.0 5.1 %collective-permute-start.2 = (bf16[96,1152]{1,0:T(8,128)(2,1)S(1)}, bf16[96,1152]{1,0:T(8,128)(2,1)S(1)}, u32[]{:S(2)}, u32[]{:S(2)}) collective-permute-start(bf16[96,1152]{1,0:T(8,128)(2,1)S(1)} %other_send.1), channel_id=1, source_target_pairs={{0,16},{16,0},{1,17},{17,1},{2,18},{18,2},{3,19},{19,3},{4,20},{20... | collective-permute-start | bytes 663560 | tf_op jit(solution)/shard_map/ppermute | solution.py:334
  15.5 19.1 %collective-permute-start.7 = (bf16[872,128]{1,0:T(8,128)(2,1)S(1)}, bf16[872,128]{1,0:T(8,128)(2,1)S(1)}, u32[]{:S(2)}, u32[]{:S(2)}) collective-permute-start(bf16[872,128]{1,0:T(8,128)(2,1)S(1)} %get-tuple-element.42.refs_2_), channel_id=1, source_target_pairs={{0,1},{1,0},{2,3},{3,2},{4,5},{5,4},{6,7},{7,6},{8,9},{9,8},{10,11... | collective-permute-start | bytes 669704 | tf_op jit(solution)/shard_map/ppermute | solution.py:358
  19.4 15.2 %collective-permute-start.6 = (bf16[872,128]{1,0:T(8,128)(2,1)S(1)}, bf16[872,128]{1,0:T(8,128)(2,1)S(1)}, u32[]{:S(2)}, u32[]{:S(2)}) collective-permute-start(bf16[872,128]{1,0:T(8,128)(2,1)S(1)} %get-tuple-element.41.refs_0_), channel_id=1, source_target_pairs={{0,2},{2,0},{4,6},{6,4},{8,10},{10,8},{12,14},{14,12},{1,3},{3,1},... | collective-permute-start | bytes 669704 | tf_op jit(solution)/shard_map/ppermute | solution.py:280
  20.7 13.9 %collective-permute-start.11 = (bf16[872,128]{1,0:T(8,128)(2,1)S(1)}, bf16[872,128]{1,0:T(8,128)(2,1)S(1)}, u32[]{:S(2)}, u32[]{:S(2)}) collective-permute-start(bf16[872,128]{1,0:T(8,128)(2,1)S(1)} %collective-permute-done.10.refs_6_), channel_id=1, source_target_pairs={{0,1},{1,0},{2,3},{3,2},{4,5},{5,4},{6,7},{7,6},{8,9},{9,8},{10,11... | collective-permute-start | bytes 669704 | tf_op jit(solution)/shard_map/ppermute | solution.py:358
  24.3 10.2 %collective-permute-start.9 = (bf16[872,128]{1,0:T(8,128)(2,1)S(1)}, bf16[872,128]{1,0:T(8,128)(2,1)S(1)}, u32[]{:S(2)}, u32[]{:S(2)}) collective-permute-start(bf16[872,128]{1,0:T(8,128)(2,1)S(1)} %collective-permute-done.8.refs_4_), channel_id=1, source_target_pairs={{0,1},{1,0},{2,3},{3,2},{4,5},{5,4},{6,7},{7,6},{8,9},{9,8},{10,11... | collective-permute-start | bytes 669704 | tf_op jit(solution)/shard_map/ppermute | solution.py:358
  33.9 2.0 %collective-permute-start.5 = (bf16[872,128]{1,0:T(8,128)(2,1)S(1)}, bf16[872,128]{1,0:T(8,128)(2,1)S(1)}, u32[]{:S(2)}, u32[]{:S(2)}) collective-permute-start(bf16[872,128]{1,0:T(8,128)(2,1)S(1)} %relay.3.refs_1_), channel_id=1, source_target_pairs={{0,1},{1,0},{2,3},{3,2},{4,5},{5,4},{6,7},{7,6},{8,9},{9,8},{10,11... | collective-permute-start | bytes 669704 | tf_op jit(solution)/shard_map/ppermute | solution.py:358
  36.7 11.9 %collective-permute-start.12 = (bf16[872,128]{1,0:T(8,128)(2,1)S(1)}, bf16[872,128]{1,0:T(8,128)(2,1)S(1)}, u32[]{:S(2)}, u32[]{:S(2)}) collective-permute-start(bf16[872,128]{1,0:T(8,128)(2,1)S(1)} %pairs.5), channel_id=1, source_target_pairs={{0,2},{2,0},{4,6},{6,4},{8,10},{10,8},{12,14},{14,12},{1,3},{3,1},... | collective-permute-start | bytes 669704 | tf_op jit(solution)/shard_map/ppermute | solution.py:280
  38.0 11.8 %collective-permute-start.15 = (bf16[872,128]{1,0:T(8,128)(2,1)S(1)}, bf16[872,128]{1,0:T(8,128)(2,1)S(1)}, u32[]{:S(2)}, u32[]{:S(2)}) collective-permute-start(bf16[872,128]{1,0:T(8,128)(2,1)S(1)} %pairs.5), channel_id=1, source_target_pairs={{0,18},{2,16},{4,22},{6,20},{8,26},{10,24},{12,30},{14,28},{16,2},... | collective-permute-start | bytes 669704 | tf_op jit(solution)/shard_map/ppermute | solution.py:401
  38.7 11.0 %collective-permute-start.14 = (bf16[96,1152]{1,0:T(8,128)(2,1)S(1)}, bf16[96,1152]{1,0:T(8,128)(2,1)S(1)}, u32[]{:S(2)}, u32[]{:S(2)}) collective-permute-start(bf16[96,1152]{1,0:T(8,128)(2,1)S(1)} %get-tuple-element.58), channel_id=1, source_target_pairs={{0,16},{16,0},{1,17},{17,1},{2,18},{18,2},{3,19},{19,3},{4,20},{20... | collective-permute-start | bytes 663560 | tf_op jit(solution)/shard_map/ppermute | solution.py:403
  48.8 2.1 %collective-permute-start.13 = (bf16[104,1152]{1,0:T(8,128)(2,1)S(1)}, bf16[104,1152]{1,0:T(8,128)(2,1)S(1)}, u32[]{:S(2)}, u32[]{:S(2)}) collective-permute-start(bf16[104,1152]{1,0:T(8,128)(2,1)S(1)} %get-tuple-element.52.mine), channel_id=1, source_target_pairs={{0,1},{1,0},{2,3},{3,2},{4,5},{5,4},{6,7},{7,6},{8,9},{9,8},{10,11... | collective-permute-start | bytes 718856 | tf_op jit(solution)/shard_map/ppermute | solution.py:411
  50.0 2.1 %collective-permute-start.16 = (bf16[96,1152]{1,0:T(8,128)(2,1)S(1)}, bf16[96,1152]{1,0:T(8,128)(2,1)S(1)}, u32[]{:S(2)}, u32[]{:S(2)}) collective-permute-start(bf16[96,1152]{1,0:T(8,128)(2,1)S(1)} %other_demb.1.mine), channel_id=1, source_target_pairs={{0,1},{1,0},{2,3},{3,2},{4,5},{5,4},{6,7},{7,6},{8,9},{9,8},{10,11... | collective-permute-start | bytes 663560 | tf_op jit(solution)/shard_map/ppermute | solution.py:419

commit v8 on v7

--- a/solution.py
+++ b/solution.py
@@ -190,7 +190,7 @@
         small = jnp.exp(-jnp.abs(value))
         total = 1.0 + small
         losses = jnp.maximum(value, 0.0) + jnp.log(total)
-        sigmoid = jnp.where(value >= 0.0, 1.0, small) / total
+        sigmoid = jnp.where(value >= 0.0, 1.0, small) * pl.reciprocal(total)
         weight = (jnp.where(match, -scale, scale) * sigmoid).astype(BF16)
         grad = jnp.dot(weight, visited[...], preferred_element_type=F32)
         loss = jnp.sum(losses, axis=1, keepdims=True)

time: 53.5 us -> 53.5 us (level)
  no operation moved by 1% of the time
where the time goes in v8:
time: 53.5 us; the launch traced here: 53.3 us
  waiting for transfers between devices  23 us (43%)
  starting transfers between devices  18.3 us (34%)
  Pallas kernels  10 us (19%)
  between operations  2.07 us (4%)
    ppermute x5, waiting for transfers between devices, across_blk(): return lax.ppermute(value, 'blk', [(i, i ^ step) for i in range(blocks)])  16.8 us
    pallas_call x16, Pallas kernels, local_call(): pl.pallas_call(kernel, out_shape=outs, in_specs=[pl.BlockSpec(memory_spac...  10 us
    ppermute x4, starting transfers between devices, per_device(): theirs = [lax.ppermute(v, 'mp', SWAP) for v in mine]  7.84 us
    ppermute x5, starting transfers between devices, across_blk(): return lax.ppermute(value, 'blk', [(i, i ^ step) for i in range(blocks)])  5.32 us
    ppermute x1, waiting for transfers between devices, per_device(): other_summed = lax.ppermute(own_send, 'sec', SWAP)  4.05 us
    ppermute x1, starting transfers between devices, per_device(): across = lax.ppermute(grad_own, 'sec', SWAP)  1.43 us
    ppermute x1, waiting for transfers between devices, per_device(): own_summed = lax.ppermute(other_send, 'sec', SWAP)  1.29 us
  transfers between devices with their start and end apart: 17, of which 5 were waited for; matrix products, arithmetic and copies ran while one was open for 0% of the time, Pallas kernels for 12%

profile of v8, /device:TPU:19, one launch (start us, length us, event | category | flops | bytes accessed | tf_op | source)
XLA Modules:
  0.0 53.3 jit_solution(746581793438671495)
XLA Ops:
  0.6 1.7 %own_sent.1 = (bf16[96,1152]{1,0:T(8,128)(2,1)S(1)}, bf16[192,384]{1,0:T(8,128)(2,1)S(1)}, bf16[192,512]{1,0:T(8,128)(2,1)S(1)}, bf16[384,1152]{1,0:T(8,128)(2,1)S(1)}, bf16[512,1152]{1,0:T(8,128)(2,1)S(1)}) custom-call(bf16[192,384]{1,0:T(8,128)(2,1)} %image_pooled.3, bf16[192,512]{1,0:T(8,128)(2,1)} %text_pooled.3, bf16[384,1152]{1,0:T(8,128)(2,1)} %image_proj.3, ...), custom_call_target="tpu_custom_call" | custom-call | flops 99090432 | bytes 2408448 | tf_op jit(solution)/shard_map/own_sent/pallas_call | solution.py:22
  2.4 0.7 %collective-permute-start = (bf16[96,1152]{1,0:T(8,128)(2,1)S(1)}, bf16[96,1152]{1,0:T(8,128)(2,1)S(1)}, u32[]{:S(2)}, u32[]{:S(2)}) collective-permute-start(bf16[96,1152]{1,0:T(8,128)(2,1)S(1)} %get-tuple-element.37), channel_id=1, source_target_pairs={{0,1},{1,0},{2,3},{3,2},{4,5},{5,4},{6,7},{7,6},{8,9},{9,8},{10,11... | collective-permute-start | bytes 663560 | tf_op jit(solution)/shard_map/ppermute | solution.py:312
  3.1 0.3 own_kept.1.kept
  3.5 0.8 %collective-permute-done.got = bf16[96,1152]{1,0:T(8,128)(2,1)S(1)} collective-permute-done((bf16[96,1152]{1,0:T(8,128)(2,1)S(1)}, bf16[96,1152]{1,0:T(8,128)(2,1)S(1)}, u32[]{:S(2)}, u32[]{:S(2)}) %collective-permute-start) | collective-permute-done | bytes 221216 | tf_op jit(solution)/shard_map/ppermute | solution.py:312
  4.3 0.2 collective-permute-start.3
  4.4 1.7 %other_embed.1 = (bf16[96,1152]{1,0:T(8,128)(2,1)S(1)}, f32[96,1152]{1,0:T(8,128)S(1)}, bf16[384,1152]{1,0:T(8,128)(2,1)S(1)}, bf16[512,1152]{1,0:T(8,128)(2,1)S(1)}) custom-call(bf16[192,384]{1,0:T(8,128)(2,1)S(1)} %get-tuple-element.33.image_rows.image_rows_in, ...), custom_call_target="tpu_custom_call", output_to_operand_aliasing={{2}: (2, {}), {3}: (3, {})} | custom-call | flops 198180864 | bytes 5038080 | tf_op jit(solution)/shard_map/other_embed/pallas_call | solution.py:22
  6.2 0.0 copy-start
  6.2 0.7 %collective-permute-start.1 = (bf16[96,1152]{1,0:T(8,128)(2,1)S(1)}, bf16[96,1152]{1,0:T(8,128)(2,1)S(1)}, u32[]{:S(2)}, u32[]{:S(2)}) collective-permute-start(bf16[96,1152]{1,0:T(8,128)(2,1)S(1)} %get-tuple-element.39), channel_id=1, source_target_pairs={{0,1},{1,0},{2,3},{3,2},{4,5},{5,4},{6,7},{7,6},{8,9},{9,8},{10,11... | collective-permute-start | bytes 663560 | tf_op jit(solution)/shard_map/ppermute | solution.py:330
  6.9 4.1 %collective-permute-done.3.block = bf16[96,1152]{1,0:T(8,128)(2,1)S(1)} collective-permute-done((bf16[96,1152]{1,0:T(8,128)(2,1)S(1)}, bf16[96,1152]{1,0:T(8,128)(2,1)S(1)}, u32[]{:S(2)}, u32[]{:S(2)}) %collective-permute-start.3) | collective-permute-done | bytes 221216 | tf_op jit(solution)/shard_map/ppermute | solution.py:317
  11.0 0.0 collective-permute-done.1.got
  11.0 0.2 other_unit.1
  11.2 0.1 collective-permute-start.10
  11.3 1.3 %collective-permute-start.8 = (bf16[872,128]{1,0:T(8,128)(2,1)S(1)}, bf16[872,128]{1,0:T(8,128)(2,1)S(1)}, u32[]{:S(2)}, u32[]{:S(2)}) collective-permute-start(bf16[872,128]{1,0:T(8,128)(2,1)S(1)} %get-tuple-element.42.refs_2_), channel_id=1, source_target_pairs={{0,4},{2,6},{4,0},{6,2},{8,12},{10,14},{12,8},{14,10},{1,5},{3,7},... | collective-permute-start | bytes 669704 | tf_op jit(solution)/shard_map/ppermute | solution.py:280
  12.7 1.3 %collective-permute-start.4 = (bf16[872,128]{1,0:T(8,128)(2,1)S(1)}, bf16[872,128]{1,0:T(8,128)(2,1)S(1)}, u32[]{:S(2)}, u32[]{:S(2)}) collective-permute-start(bf16[872,128]{1,0:T(8,128)(2,1)S(1)} %get-tuple-element.42.refs_2_), channel_id=1, source_target_pairs={{0,12},{2,14},{4,8},{6,10},{8,4},{10,6},{12,0},{14,2},{1,13},{3,15... | collective-permute-start | bytes 669704 | tf_op jit(solution)/shard_map/ppermute | solution.py:280
  13.9 0.1 other_send.1
  14.0 0.2 collective-permute-start.2
  15.5 2.4 %collective-permute-start.7 = (bf16[872,128]{1,0:T(8,128)(2,1)S(1)}, bf16[872,128]{1,0:T(8,128)(2,1)S(1)}, u32[]{:S(2)}, u32[]{:S(2)}) collective-permute-start(bf16[872,128]{1,0:T(8,128)(2,1)S(1)} %get-tuple-element.42.refs_2_), channel_id=1, source_target_pairs={{0,1},{1,0},{2,3},{3,2},{4,5},{5,4},{6,7},{7,6},{8,9},{9,8},{10,11... | collective-permute-start | bytes 669704 | tf_op jit(solution)/shard_map/ppermute | solution.py:358
  17.8 1.3 %collective-permute-done.2.summed = bf16[96,1152]{1,0:T(8,128)(2,1)S(1)} collective-permute-done((bf16[96,1152]{1,0:T(8,128)(2,1)S(1)}, bf16[96,1152]{1,0:T(8,128)(2,1)S(1)}, u32[]{:S(2)}, u32[]{:S(2)}) %collective-permute-start.2) | collective-permute-done | bytes 221216 | tf_op jit(solution)/shard_map/ppermute | solution.py:334
  19.1 0.2 own_unit.1
  19.4 1.3 %collective-permute-start.6 = (bf16[872,128]{1,0:T(8,128)(2,1)S(1)}, bf16[872,128]{1,0:T(8,128)(2,1)S(1)}, u32[]{:S(2)}, u32[]{:S(2)}) collective-permute-start(bf16[872,128]{1,0:T(8,128)(2,1)S(1)} %get-tuple-element.41.refs_0_), channel_id=1, source_target_pairs={{0,2},{2,0},{4,6},{6,4},{8,10},{10,8},{12,14},{14,12},{1,3},{3,1},... | collective-permute-start | bytes 669704 | tf_op jit(solution)/shard_map/ppermute | solution.py:280
  20.7 0.0 collective-permute-done.10.refs_6_
  20.7 3.6 %collective-permute-start.11 = (bf16[872,128]{1,0:T(8,128)(2,1)S(1)}, bf16[872,128]{1,0:T(8,128)(2,1)S(1)}, u32[]{:S(2)}, u32[]{:S(2)}) collective-permute-start(bf16[872,128]{1,0:T(8,128)(2,1)S(1)} %collective-permute-done.10.refs_6_), channel_id=1, source_target_pairs={{0,1},{1,0},{2,3},{3,2},{4,5},{5,4},{6,7},{7,6},{8,9},{9,8},{10,11... | collective-permute-start | bytes 669704 | tf_op jit(solution)/shard_map/ppermute | solution.py:358
  24.3 0.0 collective-permute-done.8.refs_4_
  24.3 1.3 %collective-permute-start.9 = (bf16[872,128]{1,0:T(8,128)(2,1)S(1)}, bf16[872,128]{1,0:T(8,128)(2,1)S(1)}, u32[]{:S(2)}, u32[]{:S(2)}) collective-permute-start(bf16[872,128]{1,0:T(8,128)(2,1)S(1)} %collective-permute-done.8.refs_4_), channel_id=1, source_target_pairs={{0,1},{1,0},{2,3},{3,2},{4,5},{5,4},{6,7},{7,6},{8,9},{9,8},{10,11... | collective-permute-start | bytes 669704 | tf_op jit(solution)/shard_map/ppermute | solution.py:358
  25.6 8.4 %collective-permute-done.4.block = bf16[872,128]{1,0:T(8,128)(2,1)S(1)} collective-permute-done((bf16[872,128]{1,0:T(8,128)(2,1)S(1)}, bf16[872,128]{1,0:T(8,128)(2,1)S(1)}, u32[]{:S(2)}, u32[]{:S(2)}) %collective-permute-start.4) | collective-permute-done | bytes 223264 | tf_op jit(solution)/shard_map/ppermute | solution.py:280
  33.9 0.6 %collective-permute-start.5 = (bf16[872,128]{1,0:T(8,128)(2,1)S(1)}, bf16[872,128]{1,0:T(8,128)(2,1)S(1)}, u32[]{:S(2)}, u32[]{:S(2)}) collective-permute-start(bf16[872,128]{1,0:T(8,128)(2,1)S(1)} %relay.3.refs_1_), channel_id=1, source_target_pairs={{0,1},{1,0},{2,3},{3,2},{4,5},{5,4},{6,7},{7,6},{8,9},{9,8},{10,11... | collective-permute-start | bytes 669704 | tf_op jit(solution)/shard_map/ppermute | solution.py:358
  34.5 0.0 collective-permute-done.7.refs_3_
  34.5 0.0 collective-permute-done.6.refs_1_.refs_0_
  34.5 0.0 collective-permute-done.11.refs_7_
  34.5 0.0 collective-permute-done.9.refs_5_
  34.5 1.4 %pairs.3 = (f32[192,1152]{1,0:T(8,128)S(1)}, f32[192,1]{1,0:T(8,128)S(1)}) custom-call(f32[2,128]{1,0:T(2,128)S(1)} %get-tuple-element.40.params, bf16[872,128]{1,0:T(8,128)(2,1)S(1)} %get-tuple-element.41.refs_0_, bf16[872,128]{1,0:T(8,128)(2,1)S(1)} %collective-permute-done.6.refs_1_.refs_0_, bf16[872,128]{1,0:T(8,128)(2,1)S(1)} %get-tuple-element.42.refs_2_, ...), custom_call_target="tpu_custom_call" | custom-call | flops 509607936 | bytes 1786880 | tf_op jit(solution)/shard_map/pairs/pallas_call | solution.py:22
  36.0 0.0 collective-permute-done.5.refs_2_
  36.0 0.7 %pairs.5 = bf16[872,128]{1,0:T(8,128)(2,1)S(1)} custom-call(f32[2,128]{1,0:T(2,128)S(1)} %get-tuple-element.40.params, bf16[872,128]{1,0:T(8,128)(2,1)S(1)} %collective-permute-done.6.refs_1_.refs_0_, bf16[872,128]{1,0:T(8,128)(2,1)S(1)} %relay.3.refs_1_, bf16[872,128]{1,0:T(8,128)(2,1)S(1)} %collective-permute-done.5.refs_2_, ...), custom_call_target="tpu_custom_call" | custom-call | flops 84934656 | bytes 1556224 | tf_op jit(solution)/shard_map/pairs/pallas_call | solution.py:22
  36.7 1.3 %collective-permute-start.12 = (bf16[872,128]{1,0:T(8,128)(2,1)S(1)}, bf16[872,128]{1,0:T(8,128)(2,1)S(1)}, u32[]{:S(2)}, u32[]{:S(2)}) collective-permute-start(bf16[872,128]{1,0:T(8,128)(2,1)S(1)} %pairs.5), channel_id=1, source_target_pairs={{0,2},{2,0},{4,6},{6,4},{8,10},{10,8},{12,14},{14,12},{1,3},{3,1},... | collective-permute-start | bytes 669704 | tf_op jit(solution)/shard_map/ppermute | solution.py:280
  38.0 0.1 collective-permute-start.15
  38.0 0.7 %pairs.4 = (f32[96,1152]{1,0:T(8,128)S(1)}, bf16[96,1152]{1,0:T(8,128)(2,1)S(1)}, f32[1,96]{1,0:T(1,128)S(1)}) custom-call(f32[2,128]{1,0:T(2,128)S(1)} %get-tuple-element.40.params, bf16[872,128]{1,0:T(8,128)(2,1)S(1)} %get-tuple-element.41.refs_0_, bf16[872,128]{1,0:T(8,128)(2,1)S(1)} %relay.3.refs_1_, ...), custom_call_target="tpu_custom_call" | custom-call | flops 84934656 | bytes 1556224 | tf_op jit(solution)/shard_map/pairs/pallas_call | solution.py:22
  38.7 1.4 %collective-permute-start.14 = (bf16[96,1152]{1,0:T(8,128)(2,1)S(1)}, bf16[96,1152]{1,0:T(8,128)(2,1)S(1)}, u32[]{:S(2)}, u32[]{:S(2)}) collective-permute-start(bf16[96,1152]{1,0:T(8,128)(2,1)S(1)} %get-tuple-element.58), channel_id=1, source_target_pairs={{0,16},{16,0},{1,17},{17,1},{2,18},{18,2},{3,19},{19,3},{4,20},{20... | collective-permute-start | bytes 663560 | tf_op jit(solution)/shard_map/ppermute | solution.py:403
  40.1 8.5 %collective-permute-done.12.near = bf16[872,128]{1,0:T(8,128)(2,1)S(1)} collective-permute-done((bf16[872,128]{1,0:T(8,128)(2,1)S(1)}, bf16[872,128]{1,0:T(8,128)(2,1)S(1)}, u32[]{:S(2)}, u32[]{:S(2)}) %collective-permute-start.12) | collective-permute-done | bytes 223264 | tf_op jit(solution)/shard_map/ppermute | solution.py:280
  48.6 0.2 own_demb.1
  48.8 0.9 %collective-permute-start.13 = (bf16[104,1152]{1,0:T(8,128)(2,1)S(1)}, bf16[104,1152]{1,0:T(8,128)(2,1)S(1)}, u32[]{:S(2)}, u32[]{:S(2)}) collective-permute-start(bf16[104,1152]{1,0:T(8,128)(2,1)S(1)} %get-tuple-element.52.mine), channel_id=1, source_target_pairs={{0,1},{1,0},{2,3},{3,2},{4,5},{5,4},{6,7},{7,6},{8,9},{9,8},{10,11... | collective-permute-start | bytes 718856 | tf_op jit(solution)/shard_map/ppermute | solution.py:411
  49.7 0.0 collective-permute-done.14.across
  49.7 0.0 collective-permute-done.15.diagonal
  49.7 0.2 other_demb.1.mine
  50.0 0.9 %collective-permute-start.16 = (bf16[96,1152]{1,0:T(8,128)(2,1)S(1)}, bf16[96,1152]{1,0:T(8,128)(2,1)S(1)}, u32[]{:S(2)}, u32[]{:S(2)}) collective-permute-start(bf16[96,1152]{1,0:T(8,128)(2,1)S(1)} %other_demb.1.mine), channel_id=1, source_target_pairs={{0,1},{1,0},{2,3},{3,2},{4,5},{5,4},{6,7},{7,6},{8,9},{9,8},{10,11... | collective-permute-start | bytes 663560 | tf_op jit(solution)/shard_map/ppermute | solution.py:419
  50.9 0.0 collective-permute-done.13.theirs
  50.9 1.2 %own_grad.1 = (f32[1,192]{1,0:T(1,128)}, bf16[192,512]{1,0:T(8,128)(2,1)S(1)}) custom-call(bf16[104,1152]{1,0:T(8,128)(2,1)S(1)} %get-tuple-element.52.mine, bf16[104,1152]{1,0:T(8,128)(2,1)S(1)} %collective-permute-done.13.theirs, f32[1,96]{1,0:T(1,128)S(1)} %get-tuple-element.53.loss_mine, bf16[384,1152]{1,0:T(8,128)(2,1)S(1)} %get-tuple-element.54.image_proj, ...), custom_call_target="tpu_custom_call" | custom-call | flops 198180864 | bytes 2544000 | tf_op jit(solution)/shard_map/own_grad/pallas_call | solution.py:22
  52.1 0.0 collective-permute-done.16.theirs
  52.1 1.2 %grads.1 = (bf16[192,384]{1,0:T(8,128)(2,1)}, bf16[192,512]{1,0:T(8,128)(2,1)}) custom-call(bf16[192,512]{1,0:T(8,128)(2,1)S(1)} %get-tuple-element.57.own_grad, bf16[96,1152]{1,0:T(8,128)(2,1)S(1)} %other_demb.1.mine, bf16[96,1152]{1,0:T(8,128)(2,1)S(1)} %collective-permute-done.16.theirs, bf16[384,1152]{1,0:T(8,128)(2,1)S(1)} %get-tuple-element.54.image_proj, ...), custom_call_target="tpu_custom_call" | custom-call | flops 198180864 | bytes 2703360 | tf_op jit(solution)/shard_map/grads/pallas_call | solution.py:22
  (4 shorter events, 0.1 us)
Async XLA Ops:
  2.4 1.9 %collective-permute-start = (bf16[96,1152]{1,0:T(8,128)(2,1)S(1)}, bf16[96,1152]{1,0:T(8,128)(2,1)S(1)}, u32[]{:S(2)}, u32[]{:S(2)}) collective-permute-start(bf16[96,1152]{1,0:T(8,128)(2,1)S(1)} %get-tuple-element.37), channel_id=1, source_target_pairs={{0,1},{1,0},{2,3},{3,2},{4,5},{5,4},{6,7},{7,6},{8,9},{9,8},{10,11... | collective-permute-start | bytes 663560 | tf_op jit(solution)/shard_map/ppermute | solution.py:312
  4.3 6.7 %collective-permute-start.3 = (bf16[96,1152]{1,0:T(8,128)(2,1)S(1)}, bf16[96,1152]{1,0:T(8,128)(2,1)S(1)}, u32[]{:S(2)}, u32[]{:S(2)}) collective-permute-start(bf16[96,1152]{1,0:T(8,128)(2,1)S(1)} %own_send.1._), channel_id=1, source_target_pairs={{0,16},{16,0},{1,17},{17,1},{2,18},{18,2},{3,19},{19,3},{4,20},{20... | collective-permute-start | bytes 663560 | tf_op jit(solution)/shard_map/ppermute | solution.py:317
  6.2 4.8 %copy-start = (s32[192]{0:T(256)S(1)}, s32[192]{0:T(256)}, u32[]{:S(2)}) copy-start(s32[192]{0:T(256)} %param.13) | copy-start | bytes 2308
  6.2 4.8 %collective-permute-start.1 = (bf16[96,1152]{1,0:T(8,128)(2,1)S(1)}, bf16[96,1152]{1,0:T(8,128)(2,1)S(1)}, u32[]{:S(2)}, u32[]{:S(2)}) collective-permute-start(bf16[96,1152]{1,0:T(8,128)(2,1)S(1)} %get-tuple-element.39), channel_id=1, source_target_pairs={{0,1},{1,0},{2,3},{3,2},{4,5},{5,4},{6,7},{7,6},{8,9},{9,8},{10,11... | collective-permute-start | bytes 663560 | tf_op jit(solution)/shard_map/ppermute | solution.py:330
  11.2 9.4 %collective-permute-start.10 = (bf16[872,128]{1,0:T(8,128)(2,1)S(1)}, bf16[872,128]{1,0:T(8,128)(2,1)S(1)}, u32[]{:S(2)}, u32[]{:S(2)}) collective-permute-start(bf16[872,128]{1,0:T(8,128)(2,1)S(1)} %get-tuple-element.42.refs_2_), channel_id=1, source_target_pairs={{0,8},{2,10},{4,12},{6,14},{8,0},{10,2},{12,4},{14,6},{1,9},{3,11}... | collective-permute-start | bytes 669704 | tf_op jit(solution)/shard_map/ppermute | solution.py:280
  11.3 12.9 %collective-permute-start.8 = (bf16[872,128]{1,0:T(8,128)(2,1)S(1)}, bf16[872,128]{1,0:T(8,128)(2,1)S(1)}, u32[]{:S(2)}, u32[]{:S(2)}) collective-permute-start(bf16[872,128]{1,0:T(8,128)(2,1)S(1)} %get-tuple-element.42.refs_2_), channel_id=1, source_target_pairs={{0,4},{2,6},{4,0},{6,2},{8,12},{10,14},{12,8},{14,10},{1,5},{3,7},... | collective-permute-start | bytes 669704 | tf_op jit(solution)/shard_map/ppermute | solution.py:280
  12.7 21.3 %collective-permute-start.4 = (bf16[872,128]{1,0:T(8,128)(2,1)S(1)}, bf16[872,128]{1,0:T(8,128)(2,1)S(1)}, u32[]{:S(2)}, u32[]{:S(2)}) collective-permute-start(bf16[872,128]{1,0:T(8,128)(2,1)S(1)} %get-tuple-element.42.refs_2_), channel_id=1, source_target_pairs={{0,12},{2,14},{4,8},{6,10},{8,4},{10,6},{12,0},{14,2},{1,13},{3,15... | collective-permute-start | bytes 669704 | tf_op jit(solution)/shard_map/ppermute | solution.py:280
  14.0 5.1 %collective-permute-start.2 = (bf16[96,1152]{1,0:T(8,128)(2,1)S(1)}, bf16[96,1152]{1,0:T(8,128)(2,1)S(1)}, u32[]{:S(2)}, u32[]{:S(2)}) collective-permute-start(bf16[96,1152]{1,0:T(8,128)(2,1)S(1)} %other_send.1), channel_id=1, source_target_pairs={{0,16},{16,0},{1,17},{17,1},{2,18},{18,2},{3,19},{19,3},{4,20},{20... | collective-permute-start | bytes 663560 | tf_op jit(solution)/shard_map/ppermute | solution.py:334
  15.5 19.1 %collective-permute-start.7 = (bf16[872,128]{1,0:T(8,128)(2,1)S(1)}, bf16[872,128]{1,0:T(8,128)(2,1)S(1)}, u32[]{:S(2)}, u32[]{:S(2)}) collective-permute-start(bf16[872,128]{1,0:T(8,128)(2,1)S(1)} %get-tuple-element.42.refs_2_), channel_id=1, source_target_pairs={{0,1},{1,0},{2,3},{3,2},{4,5},{5,4},{6,7},{7,6},{8,9},{9,8},{10,11... | collective-permute-start | bytes 669704 | tf_op jit(solution)/shard_map/ppermute | solution.py:358
  19.4 15.2 %collective-permute-start.6 = (bf16[872,128]{1,0:T(8,128)(2,1)S(1)}, bf16[872,128]{1,0:T(8,128)(2,1)S(1)}, u32[]{:S(2)}, u32[]{:S(2)}) collective-permute-start(bf16[872,128]{1,0:T(8,128)(2,1)S(1)} %get-tuple-element.41.refs_0_), channel_id=1, source_target_pairs={{0,2},{2,0},{4,6},{6,4},{8,10},{10,8},{12,14},{14,12},{1,3},{3,1},... | collective-permute-start | bytes 669704 | tf_op jit(solution)/shard_map/ppermute | solution.py:280
  20.7 13.9 %collective-permute-start.11 = (bf16[872,128]{1,0:T(8,128)(2,1)S(1)}, bf16[872,128]{1,0:T(8,128)(2,1)S(1)}, u32[]{:S(2)}, u32[]{:S(2)}) collective-permute-start(bf16[872,128]{1,0:T(8,128)(2,1)S(1)} %collective-permute-done.10.refs_6_), channel_id=1, source_target_pairs={{0,1},{1,0},{2,3},{3,2},{4,5},{5,4},{6,7},{7,6},{8,9},{9,8},{10,11... | collective-permute-start | bytes 669704 | tf_op jit(solution)/shard_map/ppermute | solution.py:358
  24.3 10.2 %collective-permute-start.9 = (bf16[872,128]{1,0:T(8,128)(2,1)S(1)}, bf16[872,128]{1,0:T(8,128)(2,1)S(1)}, u32[]{:S(2)}, u32[]{:S(2)}) collective-permute-start(bf16[872,128]{1,0:T(8,128)(2,1)S(1)} %collective-permute-done.8.refs_4_), channel_id=1, source_target_pairs={{0,1},{1,0},{2,3},{3,2},{4,5},{5,4},{6,7},{7,6},{8,9},{9,8},{10,11... | collective-permute-start | bytes 669704 | tf_op jit(solution)/shard_map/ppermute | solution.py:358
  33.9 2.0 %collective-permute-start.5 = (bf16[872,128]{1,0:T(8,128)(2,1)S(1)}, bf16[872,128]{1,0:T(8,128)(2,1)S(1)}, u32[]{:S(2)}, u32[]{:S(2)}) collective-permute-start(bf16[872,128]{1,0:T(8,128)(2,1)S(1)} %relay.3.refs_1_), channel_id=1, source_target_pairs={{0,1},{1,0},{2,3},{3,2},{4,5},{5,4},{6,7},{7,6},{8,9},{9,8},{10,11... | collective-permute-start | bytes 669704 | tf_op jit(solution)/shard_map/ppermute | solution.py:358
  36.7 11.9 %collective-permute-start.12 = (bf16[872,128]{1,0:T(8,128)(2,1)S(1)}, bf16[872,128]{1,0:T(8,128)(2,1)S(1)}, u32[]{:S(2)}, u32[]{:S(2)}) collective-permute-start(bf16[872,128]{1,0:T(8,128)(2,1)S(1)} %pairs.5), channel_id=1, source_target_pairs={{0,2},{2,0},{4,6},{6,4},{8,10},{10,8},{12,14},{14,12},{1,3},{3,1},... | collective-permute-start | bytes 669704 | tf_op jit(solution)/shard_map/ppermute | solution.py:280
  38.0 11.8 %collective-permute-start.15 = (bf16[872,128]{1,0:T(8,128)(2,1)S(1)}, bf16[872,128]{1,0:T(8,128)(2,1)S(1)}, u32[]{:S(2)}, u32[]{:S(2)}) collective-permute-start(bf16[872,128]{1,0:T(8,128)(2,1)S(1)} %pairs.5), channel_id=1, source_target_pairs={{0,18},{2,16},{4,22},{6,20},{8,26},{10,24},{12,30},{14,28},{16,2},... | collective-permute-start | bytes 669704 | tf_op jit(solution)/shard_map/ppermute | solution.py:401
  38.7 11.0 %collective-permute-start.14 = (bf16[96,1152]{1,0:T(8,128)(2,1)S(1)}, bf16[96,1152]{1,0:T(8,128)(2,1)S(1)}, u32[]{:S(2)}, u32[]{:S(2)}) collective-permute-start(bf16[96,1152]{1,0:T(8,128)(2,1)S(1)} %get-tuple-element.58), channel_id=1, source_target_pairs={{0,16},{16,0},{1,17},{17,1},{2,18},{18,2},{3,19},{19,3},{4,20},{20... | collective-permute-start | bytes 663560 | tf_op jit(solution)/shard_map/ppermute | solution.py:403
  48.8 2.1 %collective-permute-start.13 = (bf16[104,1152]{1,0:T(8,128)(2,1)S(1)}, bf16[104,1152]{1,0:T(8,128)(2,1)S(1)}, u32[]{:S(2)}, u32[]{:S(2)}) collective-permute-start(bf16[104,1152]{1,0:T(8,128)(2,1)S(1)} %get-tuple-element.52.mine), channel_id=1, source_target_pairs={{0,1},{1,0},{2,3},{3,2},{4,5},{5,4},{6,7},{7,6},{8,9},{9,8},{10,11... | collective-permute-start | bytes 718856 | tf_op jit(solution)/shard_map/ppermute | solution.py:411
  50.0 2.1 %collective-permute-start.16 = (bf16[96,1152]{1,0:T(8,128)(2,1)S(1)}, bf16[96,1152]{1,0:T(8,128)(2,1)S(1)}, u32[]{:S(2)}, u32[]{:S(2)}) collective-permute-start(bf16[96,1152]{1,0:T(8,128)(2,1)S(1)} %other_demb.1.mine), channel_id=1, source_target_pairs={{0,1},{1,0},{2,3},{3,2},{4,5},{5,4},{6,7},{7,6},{8,9},{9,8},{10,11... | collective-permute-start | bytes 663560 | tf_op jit(solution)/shard_map/ppermute | solution.py:419
